TPU v7x, 32 devices: a whole 2x2x4 slice. The times are simulated.
32 devices in a mesh: seq: 16 (over z, y, core), head: 2 (over x).
Axes of the slice: x: 2, y: 2, z: 4, core: 2. Of those that a mesh axis runs over, the one named last changes fastest.
Arguments:
- queries: bfloat16 [8192, 4096], P(('seq', 'head')), may hold values from -6 to 6
- key_vectors: bfloat16 [8192, 4096], P(('seq', 'head')), may hold values from -6 to 6
- value_vectors: bfloat16 [8192, 4096], P(('seq', 'head')), may hold values from -6 to 6
- out_grads: bfloat16 [8192, 4096], P(('seq', 'head')), may hold values from -6 to 6
Outputs:
- grad_queries: bfloat16 [8192, 4096], P('seq', 'head')
- grad_keys: bfloat16 [8192, 4096], P('seq', 'head')
- grad_values: bfloat16 [8192, 4096], P('seq', 'head')
All inputs are finite; a program needn't handle non-finite values.
Results may differ from a plain program's by a relative error of at most 0.0051.
Values may be sent and summed in bfloat16 or wider, within the bound.
No kernel may reach another device: no remote copies, remote signals or barrier semaphores. Data moves between devices by JAX's collectives and lax.ppermute only.
A program may use at most 192 MiB of HBM per device.

v0:
```python
import functools
import math

import jax
import jax.numpy as jnp
from jax import lax
from jax.experimental import pallas as pl
from jax.experimental.pallas import tpu as pltpu
from jax.sharding import PartitionSpec as P


DK = 128
F32 = jnp.float32
BF16 = jnp.bfloat16
PAIR = 2 * DK


NT = (((1,), (1,)), ((), ()))
TN = (((0,), (0,)), ((), ()))
NN = (((1,), (0,)), ((), ()))


def mm(a, b, dims):
    return lax.dot_general(a, b, dims, preferred_element_type=F32)


def cost(flops, size):
    return pl.CostEstimate(flops=flops, bytes_accessed=size, transcendentals=0)


def pack_kernel(col_ref, q_ref, k_ref, v_ref, g_ref, out_ref):
    out_ref[0] = q_ref[...]
    out_ref[1] = k_ref[...]
    out_ref[2] = v_ref[...]
    out_ref[3] = g_ref[...]


def pack(col, arrays, first, pairs):
    rows = arrays[0].shape[0]
    own = pl.BlockSpec((rows, PAIR), lambda i, c: (0, c[0] + first + i))
    return pl.pallas_call(
        pack_kernel,
        grid_spec=pltpu.PrefetchScalarGridSpec(
            num_scalar_prefetch=1,
            grid=(pairs,),
            in_specs=[own] * 4,
            out_specs=pl.BlockSpec((4, rows, PAIR), lambda i, c: (0, 0, i)),
        ),
        out_shape=jax.ShapeDtypeStruct((4, rows, pairs * PAIR), BF16),
        cost_estimate=cost(0, 16 * rows * pairs * PAIR),
        name="pack",
    )(col, *arrays)


def state_kernel(peers, col_ref, q_ref, k_ref, v_ref, g_ref, *rest):
    out_ref = rest[peers]
    for j in range(PAIR // DK):
        at = slice(j * DK, (j + 1) * DK)
        kv = mm(k_ref[:, at], v_ref[:, at], TN)
        qg = mm(q_ref[:, at], g_ref[:, at], TN)
        for r in rest[:peers]:
            kv = kv + mm(r[1, :, at], r[2, :, at], TN)
            qg = qg + mm(r[0, :, at], r[3, :, at], TN)
        out_ref[0, j] = kv.astype(out_ref.dtype)
        out_ref[1, j] = qg.astype(out_ref.dtype)


def states(col, arrays, got, first, pairs, dtype):
    rows = arrays[0].shape[0]
    own = pl.BlockSpec((rows, PAIR), lambda i, c: (0, c[0] + first + i))
    there = pl.BlockSpec((4, rows, PAIR), lambda i, c: (0, 0, i))
    tokens = rows * (1 + len(got))
    per = PAIR // DK
    return pl.pallas_call(
        functools.partial(state_kernel, len(got)),
        grid_spec=pltpu.PrefetchScalarGridSpec(
            num_scalar_prefetch=1,
            grid=(pairs,),
            in_specs=[own] * 4 + [there] * len(got),
            out_specs=pl.BlockSpec((2, per, DK, DK), lambda i, c: (0, i, 0, 0)),
        ),
        out_shape=jax.ShapeDtypeStruct((2, per * pairs, DK, DK), dtype),
        cost_estimate=cost(4 * tokens * DK * PAIR * pairs, 8 * tokens * pairs * PAIR),
        name="states",
    )(col, *arrays, *got)


def out_kernel(peers, aliased, scale, col_ref, src_ref, q_ref, k_ref, v_ref, g_ref, *rest):
    got = rest[:peers]
    pre_ref, suf_ref = rest[peers : peers + 2]
    skip = peers + 2 + 3 * aliased
    dq_ref, dk_ref, dv_ref, all_ref = rest[skip : skip + 4]
    rows = q_ref.shape[0]
    mine = pl.multiple_of(src_ref[0] * rows, rows)
    for j, ref in enumerate((q_ref, k_ref, v_ref, g_ref)):
        all_ref[j, pl.ds(mine, rows), :] = ref[...]
    for p, r in enumerate(got):
        at = pl.multiple_of(src_ref[p + 1] * rows, rows)
        for j in range(4):
            all_ref[j, pl.ds(at, rows), :] = r[j]
    total = all_ref.shape[1]
    half = total // 2
    up, down = slice(0, half), slice(half, total)
    row = lax.broadcasted_iota(jnp.int32, (half, half), 0)
    column = lax.broadcasted_iota(jnp.int32, (half, half), 1)
    lower, upper = row >= column, row <= column

    def tri(x, keep):
        return jnp.where(keep, x, 0.0).astype(BF16)

    for j in range(PAIR // DK):
        at = slice(j * DK, (j + 1) * DK)
        q_a, q_b = all_ref[0, up, at], all_ref[0, down, at]
        k_a, k_b = all_ref[1, up, at], all_ref[1, down, at]
        v_a, v_b = all_ref[2, up, at], all_ref[2, down, at]
        g_a, g_b = all_ref[3, up, at], all_ref[3, down, at]
        pre, suf = pre_ref[j], suf_ref[j]
        dq_a = mm(tri(mm(g_a, v_a, NT), lower), k_a, NN) + mm(g_a, pre, NT)
        dq_b = (
            mm(mm(g_b, v_a, NT).astype(BF16), k_a, NN)
            + mm(tri(mm(g_b, v_b, NT), lower), k_b, NN)
            + mm(g_b, pre, NT)
        )
        dq_ref[up, at] = (scale * dq_a).astype(BF16)
        dq_ref[down, at] = (scale * dq_b).astype(BF16)
        dk_a = (
            mm(tri(mm(v_a, g_a, NT), upper), q_a, NN)
            + mm(mm(v_a, g_b, NT).astype(BF16), q_b, NN)
            + mm(v_a, suf, NT)
        )
        dk_b = mm(tri(mm(v_b, g_b, NT), upper), q_b, NN) + mm(v_b, suf, NT)
        dk_ref[up, at] = (scale * dk_a).astype(BF16)
        dk_ref[down, at] = (scale * dk_b).astype(BF16)
        dv_a = (
            mm(tri(mm(k_a, q_a, NT), upper), g_a, NN)
            + mm(mm(k_a, q_b, NT).astype(BF16), g_b, NN)
            + mm(k_a, suf, NN)
        )
        dv_b = mm(tri(mm(k_b, q_b, NT), upper), g_b, NN) + mm(k_b, suf, NN)
        dv_ref[up, at] = (scale * dv_a).astype(BF16)
        dv_ref[down, at] = (scale * dv_b).astype(BF16)


def outputs(col, src, arrays, got, pre, suf, first_state, first, pairs, heads_here, scale, outs):
    rows = arrays[0].shape[0]
    total = rows * (1 + len(got))
    own = pl.BlockSpec((rows, PAIR), lambda i, c, s: (0, c[0] + first + i))
    there = pl.BlockSpec((4, rows, PAIR), lambda i, c, s: (0, 0, i))
    state = pl.BlockSpec((PAIR // DK, DK, DK), lambda i, c, s: (first_state + i, 0, 0))
    here = pl.BlockSpec((total, PAIR), lambda i, c, s: (0, first + i))
    aliased = outs is not None
    base = 2 + 4 + len(got) + 2
    return pl.pallas_call(
        functools.partial(out_kernel, len(got), int(aliased), scale),
        grid_spec=pltpu.PrefetchScalarGridSpec(
            num_scalar_prefetch=2,
            grid=(pairs,),
            in_specs=[own] * 4
            + [there] * len(got)
            + [state] * 2
            + ([pl.BlockSpec(memory_space=pl.ANY)] * 3 if aliased else []),
            out_specs=[here] * 3,
            scratch_shapes=[pltpu.VMEM((4, total, PAIR), BF16)],
        ),
        out_shape=[jax.ShapeDtypeStruct((total, heads_here * DK), BF16)] * 3,
        input_output_aliases={base + j: j for j in range(3)} if aliased else {},
        cost_estimate=cost(14 * total * total * PAIR * pairs, 14 * total * PAIR * pairs),
        name="outputs",
    )(col, src, *arrays, *got, pre, suf, *(outs if aliased else ()))


def scan(own, sent):
    count = lax.axis_size("seq")
    chips = count // 2
    core = lax.axis_index("seq") % 2
    swap = [(i, i ^ 1) for i in range(count)]
    other = lax.ppermute(sent, "seq", swap).astype(F32)
    chip = own + other
    mine = jnp.where(core == 0, chip[0], chip[1])
    total = mine
    step = 1
    while step < chips:
        pairs = [(2 * c, 2 * (c + step)) for c in range(chips - step)]
        pairs += [(2 * (c + step) + 1, 2 * c + 1) for c in range(chips - step)]
        total = total + lax.ppermute(total.astype(BF16), "seq", pairs).astype(F32)
        step *= 2
    enter = total - mine
    kept = enter.astype(BF16)
    given = (enter + jnp.where(core == 0, own[0], own[1])).astype(BF16)
    taken = lax.ppermute(given, "seq", swap)
    return jnp.where(core == 0, kept, taken), jnp.where(core == 0, taken, kept)


def local(queries, key_vectors, value_vectors, out_grads):
    return grads((queries, key_vectors, value_vectors, out_grads))


def grads(arrays):
    peers = lax.axis_size("head")
    place = lax.axis_index("head")
    rows = arrays[0].shape[0]
    heads_here = arrays[0].shape[1] // DK // peers
    pairs_here = heads_here * DK // PAIR
    total_tokens = rows * peers * lax.axis_size("seq")
    scale = 1.0 / math.sqrt(DK * total_tokens)
    late = -(-3 * pairs_here // 8)
    early = pairs_here - late
    sizes = [1, (early - 1) // 2, early - 1 - (early - 1) // 2, late - late // 3, late // 3]
    sizes = [n for n in sizes if n]
    firsts = [sum(sizes[:i]) for i in range(len(sizes))]
    chunks = range(len(sizes))
    split = firsts.index(early)
    shifts = range(1, peers)
    cols = [((place + s) % peers * pairs_here).astype(jnp.int32).reshape(1) for s in range(peers)]
    src = jnp.stack([(place - s) % peers for s in range(peers)]).astype(jnp.int32)

    def move(value, shift):
        return lax.ppermute(value, "head", [(i, (i + shift) % peers) for i in range(peers)])

    def exchange(c):
        return [move(pack(cols[s], arrays, firsts[c], sizes[c]), s) for s in shifts]

    got = {0: exchange(0)}
    late_sent = [move(states(cols[s], arrays, [], early, late, BF16), s) for s in shifts]
    for c in chunks[1:]:
        got[c] = exchange(c)
    late_own = states(cols[0], arrays, [], early, late, F32)
    for piece in late_sent:
        late_own = late_own + piece.astype(F32)
    own = []
    for c in chunks[:split]:
        own.append(states(cols[0], arrays, got[c], firsts[c], sizes[c], F32))
    own[0] = jnp.concatenate([own[0], late_own], axis=1)
    scanned = [scan(own[c], own[c].astype(BF16)) for c in chunks[:split]]

    outs = None
    order = [*chunks[: split - 1], split, split - 1, *chunks[split + 1 :]]
    for c in order:
        pre, suf = scanned[c if c < split else 0]
        at = 0 if c < split else sizes[0] + firsts[c] - early
        outs = outputs(
            cols[0], src, arrays, got[c], pre, suf, at, firsts[c], sizes[c], heads_here, scale, outs
        )
    return tuple(outs)


def solution(mesh):
    tokens = P(("seq", "head"), None)
    return jax.shard_map(
        local,
        mesh=mesh,
        in_specs=(tokens,) * 4,
        out_specs=(P("seq", "head"),) * 3,
        check_vma=False,
    )
```

profile of v0, /device:TPU:0, one launch (start us, length us, event | category | flops | bytes accessed | tf_op | source)
XLA Modules:
  0.0 160.6 jit_solution(6822919637857094028)
XLA Ops:
  0.6 3.5 %states.7 = bf16[2,6,128,128]{3,2,1,0:T(8,128)(2,1)} custom-call(s32[1]{0:T(128)} %bitcast.3.col_ref, bf16[256,4096]{1,0:T(8,128)(2,1)} %q_ref.29, bf16[256,4096]{1,0:T(8,128)(2,1)} %k_ref.29, bf16[256,4096]{1,0:T(8,128)(2,1)} %v_ref.29, bf16[256,4096]{1,0:T(8,128)(2,1)} %g_ref.29), custom_call_target="tpu_custom_call" | custom-call | flops 100663296 | bytes 1572864 | tf_op jit(solution)/shard_map/states/pallas_call | solution.py:74
  4.2 3.0 %collective-permute-start.2 = (bf16[2,6,128,128]{3,2,1,0:T(8,128)(2,1)}, bf16[2,6,128,128]{3,2,1,0:T(8,128)(2,1)S(1)}, u32[]{:S(2)}, u32[]{:S(2)}) collective-permute-start(bf16[2,6,128,128]{3,2,1,0:T(8,128)(2,1)} %states.7), channel_id=1, source_target_pairs={{0,1},{1,0},{2,3},{3,2},{4,5},{5,4},{6,7},{7,6},{8,9},{9,8},{10,11... | collective-permute-start | bytes 1179656 | tf_op jit(solution)/shard_map/ppermute | solution.py:218
  7.1 1.9 %pack.6 = bf16[4,256,256]{2,1,0:T(8,128)(2,1)} custom-call(s32[1]{0:T(128)} %bitcast.3.col_ref, bf16[256,4096]{1,0:T(8,128)(2,1)} %q_ref.29, bf16[256,4096]{1,0:T(8,128)(2,1)} %k_ref.29, bf16[256,4096]{1,0:T(8,128)(2,1)} %v_ref.29, bf16[256,4096]{1,0:T(8,128)(2,1)} %g_ref.29), custom_call_target="tpu_custom_call" | custom-call | bytes 1048576 | tf_op jit(solution)/shard_map/pack/pallas_call | solution.py:41
  9.1 3.6 %states.6 = f32[2,6,128,128]{3,2,1,0:T(8,128)} custom-call(s32[1]{0:T(128)} %bitcast.col_ref, bf16[256,4096]{1,0:T(8,128)(2,1)} %q_ref.29, bf16[256,4096]{1,0:T(8,128)(2,1)} %k_ref.29, bf16[256,4096]{1,0:T(8,128)(2,1)} %v_ref.29, bf16[256,4096]{1,0:T(8,128)(2,1)} %g_ref.29), custom_call_target="tpu_custom_call" | custom-call | flops 100663296 | bytes 1572864 | tf_op jit(solution)/shard_map/states/pallas_call | solution.py:74
  12.7 4.6 %collective-permute-done.2 = bf16[2,6,128,128]{3,2,1,0:T(8,128)(2,1)S(1)} collective-permute-done((bf16[2,6,128,128]{3,2,1,0:T(8,128)(2,1)}, bf16[2,6,128,128]{3,2,1,0:T(8,128)(2,1)S(1)}, u32[]{:S(2)}, u32[]{:S(2)}) %collective-permute-start.2) | collective-permute-done | bytes 393248 | tf_op jit(solution)/shard_map/ppermute | solution.py:218
  18.5 9.2 %collective-permute-done.1.rest_0_ = bf16[4,256,256]{2,1,0:T(8,128)(2,1)S(1)} collective-permute-done((bf16[4,256,256]{2,1,0:T(8,128)(2,1)}, bf16[4,256,256]{2,1,0:T(8,128)(2,1)S(1)}, u32[]{:S(2)}, u32[]{:S(2)}) %collective-permute-start.1) | collective-permute-done | bytes 524320 | tf_op jit(solution)/shard_map/ppermute | solution.py:218
  28.5 2.4 %states.5 = f32[2,2,128,128]{3,2,1,0:T(8,128)} custom-call(s32[1]{0:T(128)} %bitcast.col_ref, bf16[256,4096]{1,0:T(8,128)(2,1)} %q_ref.29, bf16[256,4096]{1,0:T(8,128)(2,1)} %k_ref.29, bf16[256,4096]{1,0:T(8,128)(2,1)} %v_ref.29, bf16[256,4096]{1,0:T(8,128)(2,1)} %g_ref.29, bf16[4,256,256]{2,1,0:T(8,128)(2,1)} %copy-done.6), custom_call_target="tpu_custom_call" | custom-call | flops 67108864 | bytes 1048576 | tf_op jit(solution)/shard_map/states/pallas_call | solution.py:74
  30.8 1.8 %fusion = bf16[2,8,128,128]{3,2,1,0:T(8,128)(2,1)} fusion(f32[2,6,128,128]{3,2,1,0:T(8,128)S(1)} %convert_add_fusion.1, f32[2,2,128,128]{3,2,1,0:T(8,128)} %states.5), kind=kLoop, calls=%fused_computation.6 | loop fusion | flops 262144 | bytes 1572864 | tf_op jit(solution)/shard_map/convert_element_type | solution.py:234
  32.6 2.2 %pack.9 = bf16[4,256,512]{2,1,0:T(8,128)(2,1)} custom-call(s32[1]{0:T(128)} %bitcast.3.col_ref, bf16[256,4096]{1,0:T(8,128)(2,1)} %q_ref.29, bf16[256,4096]{1,0:T(8,128)(2,1)} %k_ref.29, bf16[256,4096]{1,0:T(8,128)(2,1)} %v_ref.29, bf16[256,4096]{1,0:T(8,128)(2,1)} %g_ref.29), custom_call_target="tpu_custom_call" | custom-call | bytes 2097152 | tf_op jit(solution)/shard_map/pack/pallas_call | solution.py:41
  34.8 1.7 %collective-permute-start.15 = (bf16[4,256,512]{2,1,0:T(8,128)(2,1)}, bf16[4,256,512]{2,1,0:T(8,128)(2,1)S(1)}, u32[]{:S(2)}, u32[]{:S(2)}) collective-permute-start(bf16[4,256,512]{2,1,0:T(8,128)(2,1)} %pack.9), channel_id=1, source_target_pairs={{0,1},{1,0},{2,3},{3,2},{4,5},{5,4},{6,7},{7,6},{8,9},{9,8},{10,11... | collective-permute-start | bytes 3145736 | tf_op jit(solution)/shard_map/ppermute | solution.py:218
  36.5 2.1 %pack.7 = bf16[4,256,512]{2,1,0:T(8,128)(2,1)} custom-call(s32[1]{0:T(128)} %bitcast.3.col_ref, bf16[256,4096]{1,0:T(8,128)(2,1)} %q_ref.29, bf16[256,4096]{1,0:T(8,128)(2,1)} %k_ref.29, bf16[256,4096]{1,0:T(8,128)(2,1)} %v_ref.29, bf16[256,4096]{1,0:T(8,128)(2,1)} %g_ref.29), custom_call_target="tpu_custom_call" | custom-call | bytes 2097152 | tf_op jit(solution)/shard_map/pack/pallas_call | solution.py:41
  40.9 4.4 %collective-permute-start.4 = (bf16[8,128,128]{2,1,0:T(8,128)(2,1)}, bf16[8,128,128]{2,1,0:T(8,128)(2,1)}, u32[]{:S(2)}, u32[]{:S(2)}) collective-permute-start(bf16[8,128,128]{2,1,0:T(8,128)(2,1)} %get-tuple-element.37), channel_id=1, source_target_pairs={{0,4},{4,8},{8,12},{12,16},{16,20},{20,24},{24,28},{6,2},{10,6},{1... | collective-permute-start | bytes 786440 | tf_op jit(solution)/shard_map/ppermute | solution.py:185
  45.3 2.1 %pack.8 = bf16[4,256,512]{2,1,0:T(8,128)(2,1)} custom-call(s32[1]{0:T(128)} %bitcast.3.col_ref, bf16[256,4096]{1,0:T(8,128)(2,1)} %q_ref.29, bf16[256,4096]{1,0:T(8,128)(2,1)} %k_ref.29, bf16[256,4096]{1,0:T(8,128)(2,1)} %v_ref.29, bf16[256,4096]{1,0:T(8,128)(2,1)} %g_ref.29), custom_call_target="tpu_custom_call" | custom-call | bytes 2097152 | tf_op jit(solution)/shard_map/pack/pallas_call | solution.py:41
  47.4 1.5 collective-permute-start.14
  48.9 1.9 %pack.5 = bf16[4,256,256]{2,1,0:T(8,128)(2,1)} custom-call(s32[1]{0:T(128)} %bitcast.3.col_ref, bf16[256,4096]{1,0:T(8,128)(2,1)} %q_ref.29, bf16[256,4096]{1,0:T(8,128)(2,1)} %k_ref.29, bf16[256,4096]{1,0:T(8,128)(2,1)} %v_ref.29, bf16[256,4096]{1,0:T(8,128)(2,1)} %g_ref.29), custom_call_target="tpu_custom_call" | custom-call | bytes 1048576 | tf_op jit(solution)/shard_map/pack/pallas_call | solution.py:41
  52.0 9.0 %collective-permute-done.15.rest_0_ = bf16[4,256,512]{2,1,0:T(8,128)(2,1)S(1)} collective-permute-done((bf16[4,256,512]{2,1,0:T(8,128)(2,1)}, bf16[4,256,512]{2,1,0:T(8,128)(2,1)S(1)}, u32[]{:S(2)}, u32[]{:S(2)}) %collective-permute-start.15) | collective-permute-done | bytes 1048608 | tf_op jit(solution)/shard_map/ppermute | solution.py:218
  62.0 2.8 %states.9 = f32[2,4,128,128]{3,2,1,0:T(8,128)} custom-call(s32[1]{0:T(128)} %bitcast.col_ref, bf16[256,4096]{1,0:T(8,128)(2,1)} %q_ref.29, bf16[256,4096]{1,0:T(8,128)(2,1)} %k_ref.29, bf16[256,4096]{1,0:T(8,128)(2,1)} %v_ref.29, bf16[256,4096]{1,0:T(8,128)(2,1)} %g_ref.29, bf16[4,256,512]{2,1,0:T(8,128)(2,1)} %copy-done.3), custom_call_target="tpu_custom_call" | custom-call | flops 134217728 | bytes 2097152 | tf_op jit(solution)/shard_map/states/pallas_call | solution.py:74
  66.0 17.5 %collective-permute-done.8.rest_0_ = bf16[4,256,512]{2,1,0:T(8,128)(2,1)S(1)} collective-permute-done((bf16[4,256,512]{2,1,0:T(8,128)(2,1)}, bf16[4,256,512]{2,1,0:T(8,128)(2,1)S(1)}, u32[]{:S(2)}, u32[]{:S(2)}) %collective-permute-start.8) | collective-permute-done | bytes 1048608 | tf_op jit(solution)/shard_map/ppermute | solution.py:218
  84.5 2.8 %states.8 = f32[2,4,128,128]{3,2,1,0:T(8,128)} custom-call(s32[1]{0:T(128)} %bitcast.col_ref, bf16[256,4096]{1,0:T(8,128)(2,1)} %q_ref.29, bf16[256,4096]{1,0:T(8,128)(2,1)} %k_ref.29, bf16[256,4096]{1,0:T(8,128)(2,1)} %v_ref.29, bf16[256,4096]{1,0:T(8,128)(2,1)} %g_ref.29, bf16[4,256,512]{2,1,0:T(8,128)(2,1)} %copy-done.2), custom_call_target="tpu_custom_call" | custom-call | flops 134217728 | bytes 2097152 | tf_op jit(solution)/shard_map/states/pallas_call | solution.py:74
  89.5 3.8 %collective-permute-start.5 = (bf16[8,128,128]{2,1,0:T(8,128)(2,1)S(1)}, bf16[8,128,128]{2,1,0:T(8,128)(2,1)S(1)}, u32[]{:S(2)}, u32[]{:S(2)}) collective-permute-start(bf16[8,128,128]{2,1,0:T(8,128)(2,1)S(1)} %fusion.8), channel_id=1, source_target_pairs={{0,8},{4,12},{8,16},{12,20},{16,24},{20,28},{10,2},{14,6},{18,10},... | collective-permute-start | bytes 786440 | tf_op jit(solution)/shard_map/ppermute | solution.py:185
  93.4 3.4 %collective-permute-start.17 = (bf16[4,128,128]{2,1,0:T(8,128)(2,1)S(1)}, bf16[4,128,128]{2,1,0:T(8,128)(2,1)S(1)}, u32[]{:S(2)}, u32[]{:S(2)}) collective-permute-start(bf16[4,128,128]{2,1,0:T(8,128)(2,1)S(1)} %get-tuple-element.29), channel_id=1, source_target_pairs={{0,4},{4,8},{8,12},{12,16},{16,20},{20,24},{24,28},{6,2},{10,6},{1... | collective-permute-start | bytes 393224 | tf_op jit(solution)/shard_map/ppermute | solution.py:185
  97.0 3.4 %collective-permute-start.10 = (bf16[4,128,128]{2,1,0:T(8,128)(2,1)S(1)}, bf16[4,128,128]{2,1,0:T(8,128)(2,1)S(1)}, u32[]{:S(2)}, u32[]{:S(2)}) collective-permute-start(bf16[4,128,128]{2,1,0:T(8,128)(2,1)S(1)} %get-tuple-element.33), channel_id=1, source_target_pairs={{0,4},{4,8},{8,12},{12,16},{16,20},{20,24},{24,28},{6,2},{10,6},{1... | collective-permute-start | bytes 393224 | tf_op jit(solution)/shard_map/ppermute | solution.py:185
  100.8 4.0 %collective-permute-start.18 = (bf16[4,128,128]{2,1,0:T(8,128)(2,1)S(1)}, bf16[4,128,128]{2,1,0:T(8,128)(2,1)S(1)}, u32[]{:S(2)}, u32[]{:S(2)}) collective-permute-start(bf16[4,128,128]{2,1,0:T(8,128)(2,1)S(1)} %fusion.20), channel_id=1, source_target_pairs={{0,8},{4,12},{8,16},{12,20},{16,24},{20,28},{10,2},{14,6},{18,10},... | collective-permute-start | bytes 393224 | tf_op jit(solution)/shard_map/ppermute | solution.py:185
  104.9 3.5 %collective-permute-start.11 = (bf16[4,128,128]{2,1,0:T(8,128)(2,1)S(1)}, bf16[4,128,128]{2,1,0:T(8,128)(2,1)S(1)}, u32[]{:S(2)}, u32[]{:S(2)}) collective-permute-start(bf16[4,128,128]{2,1,0:T(8,128)(2,1)S(1)} %fusion.18), channel_id=1, source_target_pairs={{0,8},{4,12},{8,16},{12,20},{16,24},{20,28},{10,2},{14,6},{18,10},... | collective-permute-start | bytes 393224 | tf_op jit(solution)/shard_map/ppermute | solution.py:185
  108.4 4.3 %collective-permute-start.19 = (bf16[4,128,128]{2,1,0:T(8,128)(2,1)S(1)}, bf16[4,128,128]{2,1,0:T(8,128)(2,1)S(1)}, u32[]{:S(2)}, u32[]{:S(2)}) collective-permute-start(bf16[4,128,128]{2,1,0:T(8,128)(2,1)S(1)} %fusion.21), channel_id=1, source_target_pairs={{0,16},{4,20},{8,24},{12,28},{18,2},{22,6},{26,10},{30,14},{1,17},... | collective-permute-start | bytes 393224 | tf_op jit(solution)/shard_map/ppermute | solution.py:185
  112.8 3.5 %collective-permute-start.12 = (bf16[4,128,128]{2,1,0:T(8,128)(2,1)S(1)}, bf16[4,128,128]{2,1,0:T(8,128)(2,1)S(1)}, u32[]{:S(2)}, u32[]{:S(2)}) collective-permute-start(bf16[4,128,128]{2,1,0:T(8,128)(2,1)S(1)} %fusion.19), channel_id=1, source_target_pairs={{0,16},{4,20},{8,24},{12,28},{18,2},{22,6},{26,10},{30,14},{1,17},... | collective-permute-start | bytes 393224 | tf_op jit(solution)/shard_map/ppermute | solution.py:185
  119.6 3.0 %collective-permute-done.6 = bf16[8,128,128]{2,1,0:T(8,128)(2,1)S(1)} collective-permute-done((bf16[8,128,128]{2,1,0:T(8,128)(2,1)S(1)}, bf16[8,128,128]{2,1,0:T(8,128)(2,1)S(1)}, u32[]{:S(2)}, u32[]{:S(2)}) %collective-permute-start.6) | collective-permute-done | bytes 262176 | tf_op jit(solution)/shard_map/ppermute | solution.py:185
  126.2 5.2 %outputs.5 = (bf16[512,2048]{1,0:T(8,128)(2,1)}, bf16[512,2048]{1,0:T(8,128)(2,1)}, bf16[512,2048]{1,0:T(8,128)(2,1)}) custom-call(s32[1]{0:T(128)} %bitcast.col_ref, s32[2]{0:T(128)} %pad_add_fusion.src_ref, bf16[256,4096]{1,0:T(8,128)(2,1)} %q_ref.29, bf16[256,4096]{1,0:T(8,128)(2,1)} %k_ref.29, bf16[256,4096]{1,0:T(8,128)(2,1)} %v_ref.29, ...), custom_call_target="tpu_custom_call" | custom-call | flops 939524096 | bytes 1835008 | tf_op jit(solution)/shard_map/outputs/pallas_call | solution.py:153
  131.5 8.0 %outputs.6 = (bf16[512,2048]{1,0:T(8,128)(2,1)}, bf16[512,2048]{1,0:T(8,128)(2,1)}, bf16[512,2048]{1,0:T(8,128)(2,1)}) custom-call(s32[1]{0:T(128)} %bitcast.col_ref, s32[2]{0:T(128)} %pad_add_fusion.src_ref, bf16[256,4096]{1,0:T(8,128)(2,1)} %q_ref.29, bf16[256,4096]{1,0:T(8,128)(2,1)} %k_ref.29, ...), custom_call_target="tpu_custom_call", output_to_operand_aliasing={{0}: (9, {}), {1}: (10, {}), {2}: (11, {})} | custom-call | flops 1879048192 | bytes 3670016 | tf_op jit(solution)/shard_map/outputs/pallas_call | solution.py:153
  139.5 7.9 %outputs.7 = (bf16[512,2048]{1,0:T(8,128)(2,1)}, bf16[512,2048]{1,0:T(8,128)(2,1)}, bf16[512,2048]{1,0:T(8,128)(2,1)}) custom-call(s32[1]{0:T(128)} %bitcast.col_ref, s32[2]{0:T(128)} %pad_add_fusion.src_ref, bf16[256,4096]{1,0:T(8,128)(2,1)} %q_ref.29, bf16[256,4096]{1,0:T(8,128)(2,1)} %k_ref.29, ...), custom_call_target="tpu_custom_call", output_to_operand_aliasing={{0}: (9, {}), {1}: (10, {}), {2}: (11, {})} | custom-call | flops 1879048192 | bytes 3670016 | tf_op jit(solution)/shard_map/outputs/pallas_call | solution.py:153
  147.4 7.9 %outputs.8 = (bf16[512,2048]{1,0:T(8,128)(2,1)}, bf16[512,2048]{1,0:T(8,128)(2,1)}, bf16[512,2048]{1,0:T(8,128)(2,1)}) custom-call(s32[1]{0:T(128)} %bitcast.col_ref, s32[2]{0:T(128)} %pad_add_fusion.src_ref, bf16[256,4096]{1,0:T(8,128)(2,1)} %q_ref.29, bf16[256,4096]{1,0:T(8,128)(2,1)} %k_ref.29, ...), custom_call_target="tpu_custom_call", output_to_operand_aliasing={{0}: (9, {}), {1}: (10, {}), {2}: (11, {})} | custom-call | flops 1879048192 | bytes 3670016 | tf_op jit(solution)/shard_map/outputs/pallas_call | solution.py:153
  155.3 5.2 %outputs.9 = (bf16[512,2048]{1,0:T(8,128)(2,1)}, bf16[512,2048]{1,0:T(8,128)(2,1)}, bf16[512,2048]{1,0:T(8,128)(2,1)}) custom-call(s32[1]{0:T(128)} %bitcast.col_ref, s32[2]{0:T(128)} %pad_add_fusion.src_ref, bf16[256,4096]{1,0:T(8,128)(2,1)} %q_ref.29, bf16[256,4096]{1,0:T(8,128)(2,1)} %k_ref.29, ...), custom_call_target="tpu_custom_call", output_to_operand_aliasing={{0}: (9, {}), {1}: (10, {}), {2}: (11, {})} | custom-call | flops 939524096 | bytes 1835008 | tf_op jit(solution)/shard_map/outputs/pallas_call | solution.py:153
  (62 shorter events, 18.3 us)
Async XLA Ops:
  4.2 13.1 %collective-permute-start.2 = (bf16[2,6,128,128]{3,2,1,0:T(8,128)(2,1)}, bf16[2,6,128,128]{3,2,1,0:T(8,128)(2,1)S(1)}, u32[]{:S(2)}, u32[]{:S(2)}) collective-permute-start(bf16[2,6,128,128]{3,2,1,0:T(8,128)(2,1)} %states.7), channel_id=1, source_target_pairs={{0,1},{1,0},{2,3},{3,2},{4,5},{5,4},{6,7},{7,6},{8,9},{9,8},{10,11... | collective-permute-start | bytes 1179656 | tf_op jit(solution)/shard_map/ppermute | solution.py:218
  9.0 18.6 %collective-permute-start.1 = (bf16[4,256,256]{2,1,0:T(8,128)(2,1)}, bf16[4,256,256]{2,1,0:T(8,128)(2,1)S(1)}, u32[]{:S(2)}, u32[]{:S(2)}) collective-permute-start(bf16[4,256,256]{2,1,0:T(8,128)(2,1)} %pack.6), channel_id=1, source_target_pairs={{0,1},{1,0},{2,3},{3,2},{4,5},{5,4},{6,7},{7,6},{8,9},{9,8},{10,11... | collective-permute-start | bytes 1572872 | tf_op jit(solution)/shard_map/ppermute | solution.py:218
  27.7 0.8 copy-start.6
  32.6 6.3 %collective-permute-start.3 = (bf16[2,8,128,128]{3,2,1,0:T(8,128)(2,1)}, bf16[2,8,128,128]{3,2,1,0:T(8,128)(2,1)}, u32[]{:S(2)}, u32[]{:S(2)}) collective-permute-start(bf16[2,8,128,128]{3,2,1,0:T(8,128)(2,1)} %fusion), channel_id=1, source_target_pairs={{0,2},{2,0},{4,6},{6,4},{8,10},{10,8},{12,14},{14,12},{16,18},{18,... | collective-permute-start | bytes 1572872 | tf_op jit(solution)/shard_map/ppermute | solution.py:177
  34.8 4.2 %copy-start.4 = (f32[2,2,128,128]{3,2,1,0:T(8,128)S(1)}, f32[2,2,128,128]{3,2,1,0:T(8,128)}, u32[]{:S(2)}) copy-start(f32[2,2,128,128]{3,2,1,0:T(8,128)} %states.5) | copy-start | bytes 786436
  34.8 26.2 %collective-permute-start.15 = (bf16[4,256,512]{2,1,0:T(8,128)(2,1)}, bf16[4,256,512]{2,1,0:T(8,128)(2,1)S(1)}, u32[]{:S(2)}, u32[]{:S(2)}) collective-permute-start(bf16[4,256,512]{2,1,0:T(8,128)(2,1)} %pack.9), channel_id=1, source_target_pairs={{0,1},{1,0},{2,3},{3,2},{4,5},{5,4},{6,7},{7,6},{8,9},{9,8},{10,11... | collective-permute-start | bytes 3145736 | tf_op jit(solution)/shard_map/ppermute | solution.py:218
  38.7 44.8 %collective-permute-start.8 = (bf16[4,256,512]{2,1,0:T(8,128)(2,1)}, bf16[4,256,512]{2,1,0:T(8,128)(2,1)S(1)}, u32[]{:S(2)}, u32[]{:S(2)}) collective-permute-start(bf16[4,256,512]{2,1,0:T(8,128)(2,1)} %pack.7), channel_id=1, source_target_pairs={{0,1},{1,0},{2,3},{3,2},{4,5},{5,4},{6,7},{7,6},{8,9},{9,8},{10,11... | collective-permute-start | bytes 3145736 | tf_op jit(solution)/shard_map/ppermute | solution.py:218
  40.9 47.6 %collective-permute-start.4 = (bf16[8,128,128]{2,1,0:T(8,128)(2,1)}, bf16[8,128,128]{2,1,0:T(8,128)(2,1)}, u32[]{:S(2)}, u32[]{:S(2)}) collective-permute-start(bf16[8,128,128]{2,1,0:T(8,128)(2,1)} %get-tuple-element.37), channel_id=1, source_target_pairs={{0,4},{4,8},{8,12},{12,16},{16,20},{20,24},{24,28},{6,2},{10,6},{1... | collective-permute-start | bytes 786440 | tf_op jit(solution)/shard_map/ppermute | solution.py:185
  47.4 92.1 %collective-permute-start.14 = (bf16[4,256,512]{2,1,0:T(8,128)(2,1)}, bf16[4,256,512]{2,1,0:T(8,128)(2,1)}, u32[]{:S(2)}, u32[]{:S(2)}) collective-permute-start(bf16[4,256,512]{2,1,0:T(8,128)(2,1)} %pack.8), channel_id=1, source_target_pairs={{0,1},{1,0},{2,3},{3,2},{4,5},{5,4},{6,7},{7,6},{8,9},{9,8},{10,11... | collective-permute-start | bytes 3145736 | tf_op jit(solution)/shard_map/ppermute | solution.py:218
  50.8 104.5 %collective-permute-start = (bf16[4,256,256]{2,1,0:T(8,128)(2,1)}, bf16[4,256,256]{2,1,0:T(8,128)(2,1)}, u32[]{:S(2)}, u32[]{:S(2)}) collective-permute-start(bf16[4,256,256]{2,1,0:T(8,128)(2,1)} %pack.5), channel_id=1, source_target_pairs={{0,1},{1,0},{2,3},{3,2},{4,5},{5,4},{6,7},{7,6},{8,9},{9,8},{10,11... | collective-permute-start | bytes 1572872 | tf_op jit(solution)/shard_map/ppermute | solution.py:218
  61.0 1.0 copy-start.3
  65.9 27.4 %collective-permute-start.16 = (bf16[2,4,128,128]{3,2,1,0:T(8,128)(2,1)S(1)}, bf16[2,4,128,128]{3,2,1,0:T(8,128)(2,1)S(1)}, u32[]{:S(2)}, u32[]{:S(2)}) collective-permute-start(bf16[2,4,128,128]{3,2,1,0:T(8,128)(2,1)S(1)} %convert_element_type.114), channel_id=1, source_target_pairs={{0,2},{2,0},{4,6},{6,4},{8,10},{10,8},{12,14},{14,12},{16,18},{18,... | collective-permute-start | bytes 786440 | tf_op jit(solution)/shard_map/ppermute | solution.py:177
  83.5 1.0 copy-start.2
  87.3 6.0 %copy-start.1 = (f32[2,4,128,128]{3,2,1,0:T(8,128)S(1)}, f32[2,4,128,128]{3,2,1,0:T(8,128)}, u32[]{:S(2)}) copy-start(f32[2,4,128,128]{3,2,1,0:T(8,128)} %states.9) | copy-start | bytes 1572868
  87.3 9.6 %copy-start = (f32[2,4,128,128]{3,2,1,0:T(8,128)S(1)}, f32[2,4,128,128]{3,2,1,0:T(8,128)}, u32[]{:S(2)}) copy-start(f32[2,4,128,128]{3,2,1,0:T(8,128)} %states.8) | copy-start | bytes 1572868
  88.4 8.4 %collective-permute-start.9 = (bf16[2,4,128,128]{3,2,1,0:T(8,128)(2,1)S(1)}, bf16[2,4,128,128]{3,2,1,0:T(8,128)(2,1)S(1)}, u32[]{:S(2)}, u32[]{:S(2)}) collective-permute-start(bf16[2,4,128,128]{3,2,1,0:T(8,128)(2,1)S(1)} %convert_element_type.104), channel_id=1, source_target_pairs={{0,2},{2,0},{4,6},{6,4},{8,10},{10,8},{12,14},{14,12},{16,18},{18,... | collective-permute-start | bytes 786440 | tf_op jit(solution)/shard_map/ppermute | solution.py:177
  89.5 26.8 %collective-permute-start.5 = (bf16[8,128,128]{2,1,0:T(8,128)(2,1)S(1)}, bf16[8,128,128]{2,1,0:T(8,128)(2,1)S(1)}, u32[]{:S(2)}, u32[]{:S(2)}) collective-permute-start(bf16[8,128,128]{2,1,0:T(8,128)(2,1)S(1)} %fusion.8), channel_id=1, source_target_pairs={{0,8},{4,12},{8,16},{12,20},{16,24},{20,28},{10,2},{14,6},{18,10},... | collective-permute-start | bytes 786440 | tf_op jit(solution)/shard_map/ppermute | solution.py:185
  93.4 7.3 %collective-permute-start.17 = (bf16[4,128,128]{2,1,0:T(8,128)(2,1)S(1)}, bf16[4,128,128]{2,1,0:T(8,128)(2,1)S(1)}, u32[]{:S(2)}, u32[]{:S(2)}) collective-permute-start(bf16[4,128,128]{2,1,0:T(8,128)(2,1)S(1)} %get-tuple-element.29), channel_id=1, source_target_pairs={{0,4},{4,8},{8,12},{12,16},{16,20},{20,24},{24,28},{6,2},{10,6},{1... | collective-permute-start | bytes 393224 | tf_op jit(solution)/shard_map/ppermute | solution.py:185
  97.0 7.8 %collective-permute-start.10 = (bf16[4,128,128]{2,1,0:T(8,128)(2,1)S(1)}, bf16[4,128,128]{2,1,0:T(8,128)(2,1)S(1)}, u32[]{:S(2)}, u32[]{:S(2)}) collective-permute-start(bf16[4,128,128]{2,1,0:T(8,128)(2,1)S(1)} %get-tuple-element.33), channel_id=1, source_target_pairs={{0,4},{4,8},{8,12},{12,16},{16,20},{20,24},{24,28},{6,2},{10,6},{1... | collective-permute-start | bytes 393224 | tf_op jit(solution)/shard_map/ppermute | solution.py:185
  100.8 7.6 %collective-permute-start.18 = (bf16[4,128,128]{2,1,0:T(8,128)(2,1)S(1)}, bf16[4,128,128]{2,1,0:T(8,128)(2,1)S(1)}, u32[]{:S(2)}, u32[]{:S(2)}) collective-permute-start(bf16[4,128,128]{2,1,0:T(8,128)(2,1)S(1)} %fusion.20), channel_id=1, source_target_pairs={{0,8},{4,12},{8,16},{12,20},{16,24},{20,28},{10,2},{14,6},{18,10},... | collective-permute-start | bytes 393224 | tf_op jit(solution)/shard_map/ppermute | solution.py:185
  104.9 7.9 %collective-permute-start.11 = (bf16[4,128,128]{2,1,0:T(8,128)(2,1)S(1)}, bf16[4,128,128]{2,1,0:T(8,128)(2,1)S(1)}, u32[]{:S(2)}, u32[]{:S(2)}) collective-permute-start(bf16[4,128,128]{2,1,0:T(8,128)(2,1)S(1)} %fusion.18), channel_id=1, source_target_pairs={{0,8},{4,12},{8,16},{12,20},{16,24},{20,28},{10,2},{14,6},{18,10},... | collective-permute-start | bytes 393224 | tf_op jit(solution)/shard_map/ppermute | solution.py:185
  108.4 10.3 %collective-permute-start.19 = (bf16[4,128,128]{2,1,0:T(8,128)(2,1)S(1)}, bf16[4,128,128]{2,1,0:T(8,128)(2,1)S(1)}, u32[]{:S(2)}, u32[]{:S(2)}) collective-permute-start(bf16[4,128,128]{2,1,0:T(8,128)(2,1)S(1)} %fusion.21), channel_id=1, source_target_pairs={{0,16},{4,20},{8,24},{12,28},{18,2},{22,6},{26,10},{30,14},{1,17},... | collective-permute-start | bytes 393224 | tf_op jit(solution)/shard_map/ppermute | solution.py:185
  112.8 9.8 %copy-start.5 = (f32[2,2,128,128]{3,2,1,0:T(8,128)S(1)}, f32[2,2,128,128]{3,2,1,0:T(8,128)}, u32[]{:S(2)}) copy-start(f32[2,2,128,128]{3,2,1,0:T(8,128)} %states.5) | copy-start | bytes 786436
  112.8 6.1 %collective-permute-start.12 = (bf16[4,128,128]{2,1,0:T(8,128)(2,1)S(1)}, bf16[4,128,128]{2,1,0:T(8,128)(2,1)S(1)}, u32[]{:S(2)}, u32[]{:S(2)}) collective-permute-start(bf16[4,128,128]{2,1,0:T(8,128)(2,1)S(1)} %fusion.19), channel_id=1, source_target_pairs={{0,16},{4,20},{8,24},{12,28},{18,2},{22,6},{26,10},{30,14},{1,17},... | collective-permute-start | bytes 393224 | tf_op jit(solution)/shard_map/ppermute | solution.py:185
  117.4 5.2 %collective-permute-start.6 = (bf16[8,128,128]{2,1,0:T(8,128)(2,1)S(1)}, bf16[8,128,128]{2,1,0:T(8,128)(2,1)S(1)}, u32[]{:S(2)}, u32[]{:S(2)}) collective-permute-start(bf16[8,128,128]{2,1,0:T(8,128)(2,1)S(1)} %fusion.9), channel_id=1, source_target_pairs={{0,16},{4,20},{8,24},{12,28},{18,2},{22,6},{26,10},{30,14},{1,17},... | collective-permute-start | bytes 786440 | tf_op jit(solution)/shard_map/ppermute | solution.py:185
  118.8 5.0 %collective-permute-start.20 = (bf16[4,128,128]{2,1,0:T(8,128)(2,1)S(1)}, bf16[4,128,128]{2,1,0:T(8,128)(2,1)S(1)}, u32[]{:S(2)}, u32[]{:S(2)}) collective-permute-start(bf16[4,128,128]{2,1,0:T(8,128)(2,1)S(1)} %get-tuple-element.27), channel_id=1, source_target_pairs={{0,2},{2,0},{4,6},{6,4},{8,10},{10,8},{12,14},{14,12},{16,18},{18,... | collective-permute-start | bytes 393224 | tf_op jit(solution)/shard_map/ppermute | solution.py:190
  119.0 5.6 %collective-permute-start.13 = (bf16[4,128,128]{2,1,0:T(8,128)(2,1)S(1)}, bf16[4,128,128]{2,1,0:T(8,128)(2,1)S(1)}, u32[]{:S(2)}, u32[]{:S(2)}) collective-permute-start(bf16[4,128,128]{2,1,0:T(8,128)(2,1)S(1)} %get-tuple-element.31), channel_id=1, source_target_pairs={{0,2},{2,0},{4,6},{6,4},{8,10},{10,8},{12,14},{14,12},{16,18},{18,... | collective-permute-start | bytes 393224 | tf_op jit(solution)/shard_map/ppermute | solution.py:190
  123.8 1.6 collective-permute-start.7
where the time goes:
time: 163 us; the launch traced here: 161 us
  Pallas kernels  59.6 us (37%)
  waiting for transfers between devices  43.7 us (27%)
  starting transfers between devices  39.5 us (24%)
  other arithmetic  14 us (9%)
  local copies, waits for them, and re-layouts  2.78 us (2%)
    ppermute x6, waiting for transfers between devices, move(): lax.ppermute(value, 'head', [(i, (i + shift) % peers) for i in range(peer...  40.3 us
    pallas_call x5, Pallas kernels, outputs(): pl.pallas_call(functools.partial(out_kernel, len(got), int(aliased), scal...  34.3 us
    ppermute x9, starting transfers between devices, scan(): total = total + lax.ppermute(total.astype(BF16), 'seq', pairs).astype(F32)  31.6 us
    pallas_call x5, Pallas kernels, states(): pl.pallas_call(functools.partial(state_kernel, len(got)), grid_spec=pltpu...  15.1 us
    pallas_call x5, Pallas kernels, pack(): pl.pallas_call(pack_kernel, grid_spec=pltpu.PrefetchScalarGridSpec(num_sc...  10.3 us
    ppermute x6, starting transfers between devices, move(): lax.ppermute(value, 'head', [(i, (i + shift) % peers) for i in range(peer...  7.02 us
    convert_element_type x3, other arithmetic, grads(): scanned = [scan(own[c], own[c].astype(BF16)) for c in chunks[:split]]  4.04 us
    ppermute x9, waiting for transfers between devices, scan(): total = total + lax.ppermute(total.astype(BF16), 'seq', pairs).astype(F32)  3.35 us
  transfers between devices with their start and end apart: 21, of which 6 were waited for; matrix products, arithmetic and copies ran while one was open for 8% of the time, Pallas kernels for 30%

commit v1 on v0

--- a/solution.py
+++ b/solution.py
@@ -28,28 +28,44 @@
     return pl.CostEstimate(flops=flops, bytes_accessed=size, transcendentals=0)
 
 
-def pack_kernel(col_ref, q_ref, k_ref, v_ref, g_ref, out_ref):
-    out_ref[0] = q_ref[...]
-    out_ref[1] = k_ref[...]
-    out_ref[2] = v_ref[...]
-    out_ref[3] = g_ref[...]
-
-
-def pack(col, arrays, first, pairs):
-    rows = arrays[0].shape[0]
-    own = pl.BlockSpec((rows, PAIR), lambda i, c: (0, c[0] + first + i))
-    return pl.pallas_call(
-        pack_kernel,
+def pack_kernel(bounds, peers, col_ref, *refs):
+    at = pl.program_id(0)
+    ins, outs = refs[: 4 * (peers - 1)], refs[4 * (peers - 1) :]
+    for c, (low, high) in enumerate(bounds):
+
+        @pl.when((at >= low) & (at < high))
+        def _():
+            for s in range(peers - 1):
+                for j in range(4):
+                    outs[c * (peers - 1) + s][j] = ins[4 * s + j][...]
+
+
+def pack(cols, peers, arrays, first, sizes):
+    rows = arrays[0].shape[0]
+    bounds = [(sum(sizes[:i]), sum(sizes[: i + 1])) for i in range(len(sizes))]
+
+    def own(s):
+        return pl.BlockSpec((rows, PAIR), lambda i, c: (0, c[s] + first + i))
+
+    def there(low, high):
+        return pl.BlockSpec((4, rows, PAIR), lambda i, c: (0, 0, jnp.clip(i - low, 0, high - low - 1)))
+
+    total = sum(sizes)
+    flat = pl.pallas_call(
+        functools.partial(pack_kernel, bounds, peers),
         grid_spec=pltpu.PrefetchScalarGridSpec(
             num_scalar_prefetch=1,
-            grid=(pairs,),
-            in_specs=[own] * 4,
-            out_specs=pl.BlockSpec((4, rows, PAIR), lambda i, c: (0, 0, i)),
-        ),
-        out_shape=jax.ShapeDtypeStruct((4, rows, pairs * PAIR), BF16),
-        cost_estimate=cost(0, 16 * rows * pairs * PAIR),
+            grid=(total,),
+            in_specs=[own(s) for s in range(1, peers) for _ in range(4)],
+            out_specs=[there(*at) for at in bounds for _ in range(1, peers)],
+        ),
+        out_shape=[
+            jax.ShapeDtypeStruct((4, rows, n * PAIR), BF16) for n in sizes for _ in range(1, peers)
+        ],
+        cost_estimate=cost(0, 16 * rows * total * PAIR * (peers - 1)),
         name="pack",
-    )(col, *arrays)
+    )(cols, *(list(arrays) * (peers - 1)))
+    return [flat[i * (peers - 1) : (i + 1) * (peers - 1)] for i in range(len(sizes))]
 
 
 def state_kernel(peers, col_ref, q_ref, k_ref, v_ref, g_ref, *rest):
@@ -65,7 +81,7 @@
         out_ref[1, j] = qg.astype(out_ref.dtype)
 
 
-def states(col, arrays, got, first, pairs, dtype):
+def states(cols, arrays, got, first, pairs):
     rows = arrays[0].shape[0]
     own = pl.BlockSpec((rows, PAIR), lambda i, c: (0, c[0] + first + i))
     there = pl.BlockSpec((4, rows, PAIR), lambda i, c: (0, 0, i))
@@ -79,16 +95,49 @@
             in_specs=[own] * 4 + [there] * len(got),
             out_specs=pl.BlockSpec((2, per, DK, DK), lambda i, c: (0, i, 0, 0)),
         ),
-        out_shape=jax.ShapeDtypeStruct((2, per * pairs, DK, DK), dtype),
+        out_shape=jax.ShapeDtypeStruct((2, per * pairs, DK, DK), BF16),
         cost_estimate=cost(4 * tokens * DK * PAIR * pairs, 8 * tokens * pairs * PAIR),
         name="states",
-    )(col, *arrays, *got)
+    )(cols, *arrays, *got)
+
+
+def source_kernel(peers, col_ref, *refs):
+    for s in range(peers):
+        q_ref, k_ref, v_ref, g_ref = refs[4 * s : 4 * s + 4]
+        out_ref = refs[4 * peers + s]
+        for j in range(PAIR // DK):
+            at = slice(j * DK, (j + 1) * DK)
+            out_ref[0, j] = mm(k_ref[:, at], v_ref[:, at], TN).astype(out_ref.dtype)
+            out_ref[1, j] = mm(q_ref[:, at], g_ref[:, at], TN).astype(out_ref.dtype)
+
+
+def source_states(cols, peers, arrays, first, pairs):
+    rows = arrays[0].shape[0]
+    per = PAIR // DK
+
+    def own(s):
+        return pl.BlockSpec((rows, PAIR), lambda i, c: (0, c[s] + first + i))
+
+    return pl.pallas_call(
+        functools.partial(source_kernel, peers),
+        grid_spec=pltpu.PrefetchScalarGridSpec(
+            num_scalar_prefetch=1,
+            grid=(pairs,),
+            in_specs=[own(s) for s in range(peers) for _ in range(4)],
+            out_specs=[pl.BlockSpec((2, per, DK, DK), lambda i, c: (0, i, 0, 0))] * peers,
+        ),
+        out_shape=[
+            jax.ShapeDtypeStruct((2, per * pairs, DK, DK), F32 if s == 0 else BF16) for s in range(peers)
+        ],
+        cost_estimate=cost(4 * rows * peers * DK * PAIR * pairs, 8 * rows * peers * pairs * PAIR),
+        name="source_states",
+    )(cols, *(list(arrays) * peers))
 
 
 def out_kernel(peers, aliased, scale, col_ref, src_ref, q_ref, k_ref, v_ref, g_ref, *rest):
     got = rest[:peers]
-    pre_ref, suf_ref = rest[peers : peers + 2]
-    skip = peers + 2 + 3 * aliased
+    sum_ref = rest[peers]
+    skip = peers + 1 + 3 * aliased
     dq_ref, dk_ref, dv_ref, all_ref = rest[skip : skip + 4]
     rows = q_ref.shape[0]
     mine = pl.multiple_of(src_ref[0] * rows, rows)
@@ -114,7 +163,7 @@
         k_a, k_b = all_ref[1, up, at], all_ref[1, down, at]
         v_a, v_b = all_ref[2, up, at], all_ref[2, down, at]
         g_a, g_b = all_ref[3, up, at], all_ref[3, down, at]
-        pre, suf = pre_ref[j], suf_ref[j]
+        pre, suf = sum_ref[0, j], sum_ref[1, j]
         dq_a = mm(tri(mm(g_a, v_a, NT), lower), k_a, NN) + mm(g_a, pre, NT)
         dq_b = (
             mm(mm(g_b, v_a, NT).astype(BF16), k_a, NN)
@@ -141,15 +190,15 @@
         dv_ref[down, at] = (scale * dv_b).astype(BF16)
 
 
-def outputs(col, src, arrays, got, pre, suf, first_state, first, pairs, heads_here, scale, outs):
+def outputs(cols, src, arrays, got, sums, first_sum, first, pairs, heads_here, scale, outs):
     rows = arrays[0].shape[0]
     total = rows * (1 + len(got))
     own = pl.BlockSpec((rows, PAIR), lambda i, c, s: (0, c[0] + first + i))
     there = pl.BlockSpec((4, rows, PAIR), lambda i, c, s: (0, 0, i))
-    state = pl.BlockSpec((PAIR // DK, DK, DK), lambda i, c, s: (first_state + i, 0, 0))
+    state = pl.BlockSpec((2, PAIR // DK, DK, DK), lambda i, c, s: (0, first_sum + i, 0, 0))
     here = pl.BlockSpec((total, PAIR), lambda i, c, s: (0, first + i))
     aliased = outs is not None
-    base = 2 + 4 + len(got) + 2
+    base = 2 + 4 + len(got) + 1
     return pl.pallas_call(
         functools.partial(out_kernel, len(got), int(aliased), scale),
         grid_spec=pltpu.PrefetchScalarGridSpec(
@@ -157,7 +206,7 @@
             grid=(pairs,),
             in_specs=[own] * 4
             + [there] * len(got)
-            + [state] * 2
+            + [state]
             + ([pl.BlockSpec(memory_space=pl.ANY)] * 3 if aliased else []),
             out_specs=[here] * 3,
             scratch_shapes=[pltpu.VMEM((4, total, PAIR), BF16)],
@@ -166,29 +215,21 @@
         input_output_aliases={base + j: j for j in range(3)} if aliased else {},
         cost_estimate=cost(14 * total * total * PAIR * pairs, 14 * total * PAIR * pairs),
         name="outputs",
-    )(col, src, *arrays, *got, pre, suf, *(outs if aliased else ()))
-
-
-def scan(own, sent):
+    )(cols, src, *arrays, *got, sums, *(outs if aliased else ()))
+
+
+def scan(own):
     count = lax.axis_size("seq")
-    chips = count // 2
-    core = lax.axis_index("seq") % 2
-    swap = [(i, i ^ 1) for i in range(count)]
-    other = lax.ppermute(sent, "seq", swap).astype(F32)
-    chip = own + other
-    mine = jnp.where(core == 0, chip[0], chip[1])
-    total = mine
-    step = 1
-    while step < chips:
-        pairs = [(2 * c, 2 * (c + step)) for c in range(chips - step)]
-        pairs += [(2 * (c + step) + 1, 2 * c + 1) for c in range(chips - step)]
-        total = total + lax.ppermute(total.astype(BF16), "seq", pairs).astype(F32)
-        step *= 2
-    enter = total - mine
-    kept = enter.astype(BF16)
-    given = (enter + jnp.where(core == 0, own[0], own[1])).astype(BF16)
-    taken = lax.ppermute(given, "seq", swap)
-    return jnp.where(core == 0, kept, taken), jnp.where(core == 0, taken, kept)
+    part = own.reshape(count, -1, DK)
+    parts = lax.all_to_all(part, "seq", 0, 0, tiled=True).astype(F32)
+    running, before = jnp.zeros_like(parts[0]), []
+    for i in range(count):
+        before.append(running)
+        running = running + parts[i]
+    before = jnp.stack(before)
+    after = running[None] - before - parts
+    mine = jnp.where(lax.axis_index("seq") < count // 2, before, after).astype(BF16)
+    return lax.all_to_all(mine, "seq", 0, 0, tiled=True).reshape(own.shape)
 
 
 def local(queries, key_vectors, value_vectors, out_grads):
@@ -211,35 +252,35 @@
     chunks = range(len(sizes))
     split = firsts.index(early)
     shifts = range(1, peers)
-    cols = [((place + s) % peers * pairs_here).astype(jnp.int32).reshape(1) for s in range(peers)]
-    src = jnp.stack([(place - s) % peers for s in range(peers)]).astype(jnp.int32)
-
-    def move(value, shift):
-        return lax.ppermute(value, "head", [(i, (i + shift) % peers) for i in range(peers)])
-
-    def exchange(c):
-        return [move(pack(cols[s], arrays, firsts[c], sizes[c]), s) for s in shifts]
-
-    got = {0: exchange(0)}
-    late_sent = [move(states(cols[s], arrays, [], early, late, BF16), s) for s in shifts]
-    for c in chunks[1:]:
-        got[c] = exchange(c)
-    late_own = states(cols[0], arrays, [], early, late, F32)
-    for piece in late_sent:
-        late_own = late_own + piece.astype(F32)
-    own = []
+    cols = ((place + jnp.arange(peers)) % peers * pairs_here).astype(jnp.int32)
+    src = ((place - jnp.arange(peers)) % peers).astype(jnp.int32)
+
+    def move(values):
+        return [
+            lax.ppermute(value, "head", [(i, (i + s) % peers) for i in range(peers)])
+            for s, value in zip(shifts, values)
+        ]
+
+    (packed,) = pack(cols, peers, arrays, 0, sizes[:1])
+    got = [move(packed)]
+    late_sums, *late_sent = source_states(cols, peers, arrays, early, late)
+    late_got = move(late_sent)
+    for c, packed in zip(chunks[1:], pack(cols, peers, arrays, sizes[0], sizes[1:])):
+        got.append(move(packed))
+    for piece in late_got:
+        late_sums = late_sums + piece.astype(F32)
+    sums = []
     for c in chunks[:split]:
-        own.append(states(cols[0], arrays, got[c], firsts[c], sizes[c], F32))
-    own[0] = jnp.concatenate([own[0], late_own], axis=1)
-    scanned = [scan(own[c], own[c].astype(BF16)) for c in chunks[:split]]
+        own = states(cols, arrays, got[c], firsts[c], sizes[c])
+        if c == 0:
+            own = jnp.concatenate([own, late_sums.astype(BF16)], axis=1)
+        sums.append(scan(own))
 
     outs = None
-    order = [*chunks[: split - 1], split, split - 1, *chunks[split + 1 :]]
-    for c in order:
-        pre, suf = scanned[c if c < split else 0]
+    for c in [*chunks[: split - 1], split, split - 1, *chunks[split + 1 :]]:
         at = 0 if c < split else sizes[0] + firsts[c] - early
         outs = outputs(
-            cols[0], src, arrays, got[c], pre, suf, at, firsts[c], sizes[c], heads_here, scale, outs
+            cols, src, arrays, got[c], sums[c if c < split else 0], at, firsts[c], sizes[c], heads_here, scale, outs
         )
     return tuple(outs)
 

time: 163 us -> 183 us (1.12)
  waiting for transfers between devices: 43.7 us -> 73.5 us
  other arithmetic: 14 us -> 7.12 us
  starting transfers between devices: 39.5 us -> 35 us
  local copies, waits for them, and re-layouts: 2.78 us -> 6.25 us
    all_to_all x0 -> x6, waiting for transfers between devices: none -> 40.6 us  [the longest x3 23.1 us: scan(): return lax.all_to_all(mine, 'seq', 0, 0, tiled=True).reshape(own.shape)]
    ppermute x21 -> x6, starting transfers between devices: 39.5 us -> 7.2 us  [move(): lax.ppermute(value, 'head', [(i, (i + s) % peers) for i in range(peers)])]
    all_to_all x0 -> x6, starting transfers between devices: none -> 27.8 us  [the longest x3 16.6 us: scan(): parts = lax.all_to_all(part, 'seq', 0, 0, tiled=True).astype(F32)]
    ppermute x21 -> x6, waiting for transfers between devices: 43.7 us -> 32.9 us  [move(): lax.ppermute(value, 'head', [(i, (i + s) % peers) for i in range(peers)])]
    pallas_call x5 -> x3, Pallas kernels: 15.1 us -> 9.82 us  [states(): pl.pallas_call(functools.partial(state_kernel, len(got)), grid_spec=pltpu...]
    convert_element_type x15 -> x7, other arithmetic: 8.53 us -> 3.98 us  [the longest x3 2.58 us: scan(): jnp.where(lax.axis_index('seq') < count // 2, before, after).astype(BF16)]
    pallas_call x5 -> x3, Pallas kernels: 10.3 us -> 14.8 us  [the longest x2 9.75 us: pack(): pl.pallas_call(functools.partial(pack_kernel, bounds, peers), grid_spec=p...]
    unnamed x14 -> x44, local copies, waits for them, and re-layouts: 2.78 us -> 6.25 us
  transfers between devices with their start and end apart: 21 -> 12, of which waited for: 6 -> 7; matrix products, arithmetic and copies ran while one was open for 8% -> 5% of each run, Pallas kernels for 30% -> 27%
where the time goes in v1:
time: 183 us; the launch traced here: 182 us
  waiting for transfers between devices  73.5 us (40%)
  Pallas kernels  58.7 us (32%)
  starting transfers between devices  35 us (19%)
  other arithmetic  7.12 us (4%)
  local copies, waits for them, and re-layouts  6.25 us (3%)
    pallas_call x5, Pallas kernels, outputs(): pl.pallas_call(functools.partial(out_kernel, len(got), int(aliased), scal...  34.1 us
    ppermute x6, waiting for transfers between devices, move(): lax.ppermute(value, 'head', [(i, (i + s) % peers) for i in range(peers)])  32.9 us
    all_to_all x3, waiting for transfers between devices, scan(): return lax.all_to_all(mine, 'seq', 0, 0, tiled=True).reshape(own.shape)  23.1 us
    all_to_all x3, waiting for transfers between devices, scan(): parts = lax.all_to_all(part, 'seq', 0, 0, tiled=True).astype(F32)  17.5 us
    all_to_all x3, starting transfers between devices, scan(): parts = lax.all_to_all(part, 'seq', 0, 0, tiled=True).astype(F32)  16.6 us
    all_to_all x3, starting transfers between devices, scan(): return lax.all_to_all(mine, 'seq', 0, 0, tiled=True).reshape(own.shape)  11.2 us
    pallas_call x3, Pallas kernels, states(): pl.pallas_call(functools.partial(state_kernel, len(got)), grid_spec=pltpu...  9.82 us
    pallas_call x2, Pallas kernels, pack(): pl.pallas_call(functools.partial(pack_kernel, bounds, peers), grid_spec=p...  9.75 us
  transfers between devices with their start and end apart: 12, of which 7 were waited for; matrix products, arithmetic and copies ran while one was open for 5% of the time, Pallas kernels for 27%

profile of v1, /device:TPU:0, one launch (start us, length us, event | category | flops | bytes accessed | tf_op | source)
XLA Modules:
  0.0 181.7 jit_solution(1555156717419777227)
XLA Ops:
  1.2 5.0 %source_states.1 = (f32[2,6,128,128]{3,2,1,0:T(8,128)}, bf16[2,6,128,128]{3,2,1,0:T(8,128)(2,1)}) custom-call(s32[2]{0:T(128)} %fusion.3.col_ref, bf16[256,4096]{1,0:T(8,128)(2,1)} %q_ref.15, bf16[256,4096]{1,0:T(8,128)(2,1)} %k_ref.15, bf16[256,4096]{1,0:T(8,128)(2,1)} %v_ref.15, bf16[256,4096]{1,0:T(8,128)(2,1)} %g_ref.15, bf16[256,4096]{1,0:T(8,128)(2,1)} %q_ref.15, ...), custom_call_target="tpu_custom_call" | custom-call | flops 201326592 | bytes 3145728 | tf_op jit(solution)/shard_map/source_states/pallas_call | solution.py:121
  6.2 3.0 %collective-permute-start.2 = (bf16[2,6,128,128]{3,2,1,0:T(8,128)(2,1)}, bf16[2,6,128,128]{3,2,1,0:T(8,128)(2,1)S(1)}, u32[]{:S(2)}, u32[]{:S(2)}) collective-permute-start(bf16[2,6,128,128]{3,2,1,0:T(8,128)(2,1)} %get-tuple-element.23), channel_id=1, source_target_pairs={{0,1},{1,0},{2,3},{3,2},{4,5},{5,4},{6,7},{7,6},{8,9},{9,8},{10,11... | collective-permute-start | bytes 1179656 | tf_op jit(solution)/shard_map/ppermute | solution.py:260
  9.2 2.6 %pack.3 = bf16[4,256,256]{2,1,0:T(8,128)(2,1)} custom-call(s32[2]{0:T(128)} %fusion.3.col_ref, bf16[256,4096]{1,0:T(8,128)(2,1)} %q_ref.15, bf16[256,4096]{1,0:T(8,128)(2,1)} %k_ref.15, bf16[256,4096]{1,0:T(8,128)(2,1)} %v_ref.15, bf16[256,4096]{1,0:T(8,128)(2,1)} %g_ref.15), custom_call_target="tpu_custom_call" | custom-call | bytes 1048576 | tf_op jit(solution)/shard_map/pack/pallas_call | solution.py:54
  11.8 7.2 %pack.2 = (bf16[4,256,512]{2,1,0:T(8,128)(2,1)}, bf16[4,256,512]{2,1,0:T(8,128)(2,1)}, bf16[4,256,512]{2,1,0:T(8,128)(2,1)}, bf16[4,256,256]{2,1,0:T(8,128)(2,1)}) custom-call(s32[2]{0:T(128)} %fusion.3.col_ref, bf16[256,4096]{1,0:T(8,128)(2,1)} %q_ref.15, bf16[256,4096]{1,0:T(8,128)(2,1)} %k_ref.15, bf16[256,4096]{1,0:T(8,128)(2,1)} %v_ref.15, ...), custom_call_target="tpu_custom_call" | custom-call | bytes 7340032 | tf_op jit(solution)/shard_map/pack/pallas_call | solution.py:54
  19.0 2.0 %collective-permute-start.5 = (bf16[4,256,512]{2,1,0:T(8,128)(2,1)}, bf16[4,256,512]{2,1,0:T(8,128)(2,1)S(1)}, u32[]{:S(2)}, u32[]{:S(2)}) collective-permute-start(bf16[4,256,512]{2,1,0:T(8,128)(2,1)} %get-tuple-element.26), channel_id=1, source_target_pairs={{0,1},{1,0},{2,3},{3,2},{4,5},{5,4},{6,7},{7,6},{8,9},{9,8},{10,11... | collective-permute-start | bytes 3145736 | tf_op jit(solution)/shard_map/ppermute | solution.py:260
  21.1 1.2 add_convert_fusion
  22.3 8.3 %collective-permute-done.1.rest_0_ = bf16[4,256,256]{2,1,0:T(8,128)(2,1)S(1)} collective-permute-done((bf16[4,256,256]{2,1,0:T(8,128)(2,1)}, bf16[4,256,256]{2,1,0:T(8,128)(2,1)S(1)}, u32[]{:S(2)}, u32[]{:S(2)}) %collective-permute-start.1) | collective-permute-done | bytes 524320 | tf_op jit(solution)/shard_map/ppermute | solution.py:260
  31.4 3.0 %states.3 = bf16[2,2,128,128]{3,2,1,0:T(8,128)(2,1)} custom-call(s32[2]{0:T(128)} %fusion.3.col_ref, bf16[256,4096]{1,0:T(8,128)(2,1)} %q_ref.15, bf16[256,4096]{1,0:T(8,128)(2,1)} %k_ref.15, bf16[256,4096]{1,0:T(8,128)(2,1)} %v_ref.15, bf16[256,4096]{1,0:T(8,128)(2,1)} %g_ref.15, bf16[4,256,256]{2,1,0:T(8,128)(2,1)} %copy-done.3), custom_call_target="tpu_custom_call" | custom-call | flops 67108864 | bytes 1048576 | tf_op jit(solution)/shard_map/states/pallas_call | solution.py:90
  34.4 1.7 pad_maximum_fusion
  36.2 6.5 %all-to-all-start = ((bf16[16,128,128]{2,1,0:T(8,128)(2,1)}), bf16[16,128,128]{2,1,0:T(8,128)(2,1)S(1)}, u32[]{:S(2)}, u32[]{:S(2)}) async-start(bf16[16,128,128]{2,1,0:T(8,128)(2,1)} %bitcast), calls=%async_computation | async-start | bytes 1048576 | tf_op jit(solution)/shard_map/all_to_all | solution.py:224
  42.7 1.6 collective-permute-start.4
  46.6 6.5 %collective-permute-done.5.rest_0_ = bf16[4,256,512]{2,1,0:T(8,128)(2,1)S(1)} collective-permute-done((bf16[4,256,512]{2,1,0:T(8,128)(2,1)}, bf16[4,256,512]{2,1,0:T(8,128)(2,1)S(1)}, u32[]{:S(2)}, u32[]{:S(2)}) %collective-permute-start.5) | collective-permute-done | bytes 1048608 | tf_op jit(solution)/shard_map/ppermute | solution.py:260
  53.1 1.0 copy-done.2
  54.1 3.4 %states.5 = bf16[2,4,128,128]{3,2,1,0:T(8,128)(2,1)} custom-call(s32[2]{0:T(128)} %fusion.3.col_ref, bf16[256,4096]{1,0:T(8,128)(2,1)} %q_ref.15, bf16[256,4096]{1,0:T(8,128)(2,1)} %k_ref.15, bf16[256,4096]{1,0:T(8,128)(2,1)} %v_ref.15, bf16[256,4096]{1,0:T(8,128)(2,1)} %g_ref.15, bf16[4,256,512]{2,1,0:T(8,128)(2,1)} %copy-done.2), custom_call_target="tpu_custom_call" | custom-call | flops 134217728 | bytes 2097152 | tf_op jit(solution)/shard_map/states/pallas_call | solution.py:90
  57.5 18.1 %collective-permute-done.3.rest_0_ = bf16[4,256,512]{2,1,0:T(8,128)(2,1)S(1)} collective-permute-done((bf16[4,256,512]{2,1,0:T(8,128)(2,1)}, bf16[4,256,512]{2,1,0:T(8,128)(2,1)S(1)}, u32[]{:S(2)}, u32[]{:S(2)}) %collective-permute-start.3) | collective-permute-done | bytes 1048608 | tf_op jit(solution)/shard_map/ppermute | solution.py:260
  75.6 1.0 copy-done.1
  76.6 3.4 %states.4 = bf16[2,4,128,128]{3,2,1,0:T(8,128)(2,1)} custom-call(s32[2]{0:T(128)} %fusion.3.col_ref, bf16[256,4096]{1,0:T(8,128)(2,1)} %q_ref.15, bf16[256,4096]{1,0:T(8,128)(2,1)} %k_ref.15, bf16[256,4096]{1,0:T(8,128)(2,1)} %v_ref.15, bf16[256,4096]{1,0:T(8,128)(2,1)} %g_ref.15, bf16[4,256,512]{2,1,0:T(8,128)(2,1)} %copy-done.1), custom_call_target="tpu_custom_call" | custom-call | flops 134217728 | bytes 2097152 | tf_op jit(solution)/shard_map/states/pallas_call | solution.py:90
  80.0 6.6 %all-to-all-start.4 = ((bf16[16,64,128]{2,1,0:T(8,128)(2,1)}), bf16[16,64,128]{2,1,0:T(8,128)(2,1)S(1)}, u32[]{:S(2)}, u32[]{:S(2)}) async-start(bf16[16,64,128]{2,1,0:T(8,128)(2,1)} %bitcast.6), calls=%async_computation.4 | async-start | bytes 524288 | tf_op jit(solution)/shard_map/all_to_all | solution.py:224
  87.0 1.0 select_convert_fusion
  88.0 8.6 %all-to-all-done.4 = bf16[16,64,128]{2,1,0:T(8,128)(2,1)S(1)} async-done(((bf16[16,64,128]{2,1,0:T(8,128)(2,1)}), bf16[16,64,128]{2,1,0:T(8,128)(2,1)S(1)}, u32[]{:S(2)}, u32[]{:S(2)}) %all-to-all-start.4) | async-done | bytes 262176 | tf_op jit(solution)/shard_map/all_to_all | solution.py:224
  96.6 3.5 %all-to-all-start.2 = ((bf16[16,64,128]{2,1,0:T(8,128)(2,1)}), bf16[16,64,128]{2,1,0:T(8,128)(2,1)S(1)}, u32[]{:S(2)}, u32[]{:S(2)}) async-start(bf16[16,64,128]{2,1,0:T(8,128)(2,1)} %bitcast.3), calls=%async_computation.2 | async-start | bytes 524288 | tf_op jit(solution)/shard_map/all_to_all | solution.py:224
  101.3 8.9 %all-to-all-done.2 = bf16[16,64,128]{2,1,0:T(8,128)(2,1)S(1)} async-done(((bf16[16,64,128]{2,1,0:T(8,128)(2,1)}), bf16[16,64,128]{2,1,0:T(8,128)(2,1)S(1)}, u32[]{:S(2)}, u32[]{:S(2)}) %all-to-all-start.2) | async-done | bytes 262176 | tf_op jit(solution)/shard_map/all_to_all | solution.py:224
  110.1 3.5 %all-to-all-start.5 = ((bf16[16,64,128]{2,1,0:T(8,128)(2,1)}), bf16[16,64,128]{2,1,0:T(8,128)(2,1)S(1)}, u32[]{:S(2)}, u32[]{:S(2)}) async-start(bf16[16,64,128]{2,1,0:T(8,128)(2,1)} %select_convert_fusion.1), calls=%async_computation.5 | async-start | bytes 524288 | tf_op jit(solution)/shard_map/all_to_all | solution.py:232
  113.9 9.7 %all-to-all-done.5 = bf16[16,64,128]{2,1,0:T(8,128)(2,1)S(1)} async-done(((bf16[16,64,128]{2,1,0:T(8,128)(2,1)}), bf16[16,64,128]{2,1,0:T(8,128)(2,1)S(1)}, u32[]{:S(2)}, u32[]{:S(2)}) %all-to-all-start.5) | async-done | bytes 262176 | tf_op jit(solution)/shard_map/all_to_all | solution.py:232
  123.7 3.6 %all-to-all-start.1 = ((bf16[16,128,128]{2,1,0:T(8,128)(2,1)}), bf16[16,128,128]{2,1,0:T(8,128)(2,1)S(1)}, u32[]{:S(2)}, u32[]{:S(2)}) async-start(bf16[16,128,128]{2,1,0:T(8,128)(2,1)} %select_convert_fusion), calls=%async_computation.1 | async-start | bytes 1048576 | tf_op jit(solution)/shard_map/all_to_all | solution.py:232
  128.1 13.4 %all-to-all-done.1 = bf16[16,128,128]{2,1,0:T(8,128)(2,1)S(1)} async-done(((bf16[16,128,128]{2,1,0:T(8,128)(2,1)}), bf16[16,128,128]{2,1,0:T(8,128)(2,1)S(1)}, u32[]{:S(2)}, u32[]{:S(2)}) %all-to-all-start.1) | async-done | bytes 524320 | tf_op jit(solution)/shard_map/all_to_all | solution.py:232
  141.5 4.1 %all-to-all-start.3 = ((bf16[16,64,128]{2,1,0:T(8,128)(2,1)}), bf16[16,64,128]{2,1,0:T(8,128)(2,1)S(1)}, u32[]{:S(2)}, u32[]{:S(2)}) async-start(bf16[16,64,128]{2,1,0:T(8,128)(2,1)} %select_convert_fusion.2), calls=%async_computation.3 | async-start | bytes 524288 | tf_op jit(solution)/shard_map/all_to_all | solution.py:232
  146.1 5.2 %outputs.5 = (bf16[512,2048]{1,0:T(8,128)(2,1)}, bf16[512,2048]{1,0:T(8,128)(2,1)}, bf16[512,2048]{1,0:T(8,128)(2,1)}) custom-call(s32[2]{0:T(128)} %fusion.3.col_ref, s32[2]{0:T(128)} %and_select_fusion.src_ref, bf16[256,4096]{1,0:T(8,128)(2,1)} %q_ref.15, bf16[256,4096]{1,0:T(8,128)(2,1)} %k_ref.15, bf16[256,4096]{1,0:T(8,128)(2,1)} %v_ref.15, ...), custom_call_target="tpu_custom_call" | custom-call | flops 939524096 | bytes 1835008 | tf_op jit(solution)/shard_map/outputs/pallas_call | solution.py:202
  151.4 7.9 %outputs.6 = (bf16[512,2048]{1,0:T(8,128)(2,1)}, bf16[512,2048]{1,0:T(8,128)(2,1)}, bf16[512,2048]{1,0:T(8,128)(2,1)}) custom-call(s32[2]{0:T(128)} %fusion.3.col_ref, s32[2]{0:T(128)} %and_select_fusion.src_ref, bf16[256,4096]{1,0:T(8,128)(2,1)} %q_ref.15, bf16[256,4096]{1,0:T(8,128)(2,1)} %k_ref.15, ...), custom_call_target="tpu_custom_call", output_to_operand_aliasing={{0}: (8, {}), {1}: (9, {}), {2}: (10, {})} | custom-call | flops 1879048192 | bytes 3670016 | tf_op jit(solution)/shard_map/outputs/pallas_call | solution.py:202
  159.2 7.9 %outputs.7 = (bf16[512,2048]{1,0:T(8,128)(2,1)}, bf16[512,2048]{1,0:T(8,128)(2,1)}, bf16[512,2048]{1,0:T(8,128)(2,1)}) custom-call(s32[2]{0:T(128)} %fusion.3.col_ref, s32[2]{0:T(128)} %and_select_fusion.src_ref, bf16[256,4096]{1,0:T(8,128)(2,1)} %q_ref.15, bf16[256,4096]{1,0:T(8,128)(2,1)} %k_ref.15, ...), custom_call_target="tpu_custom_call", output_to_operand_aliasing={{0}: (8, {}), {1}: (9, {}), {2}: (10, {})} | custom-call | flops 1879048192 | bytes 3670016 | tf_op jit(solution)/shard_map/outputs/pallas_call | solution.py:202
  167.8 7.9 %outputs.8 = (bf16[512,2048]{1,0:T(8,128)(2,1)}, bf16[512,2048]{1,0:T(8,128)(2,1)}, bf16[512,2048]{1,0:T(8,128)(2,1)}) custom-call(s32[2]{0:T(128)} %fusion.3.col_ref, s32[2]{0:T(128)} %and_select_fusion.src_ref, bf16[256,4096]{1,0:T(8,128)(2,1)} %q_ref.15, bf16[256,4096]{1,0:T(8,128)(2,1)} %k_ref.15, ...), custom_call_target="tpu_custom_call", output_to_operand_aliasing={{0}: (8, {}), {1}: (9, {}), {2}: (10, {})} | custom-call | flops 1879048192 | bytes 3670016 | tf_op jit(solution)/shard_map/outputs/pallas_call | solution.py:202
  176.5 5.2 %outputs.9 = (bf16[512,2048]{1,0:T(8,128)(2,1)}, bf16[512,2048]{1,0:T(8,128)(2,1)}, bf16[512,2048]{1,0:T(8,128)(2,1)}) custom-call(s32[2]{0:T(128)} %fusion.3.col_ref, s32[2]{0:T(128)} %and_select_fusion.src_ref, bf16[256,4096]{1,0:T(8,128)(2,1)} %q_ref.15, bf16[256,4096]{1,0:T(8,128)(2,1)} %k_ref.15, ...), custom_call_target="tpu_custom_call", output_to_operand_aliasing={{0}: (8, {}), {1}: (9, {}), {2}: (10, {})} | custom-call | flops 939524096 | bytes 1835008 | tf_op jit(solution)/shard_map/outputs/pallas_call | solution.py:202
  (81 shorter events, 8.1 us)
Async XLA Ops:
  6.2 14.9 %collective-permute-start.2 = (bf16[2,6,128,128]{3,2,1,0:T(8,128)(2,1)}, bf16[2,6,128,128]{3,2,1,0:T(8,128)(2,1)S(1)}, u32[]{:S(2)}, u32[]{:S(2)}) collective-permute-start(bf16[2,6,128,128]{3,2,1,0:T(8,128)(2,1)} %get-tuple-element.23), channel_id=1, source_target_pairs={{0,1},{1,0},{2,3},{3,2},{4,5},{5,4},{6,7},{7,6},{8,9},{9,8},{10,11... | collective-permute-start | bytes 1179656 | tf_op jit(solution)/shard_map/ppermute | solution.py:260
  11.8 18.8 %collective-permute-start.1 = (bf16[4,256,256]{2,1,0:T(8,128)(2,1)}, bf16[4,256,256]{2,1,0:T(8,128)(2,1)S(1)}, u32[]{:S(2)}, u32[]{:S(2)}) collective-permute-start(bf16[4,256,256]{2,1,0:T(8,128)(2,1)} %pack.3), channel_id=1, source_target_pairs={{0,1},{1,0},{2,3},{3,2},{4,5},{5,4},{6,7},{7,6},{8,9},{9,8},{10,11... | collective-permute-start | bytes 1572872 | tf_op jit(solution)/shard_map/ppermute | solution.py:260
  19.0 34.1 %collective-permute-start.5 = (bf16[4,256,512]{2,1,0:T(8,128)(2,1)}, bf16[4,256,512]{2,1,0:T(8,128)(2,1)S(1)}, u32[]{:S(2)}, u32[]{:S(2)}) collective-permute-start(bf16[4,256,512]{2,1,0:T(8,128)(2,1)} %get-tuple-element.26), channel_id=1, source_target_pairs={{0,1},{1,0},{2,3},{3,2},{4,5},{5,4},{6,7},{7,6},{8,9},{9,8},{10,11... | collective-permute-start | bytes 3145736 | tf_op jit(solution)/shard_map/ppermute | solution.py:260
  21.0 54.6 %collective-permute-start.3 = (bf16[4,256,512]{2,1,0:T(8,128)(2,1)}, bf16[4,256,512]{2,1,0:T(8,128)(2,1)S(1)}, u32[]{:S(2)}, u32[]{:S(2)}) collective-permute-start(bf16[4,256,512]{2,1,0:T(8,128)(2,1)} %get-tuple-element.24), channel_id=1, source_target_pairs={{0,1},{1,0},{2,3},{3,2},{4,5},{5,4},{6,7},{7,6},{8,9},{9,8},{10,11... | collective-permute-start | bytes 3145736 | tf_op jit(solution)/shard_map/ppermute | solution.py:260
  30.6 0.8 copy-start.3
  36.2 43.8 %all-to-all-start = ((bf16[16,128,128]{2,1,0:T(8,128)(2,1)}), bf16[16,128,128]{2,1,0:T(8,128)(2,1)S(1)}, u32[]{:S(2)}, u32[]{:S(2)}) async-start(bf16[16,128,128]{2,1,0:T(8,128)(2,1)} %bitcast), calls=%async_computation | async-start | bytes 1048576 | tf_op jit(solution)/shard_map/all_to_all | solution.py:224
  42.7 116.6 %collective-permute-start.4 = (bf16[4,256,512]{2,1,0:T(8,128)(2,1)}, bf16[4,256,512]{2,1,0:T(8,128)(2,1)}, u32[]{:S(2)}, u32[]{:S(2)}) collective-permute-start(bf16[4,256,512]{2,1,0:T(8,128)(2,1)} %get-tuple-element.25), channel_id=1, source_target_pairs={{0,1},{1,0},{2,3},{3,2},{4,5},{5,4},{6,7},{7,6},{8,9},{9,8},{10,11... | collective-permute-start | bytes 3145736 | tf_op jit(solution)/shard_map/ppermute | solution.py:260
  44.2 131.5 %collective-permute-start = (bf16[4,256,256]{2,1,0:T(8,128)(2,1)}, bf16[4,256,256]{2,1,0:T(8,128)(2,1)S(1)}, u32[]{:S(2)}, u32[]{:S(2)}) collective-permute-start(bf16[4,256,256]{2,1,0:T(8,128)(2,1)} %get-tuple-element.21), channel_id=1, source_target_pairs={{0,1},{1,0},{2,3},{3,2},{4,5},{5,4},{6,7},{7,6},{8,9},{9,8},{10,11... | collective-permute-start | bytes 1572872 | tf_op jit(solution)/shard_map/ppermute | solution.py:260
  53.1 1.0 copy-start.2
  75.6 1.0 copy-start.1
  80.0 6.7 %copy-start.4 = (f32[16,128,128]{2,1,0:T(8,128)S(1)}, f32[16,128,128]{2,1,0:T(8,128)}, u32[]{:S(2)}) copy-start(f32[16,128,128]{2,1,0:T(8,128)} %constant_dynamic-update-slice_fusion.15) | copy-start | bytes 3145732
  80.0 16.6 %all-to-all-start.4 = ((bf16[16,64,128]{2,1,0:T(8,128)(2,1)}), bf16[16,64,128]{2,1,0:T(8,128)(2,1)S(1)}, u32[]{:S(2)}, u32[]{:S(2)}) async-start(bf16[16,64,128]{2,1,0:T(8,128)(2,1)} %bitcast.6), calls=%async_computation.4 | async-start | bytes 524288 | tf_op jit(solution)/shard_map/all_to_all | solution.py:224
  87.0 13.3 %copy-start.8 = (f32[16,64,128]{2,1,0:T(8,128)S(1)}, f32[16,64,128]{2,1,0:T(8,128)}, u32[]{:S(2)}) copy-start(f32[16,64,128]{2,1,0:T(8,128)} %constant_dynamic-update-slice_fusion.47) | copy-start | bytes 1572868
  96.6 13.5 %all-to-all-start.2 = ((bf16[16,64,128]{2,1,0:T(8,128)(2,1)}), bf16[16,64,128]{2,1,0:T(8,128)(2,1)S(1)}, u32[]{:S(2)}, u32[]{:S(2)}) async-start(bf16[16,64,128]{2,1,0:T(8,128)(2,1)} %bitcast.3), calls=%async_computation.2 | async-start | bytes 524288 | tf_op jit(solution)/shard_map/all_to_all | solution.py:224
  100.2 13.5 %copy-start.7 = (f32[16,64,128]{2,1,0:T(8,128)S(1)}, f32[16,64,128]{2,1,0:T(8,128)}, u32[]{:S(2)}) copy-start(f32[16,64,128]{2,1,0:T(8,128)} %constant_dynamic-update-slice_fusion.31) | copy-start | bytes 1572868
  110.1 13.5 %all-to-all-start.5 = ((bf16[16,64,128]{2,1,0:T(8,128)(2,1)}), bf16[16,64,128]{2,1,0:T(8,128)(2,1)S(1)}, u32[]{:S(2)}, u32[]{:S(2)}) async-start(bf16[16,64,128]{2,1,0:T(8,128)(2,1)} %select_convert_fusion.1), calls=%async_computation.5 | async-start | bytes 524288 | tf_op jit(solution)/shard_map/all_to_all | solution.py:232
  123.7 27.7 %copy-start.5 = (bf16[16,64,128]{2,1,0:T(8,128)(2,1)}, bf16[16,64,128]{2,1,0:T(8,128)(2,1)S(1)}, u32[]{:S(2)}) copy-start(bf16[16,64,128]{2,1,0:T(8,128)(2,1)S(1)} %all-to-all-done.5) | copy-start | bytes 786436
  123.7 17.8 %all-to-all-start.1 = ((bf16[16,128,128]{2,1,0:T(8,128)(2,1)}), bf16[16,128,128]{2,1,0:T(8,128)(2,1)S(1)}, u32[]{:S(2)}, u32[]{:S(2)}) async-start(bf16[16,128,128]{2,1,0:T(8,128)(2,1)} %select_convert_fusion), calls=%async_computation.1 | async-start | bytes 1048576 | tf_op jit(solution)/shard_map/all_to_all | solution.py:232
  141.5 4.6 %copy-start = (bf16[16,128,128]{2,1,0:T(8,128)(2,1)}, bf16[16,128,128]{2,1,0:T(8,128)(2,1)S(1)}, u32[]{:S(2)}) copy-start(bf16[16,128,128]{2,1,0:T(8,128)(2,1)S(1)} %all-to-all-done.1) | copy-start | bytes 1572868
  141.5 25.6 %all-to-all-start.3 = ((bf16[16,64,128]{2,1,0:T(8,128)(2,1)}), bf16[16,64,128]{2,1,0:T(8,128)(2,1)S(1)}, u32[]{:S(2)}, u32[]{:S(2)}) async-start(bf16[16,64,128]{2,1,0:T(8,128)(2,1)} %select_convert_fusion.2), calls=%async_computation.3 | async-start | bytes 524288 | tf_op jit(solution)/shard_map/all_to_all | solution.py:232
  167.1 0.7 copy-start.6
  175.7 0.8 copy-start.9

commit v2 on v0

v2 whole, which is shorter than its diff:
```python
import functools
import math

import jax
import jax.numpy as jnp
from jax import lax
from jax.experimental import pallas as pl
from jax.experimental.pallas import tpu as pltpu
from jax.sharding import PartitionSpec as P


DK = 128
F32 = jnp.float32
BF16 = jnp.bfloat16
PAIR = 2 * DK
VMEM_LIMIT = 67_000_000


NT = (((1,), (1,)), ((), ()))
TN = (((0,), (0,)), ((), ()))
NN = (((1,), (0,)), ((), ()))


def mm(a, b, dims):
    return lax.dot_general(a, b, dims, preferred_element_type=F32)


def cost(flops, size):
    return pl.CostEstimate(flops=flops, bytes_accessed=size, transcendentals=0)


def pack_kernel(sizes, first, peers, cols_ref, *refs):
    count = len(sizes) * (peers - 1)
    ins, outs, bufs = refs[:4], refs[4 : 4 + count], refs[4 + count : 4 + 2 * count]
    in_sem, out_sem = refs[4 + 2 * count :]
    reads, writes = [], []
    for c, n in enumerate(sizes):
        for s in range(peers - 1):
            i = c * (peers - 1) + s
            at = pl.multiple_of((cols_ref[s + 1] + (first + sum(sizes[:c]))) * PAIR, PAIR)
            for j in range(4):
                k = 4 * i + j
                reads.append(
                    pltpu.make_async_copy(ins[j].at[:, pl.ds(at, n * PAIR)], bufs[i].at[j], in_sem.at[k])
                )
                writes.append(pltpu.make_async_copy(bufs[i].at[j], outs[i].at[j], out_sem.at[k]))
    for read in reads:
        read.start()
    for read, write in zip(reads, writes):
        read.wait()
        write.start()
    for write in writes:
        write.wait()


def pack(cols, peers, arrays, first, sizes):
    rows = arrays[0].shape[0]
    shapes = [(4, rows, n * PAIR) for n in sizes for _ in range(1, peers)]
    flat = pl.pallas_call(
        functools.partial(pack_kernel, sizes, first, peers),
        in_specs=[pl.BlockSpec(memory_space=pltpu.SMEM)] + [pl.BlockSpec(memory_space=pl.ANY)] * 4,
        out_specs=[pl.BlockSpec(memory_space=pl.ANY)] * len(shapes),
        out_shape=[jax.ShapeDtypeStruct(shape, BF16) for shape in shapes],
        scratch_shapes=[pltpu.VMEM(shape, BF16) for shape in shapes]
        + [pltpu.SemaphoreType.DMA((4 * len(shapes),))] * 2,
        cost_estimate=cost(0, 16 * rows * sum(sizes) * PAIR * (peers - 1)),
        name="pack",
    )(cols, *arrays)
    return [flat[i * (peers - 1) : (i + 1) * (peers - 1)] for i in range(len(sizes))]


def state_kernel(peers, col_ref, q_ref, k_ref, v_ref, g_ref, *rest):
    out_ref = rest[-1]
    for j in range(PAIR // DK):
        at = slice(j * DK, (j + 1) * DK)
        kv = mm(k_ref[:, at], v_ref[:, at], TN)
        qg = mm(q_ref[:, at], g_ref[:, at], TN)
        for r in rest[:peers]:
            kv = kv + mm(r[1, :, at], r[2, :, at], TN)
            qg = qg + mm(r[0, :, at], r[3, :, at], TN)
        out_ref[0, j] = kv.astype(out_ref.dtype)
        out_ref[1, j] = qg.astype(out_ref.dtype)


def states(cols, arrays, got, first, pairs, dtype=BF16, at=0, room=None, base=0, into=None):
    rows = arrays[0].shape[0]
    own = pl.BlockSpec((rows, PAIR), lambda i, c: (0, c[at] + first + i))
    there = pl.BlockSpec((4, rows, PAIR), lambda i, c: (0, 0, i))
    tokens = rows * (1 + len(got))
    per = PAIR // DK
    shared = [] if into is None else [into]
    return pl.pallas_call(
        functools.partial(state_kernel, len(got)),
        grid_spec=pltpu.PrefetchScalarGridSpec(
            num_scalar_prefetch=1,
            grid=(pairs,),
            in_specs=[own] * 4 + [there] * len(got) + [pl.BlockSpec(memory_space=pl.ANY)] * len(shared),
            out_specs=pl.BlockSpec((2, per, DK, DK), lambda i, c: (0, base + i, 0, 0)),
        ),
        out_shape=jax.ShapeDtypeStruct((2, per * (room or pairs), DK, DK), dtype),
        input_output_aliases={5 + len(got): 0} if shared else {},
        cost_estimate=cost(4 * tokens * DK * PAIR * pairs, 8 * tokens * pairs * PAIR),
        compiler_params=pltpu.CompilerParams(vmem_limit_bytes=VMEM_LIMIT),
        name="states",
    )(cols, *arrays, *got, *shared)


def gather_rows(src_ref, owns, got, which, all_ref):
    rows = owns[0].shape[0]
    mine = pl.multiple_of(src_ref[0] * rows, rows)
    for j in which:
        all_ref[j, pl.ds(mine, rows), :] = owns[j][...]
    for p, r in enumerate(got):
        at = pl.multiple_of(src_ref[p + 1] * rows, rows)
        for j in which:
            all_ref[j, pl.ds(at, rows), :] = r[j]


def within(all_ref, at):
    total = all_ref.shape[1]
    half = total // 2
    up, down = slice(0, half), slice(half, total)
    row = lax.broadcasted_iota(jnp.int32, (half, half), 0)
    column = lax.broadcasted_iota(jnp.int32, (half, half), 1)
    lower, upper = row >= column, row <= column

    def tri(x, keep):
        return jnp.where(keep, x, 0.0).astype(BF16)

    q_a, q_b = all_ref[0, up, at], all_ref[0, down, at]
    k_a, k_b = all_ref[1, up, at], all_ref[1, down, at]
    v_a, v_b = all_ref[2, up, at], all_ref[2, down, at]
    g_a, g_b = all_ref[3, up, at], all_ref[3, down, at]
    yield 0, up, mm(tri(mm(g_a, v_a, NT), lower), k_a, NN)
    yield 0, down, mm(mm(g_b, v_a, NT).astype(BF16), k_a, NN) + mm(tri(mm(g_b, v_b, NT), lower), k_b, NN)
    yield 1, up, mm(tri(mm(v_a, g_a, NT), upper), q_a, NN) + mm(mm(v_a, g_b, NT).astype(BF16), q_b, NN)
    yield 1, down, mm(tri(mm(v_b, g_b, NT), upper), q_b, NN)
    yield 2, up, mm(tri(mm(k_a, q_a, NT), upper), g_a, NN) + mm(mm(k_a, q_b, NT).astype(BF16), g_b, NN)
    yield 2, down, mm(tri(mm(k_b, q_b, NT), upper), g_b, NN)


def across(all_ref, sum_ref, j, grad, rows, at):
    if grad == 0:
        return mm(all_ref[3, rows, at], sum_ref[0, j], NT)
    if grad == 1:
        return mm(all_ref[2, rows, at], sum_ref[1, j], NT)
    return mm(all_ref[1, rows, at], sum_ref[1, j], NN)


def whole_kernel(peers, aliased, scale, col_ref, src_ref, *refs):
    owns, got, sum_ref = refs[:4], refs[4 : 4 + peers], refs[4 + peers]
    outs, all_ref = refs[5 + peers + 3 * aliased : -1], refs[-1]
    gather_rows(src_ref, owns, got, range(4), all_ref)
    for j in range(PAIR // DK):
        at = slice(j * DK, (j + 1) * DK)
        for grad, rows, value in within(all_ref, at):
            value = value + across(all_ref, sum_ref, j, grad, rows, at)
            outs[grad][rows, at] = (scale * value).astype(BF16)


def within_kernel(peers, aliased, scale, col_ref, src_ref, *refs):
    owns, got = refs[:4], refs[4 : 4 + peers]
    outs, rows_ref, all_ref = refs[4 + peers + 4 * aliased : -2], refs[-2], refs[-1]
    gather_rows(src_ref, owns, got, range(4), all_ref)
    rows_ref[...] = all_ref[1:]
    for j in range(PAIR // DK):
        at = slice(j * DK, (j + 1) * DK)
        for grad, rows, value in within(all_ref, at):
            outs[grad][rows, at] = value


def across_kernel(aliased, scale, rows_ref, sum_ref, *refs):
    parts, outs = refs[:3], refs[3 + 3 * aliased :]
    for j in range(PAIR // DK):
        at = slice(j * DK, (j + 1) * DK)
        for grad, (which, state, dims) in enumerate(((2, 0, NT), (1, 1, NT), (0, 1, NN))):
            value = parts[grad][:, at] + mm(rows_ref[which, :, at], sum_ref[state, j], dims)
            outs[grad][:, at] = (scale * value).astype(BF16)


ANY = pl.BlockSpec(memory_space=pl.ANY)


def outputs(kernel, cols, src, arrays, got, sums, first, pairs, base, room, scale, into):
    rows = arrays[0].shape[0]
    total = rows * (1 + len(got))
    whole = kernel is whole_kernel
    own = pl.BlockSpec((rows, PAIR), lambda i, c, s: (0, c[0] + first + i))
    there = pl.BlockSpec((4, rows, PAIR), lambda i, c, s: (0, 0, i))
    operands, specs = [*arrays, *got], [own] * 4 + [there] * len(got)
    here = pl.BlockSpec((total, PAIR), lambda i, c, s: (0, base + i))
    outs, shapes = [here] * 3, [jax.ShapeDtypeStruct((total, room * PAIR), BF16 if whole else F32)] * 3
    if whole:
        sums, offset = sums
        operands.append(sums)
        specs.append(pl.BlockSpec((2, PAIR // DK, DK, DK), lambda i, c, s: (0, offset + i, 0, 0)))
    else:
        outs.append(pl.BlockSpec((3, total, PAIR), lambda i, c, s: (0, 0, base + i)))
        shapes.append(jax.ShapeDtypeStruct((3, total, room * PAIR), BF16))
    start = 2 + len(operands)
    shared = [] if into is None else list(into)
    return pl.pallas_call(
        functools.partial(kernel, len(got), int(into is not None), scale),
        grid_spec=pltpu.PrefetchScalarGridSpec(
            num_scalar_prefetch=2,
            grid=(pairs,),
            in_specs=specs + [ANY] * len(shared),
            out_specs=outs,
            scratch_shapes=[pltpu.VMEM((4, total, PAIR), BF16)],
        ),
        out_shape=shapes,
        input_output_aliases={start + j: j for j in range(len(shared))},
        cost_estimate=cost(14 * total * total * PAIR * pairs, 14 * total * PAIR * pairs),
        compiler_params=pltpu.CompilerParams(vmem_limit_bytes=VMEM_LIMIT),
    )(cols, src, *operands, *shared)


def finish(parts, sums, pairs, room, scale, into):
    total = parts[0].shape[0]
    here = pl.BlockSpec((total, PAIR), lambda i: (0, i))
    shared = [] if into is None else list(into)
    return pl.pallas_call(
        functools.partial(across_kernel, int(into is not None), scale),
        grid=(pairs,),
        in_specs=[
            pl.BlockSpec((3, total, PAIR), lambda i: (0, 0, i)),
            pl.BlockSpec((2, PAIR // DK, DK, DK), lambda i: (0, i, 0, 0)),
            *[here] * 3,
            *[ANY] * len(shared),
        ],
        out_specs=[here] * 3,
        out_shape=[jax.ShapeDtypeStruct((total, room * PAIR), BF16)] * 3,
        input_output_aliases={5 + j: j for j in range(len(shared))},
        cost_estimate=cost(6 * total * DK * PAIR * pairs, 24 * total * PAIR * pairs),
        compiler_params=pltpu.CompilerParams(vmem_limit_bytes=VMEM_LIMIT),
        name="across",
    )(parts[3], sums, *parts[:3], *shared)


def running_kernel(up_ref, part_ref, out_ref):
    count = part_ref.shape[0]

    def run(order):
        total = jnp.zeros(part_ref.shape[1:], F32)
        for i in order:
            out_ref[i] = total.astype(BF16)
            total = total + part_ref[i].astype(F32)

    @pl.when(up_ref[0] == 1)
    def _():
        run(range(count))

    @pl.when(up_ref[0] == 0)
    def _():
        run(reversed(range(count)))


def scan(own):
    count = lax.axis_size("seq")
    part = own.reshape(count, -1, DK)
    parts = lax.all_to_all(part, "seq", 0, 0, tiled=True)
    up = (lax.axis_index("seq") < count // 2).astype(jnp.int32).reshape(1)
    mine = pl.pallas_call(
        running_kernel,
        in_specs=[pl.BlockSpec(memory_space=pltpu.SMEM), pl.BlockSpec(memory_space=pltpu.VMEM)],
        out_specs=pl.BlockSpec(memory_space=pltpu.VMEM),
        out_shape=jax.ShapeDtypeStruct(parts.shape, BF16),
        cost_estimate=cost(parts.size, 4 * parts.size),
        name="running",
    )(up, parts)
    return lax.all_to_all(mine, "seq", 0, 0, tiled=True).reshape(own.shape)


def local(queries, key_vectors, value_vectors, out_grads):
    return grads((queries, key_vectors, value_vectors, out_grads))


def grads(arrays):
    peers = lax.axis_size("head")
    place = lax.axis_index("head")
    rows = arrays[0].shape[0]
    pairs_here = arrays[0].shape[1] // PAIR // peers
    total_tokens = rows * peers * lax.axis_size("seq")
    scale = 1.0 / math.sqrt(DK * total_tokens)
    late = pairs_here // 2
    early = pairs_here - late
    sizes = [early - early // 2, early // 2]
    split = len(sizes)
    sizes += [n for n in (late - 2 * (late // 4), late // 4, late // 4) if n]
    firsts = [sum(sizes[:i]) for i in range(len(sizes))]
    shifts = range(1, peers)
    cols = ((place + jnp.arange(peers)) % peers * pairs_here).astype(jnp.int32)
    src = ((place - jnp.arange(peers)) % peers).astype(jnp.int32)

    def move(values):
        return [
            lax.ppermute(value, "head", [(i, (i + s) % peers) for i in range(peers)])
            for s, value in zip(shifts, values)
        ]

    late_sent = [states(cols, arrays, [], early, late, BF16, s) for s in shifts]
    late_got = move(late_sent)
    got = []
    for packed in pack(cols, peers, arrays, 0, sizes):
        got.append(move(packed))
    late_sums = states(cols, arrays, [], early, late, F32)
    for piece in late_got:
        late_sums = late_sums + piece.astype(F32)
    late_sums = scan(late_sums.astype(BF16))
    early_sums = parts = None
    for c in range(split):
        early_sums = states(
            cols, arrays, got[c], firsts[c], sizes[c], room=early, base=firsts[c], into=early_sums
        )
    for c in range(split):
        parts = outputs(
            within_kernel, cols, src, arrays, got[c], None, firsts[c], sizes[c], firsts[c], early, scale, parts
        )
    early_sums = scan(early_sums)

    outs = None
    for c in range(split, len(sizes)):
        if c == len(sizes) - 1:
            outs = finish(parts, early_sums, early, pairs_here, scale, outs)
        sums = (late_sums, firsts[c] - early)
        outs = outputs(
            whole_kernel, cols, src, arrays, got[c], sums, firsts[c], sizes[c], firsts[c], pairs_here, scale, outs
        )
    return tuple(outs)


def solution(mesh):
    tokens = P(("seq", "head"), None)
    return jax.shard_map(
        local,
        mesh=mesh,
        in_specs=(tokens,) * 4,
        out_specs=(P("seq", "head"),) * 3,
        check_vma=False,
    )
```

time: 163 us -> 164 us (level)
  waiting for transfers between devices: 43.7 us -> 63 us
  other arithmetic: 14 us -> 3.45 us
  starting transfers between devices: 39.5 us -> 30.1 us
  Pallas kernels: 59.6 us -> 65.4 us
  local copies, waits for them, and re-layouts: 2.78 us -> 0.01 us
    ppermute x21 -> x6, starting transfers between devices: 39.5 us -> 8.7 us  [move(): lax.ppermute(value, 'head', [(i, (i + s) % peers) for i in range(peers)])]
    all_to_all x0 -> x4, waiting for transfers between devices: none -> 23.1 us  [the longest x2 12.3 us: scan(): parts = lax.all_to_all(part, 'seq', 0, 0, tiled=True)]
    all_to_all x0 -> x4, starting transfers between devices: none -> 21.4 us  [the longest x2 12.7 us: scan(): parts = lax.all_to_all(part, 'seq', 0, 0, tiled=True)]
    convert_element_type x15 -> x1, other arithmetic: 8.53 us -> 2.31 us  [grads(): late_sums = scan(late_sums.astype(BF16))]
    pallas_call x10 -> x9, Pallas kernels: 44.6 us -> 48.9 us  [the longest x5 34.1 us: outputs(): pl.pallas_call(functools.partial(kernel, len(got), int(into is not None),...]
    ppermute x21 -> x6, waiting for transfers between devices: 43.7 us -> 39.8 us  [move(): lax.ppermute(value, 'head', [(i, (i + s) % peers) for i in range(peers)])]
    unnamed x14 -> x2, local copies, waits for them, and re-layouts: 2.78 us -> 0.01 us
    add x4 -> x0, other arithmetic: 2.46 us -> none  [the longest x3 1.26 us: scan(): chip = own + other]
  transfers between devices with their start and end apart: 21 -> 10, of which waited for: 6 -> 5; matrix products, arithmetic and copies ran while one was open for 8% -> 2% of each run, Pallas kernels for 30% -> 34%
where the time goes in v2:
time: 164 us; the launch traced here: 163 us
  Pallas kernels  65.4 us (40%)
  waiting for transfers between devices  63 us (38%)
  starting transfers between devices  30.1 us (18%)
  other arithmetic  3.45 us (2%)
    ppermute x6, waiting for transfers between devices, move(): lax.ppermute(value, 'head', [(i, (i + s) % peers) for i in range(peers)])  39.8 us
    pallas_call x5, Pallas kernels, outputs(): pl.pallas_call(functools.partial(kernel, len(got), int(into is not None),...  34.1 us
    pallas_call x4, Pallas kernels, states(): pl.pallas_call(functools.partial(state_kernel, len(got)), grid_spec=pltpu...  16.5 us
    all_to_all x2, starting transfers between devices, scan(): parts = lax.all_to_all(part, 'seq', 0, 0, tiled=True)  12.7 us
    all_to_all x2, waiting for transfers between devices, scan(): parts = lax.all_to_all(part, 'seq', 0, 0, tiled=True)  12.3 us
    all_to_all x2, waiting for transfers between devices, scan(): return lax.all_to_all(mine, 'seq', 0, 0, tiled=True).reshape(own.shape)  10.8 us
    ppermute x6, starting transfers between devices, move(): lax.ppermute(value, 'head', [(i, (i + s) % peers) for i in range(peers)])  8.7 us
    all_to_all x2, starting transfers between devices, scan(): return lax.all_to_all(mine, 'seq', 0, 0, tiled=True).reshape(own.shape)  8.68 us
  transfers between devices with their start and end apart: 10, of which 5 were waited for; matrix products, arithmetic and copies ran while one was open for 2% of the time, Pallas kernels for 34%

profile of v2, /device:TPU:0, one launch (start us, length us, event | category | flops | bytes accessed | tf_op | source)
XLA Modules:
  0.0 162.6 jit_solution(12642819428652276205)
XLA Ops:
  0.6 0.6 fusion.cols_ref.col_ref
  1.2 4.8 %states.5 = bf16[2,8,128,128]{3,2,1,0:T(8,128)(2,1)} custom-call(s32[2]{0:T(128)} %fusion.cols_ref.col_ref, bf16[256,4096]{1,0:T(8,128)(2,1)} %refs_0_.11, bf16[256,4096]{1,0:T(8,128)(2,1)} %refs_1_.11, bf16[256,4096]{1,0:T(8,128)(2,1)} %refs_2_.11, bf16[256,4096]{1,0:T(8,128)(2,1)} %refs_3_.11), custom_call_target="tpu_custom_call" | custom-call | flops 134217728 | bytes 2097152 | tf_op jit(solution)/shard_map/states/pallas_call | solution.py:92
  5.9 3.0 %collective-permute-start.1 = (bf16[2,8,128,128]{3,2,1,0:T(8,128)(2,1)}, bf16[2,8,128,128]{3,2,1,0:T(8,128)(2,1)}, u32[]{:S(2)}, u32[]{:S(2)}) collective-permute-start(bf16[2,8,128,128]{3,2,1,0:T(8,128)(2,1)} %states.5), channel_id=1, source_target_pairs={{0,1},{1,0},{2,3},{3,2},{4,5},{5,4},{6,7},{7,6},{8,9},{9,8},{10,11... | collective-permute-start | bytes 1572872 | tf_op jit(solution)/shard_map/ppermute | solution.py:297
  8.9 4.7 %pack.1 = (bf16[4,256,512]{2,1,0:T(8,128)(2,1)}, bf16[4,256,512]{2,1,0:T(8,128)(2,1)}, bf16[4,256,512]{2,1,0:T(8,128)(2,1)}, bf16[4,256,256]{2,1,0:T(8,128)(2,1)}, bf16[4,256,256]{2,1,0:T(8,128)(2,1)}) custom-call(s32[2]{0:T(128)} %fusion.cols_ref.col_ref, bf16[256,4096]{1,0:T(8,128)(2,1)} %refs_0_.11, bf16[256,4096]{1,0:T(8,128)(2,1)} %refs_1_.11, ...), custom_call_target="tpu_custom_call" | custom-call | bytes 8388608 | tf_op jit(solution)/shard_map/pack/pallas_call | solution.py:59
  13.6 0.1 collective-permute-start.2
  13.7 2.0 %collective-permute-start.3 = (bf16[4,256,512]{2,1,0:T(8,128)(2,1)}, bf16[4,256,512]{2,1,0:T(8,128)(2,1)}, u32[]{:S(2)}, u32[]{:S(2)}) collective-permute-start(bf16[4,256,512]{2,1,0:T(8,128)(2,1)} %get-tuple-element.27), channel_id=1, source_target_pairs={{0,1},{1,0},{2,3},{3,2},{4,5},{5,4},{6,7},{7,6},{8,9},{9,8},{10,11... | collective-permute-start | bytes 3145736 | tf_op jit(solution)/shard_map/ppermute | solution.py:297
  15.7 4.8 %states.4 = f32[2,8,128,128]{3,2,1,0:T(8,128)} custom-call(s32[2]{0:T(128)} %fusion.cols_ref.col_ref, bf16[256,4096]{1,0:T(8,128)(2,1)} %refs_0_.11, bf16[256,4096]{1,0:T(8,128)(2,1)} %refs_1_.11, bf16[256,4096]{1,0:T(8,128)(2,1)} %refs_2_.11, bf16[256,4096]{1,0:T(8,128)(2,1)} %refs_3_.11), custom_call_target="tpu_custom_call" | custom-call | flops 134217728 | bytes 2097152 | tf_op jit(solution)/shard_map/states/pallas_call | solution.py:92
  20.5 1.5 collective-permute-done.1
  22.0 2.3 %add_convert_fusion = bf16[2,8,128,128]{3,2,1,0:T(8,128)(2,1)} fusion(f32[2,8,128,128]{3,2,1,0:T(8,128)} %states.4, bf16[2,8,128,128]{3,2,1,0:T(8,128)(2,1)} %collective-permute-done.1), kind=kLoop, calls=%fused_computation | loop fusion | flops 786432 | bytes 2097152 | tf_op jit(solution)/shard_map/convert_element_type | solution.py:309
  24.3 6.5 %all-to-all-start = ((bf16[16,128,128]{2,1,0:T(8,128)(2,1)}), bf16[16,128,128]{2,1,0:T(8,128)(2,1)}, u32[]{:S(2)}, u32[]{:S(2)}) async-start(bf16[16,128,128]{2,1,0:T(8,128)(2,1)} %bitcast.1), calls=%async_computation | async-start | bytes 1048576 | tf_op jit(solution)/shard_map/all_to_all | solution.py:261
  30.8 35.3 %collective-permute-done.3.refs_4_.rest_0_ = bf16[4,256,512]{2,1,0:T(8,128)(2,1)} collective-permute-done((bf16[4,256,512]{2,1,0:T(8,128)(2,1)}, bf16[4,256,512]{2,1,0:T(8,128)(2,1)}, u32[]{:S(2)}, u32[]{:S(2)}) %collective-permute-start.3) | collective-permute-done | bytes 1048608 | tf_op jit(solution)/shard_map/ppermute | solution.py:297
  66.1 3.4 %states.6.rest_1_ = bf16[2,8,128,128]{3,2,1,0:T(8,128)(2,1)} custom-call(s32[2]{0:T(128)} %fusion.cols_ref.col_ref, bf16[256,4096]{1,0:T(8,128)(2,1)} %refs_0_.11, bf16[256,4096]{1,0:T(8,128)(2,1)} %refs_1_.11, bf16[256,4096]{1,0:T(8,128)(2,1)} %refs_2_.11, bf16[256,4096]{1,0:T(8,128)(2,1)} %refs_3_.11, ...), custom_call_target="tpu_custom_call" | custom-call | flops 134217728 | bytes 2097152 | tf_op jit(solution)/shard_map/states/pallas_call | solution.py:92
  69.5 0.0 collective-permute-done.2.refs_4_.rest_0_
  69.5 3.5 %states.7 = bf16[2,8,128,128]{3,2,1,0:T(8,128)(2,1)} custom-call(s32[2]{0:T(128)} %fusion.cols_ref.col_ref, bf16[256,4096]{1,0:T(8,128)(2,1)} %refs_0_.11, bf16[256,4096]{1,0:T(8,128)(2,1)} %refs_1_.11, bf16[256,4096]{1,0:T(8,128)(2,1)} %refs_2_.11, bf16[256,4096]{1,0:T(8,128)(2,1)} %refs_3_.11, ...), custom_call_target="tpu_custom_call", output_to_operand_aliasing={{}: (6, {})} | custom-call | flops 134217728 | bytes 2097152 | tf_op jit(solution)/shard_map/states/pallas_call | solution.py:92
  73.0 6.2 %all-to-all-start.2 = ((bf16[16,128,128]{2,1,0:T(8,128)(2,1)}), bf16[16,128,128]{2,1,0:T(8,128)(2,1)S(1)}, u32[]{:S(2)}, u32[]{:S(2)}) async-start(bf16[16,128,128]{2,1,0:T(8,128)(2,1)} %bitcast.5), calls=%async_computation.2 | async-start | bytes 1048576 | tf_op jit(solution)/shard_map/all_to_all | solution.py:261
  79.2 1.9 %running.2 = bf16[16,128,128]{2,1,0:T(8,128)(2,1)} custom-call(s32[1]{0:T(128)} %bitcast.up_ref, bf16[16,128,128]{2,1,0:T(8,128)(2,1)} %all-to-all-done.part_ref), custom_call_target="tpu_custom_call" | custom-call | flops 262144 | bytes 1048576 | tf_op jit(solution)/shard_map/running/pallas_call | solution.py:263
  81.1 12.3 %all-to-all-done.2.part_ref = bf16[16,128,128]{2,1,0:T(8,128)(2,1)S(1)} async-done(((bf16[16,128,128]{2,1,0:T(8,128)(2,1)}), bf16[16,128,128]{2,1,0:T(8,128)(2,1)S(1)}, u32[]{:S(2)}, u32[]{:S(2)}) %all-to-all-start.2) | async-done | bytes 524320 | tf_op jit(solution)/shard_map/all_to_all | solution.py:261
  93.4 4.2 %all-to-all-start.1 = ((bf16[16,128,128]{2,1,0:T(8,128)(2,1)}), bf16[16,128,128]{2,1,0:T(8,128)(2,1)}, u32[]{:S(2)}, u32[]{:S(2)}) async-start(bf16[16,128,128]{2,1,0:T(8,128)(2,1)} %running.2), calls=%async_computation.1 | async-start | bytes 1048576 | tf_op jit(solution)/shard_map/all_to_all | solution.py:271
  97.7 1.6 collective-permute-start.5
  99.2 1.9 %running.3 = bf16[16,128,128]{2,1,0:T(8,128)(2,1)} custom-call(s32[1]{0:T(128)} %bitcast.up_ref, bf16[16,128,128]{2,1,0:T(8,128)(2,1)} %copy-done), custom_call_target="tpu_custom_call" | custom-call | flops 262144 | bytes 1048576 | tf_op jit(solution)/shard_map/running/pallas_call | solution.py:263
  101.2 10.8 %all-to-all-done.1 = bf16[16,128,128]{2,1,0:T(8,128)(2,1)} async-done(((bf16[16,128,128]{2,1,0:T(8,128)(2,1)}), bf16[16,128,128]{2,1,0:T(8,128)(2,1)}, u32[]{:S(2)}, u32[]{:S(2)}) %all-to-all-start.1) | async-done | bytes 524320 | tf_op jit(solution)/shard_map/all_to_all | solution.py:271
  112.0 4.4 %all-to-all-start.3 = ((bf16[16,128,128]{2,1,0:T(8,128)(2,1)}), bf16[16,128,128]{2,1,0:T(8,128)(2,1)}, u32[]{:S(2)}, u32[]{:S(2)}) async-start(bf16[16,128,128]{2,1,0:T(8,128)(2,1)} %running.3), calls=%async_computation.3 | async-start | bytes 1048576 | tf_op jit(solution)/shard_map/all_to_all | solution.py:271
  116.4 1.6 collective-permute-start
  118.0 0.5 collective-permute-start.4
  118.5 0.6 and_select_fusion.src_ref
  119.1 7.9 %shard_map.67 = (f32[512,1024]{1,0:T(8,128)}, f32[512,1024]{1,0:T(8,128)}, f32[512,1024]{1,0:T(8,128)}, bf16[3,512,1024]{2,1,0:T(8,128)(2,1)}) custom-call(s32[2]{0:T(128)} %fusion.cols_ref.col_ref, s32[2]{0:T(128)} %and_select_fusion.src_ref, bf16[256,4096]{1,0:T(8,128)(2,1)} %refs_0_.11, bf16[256,4096]{1,0:T(8,128)(2,1)} %refs_1_.11, ...), custom_call_target="tpu_custom_call" | custom-call | flops 1879048192 | bytes 3670016 | tf_op jit(solution)/shard_map/pallas_call | solution.py:202
  127.0 7.9 %shard_map.68 = (f32[512,1024]{1,0:T(8,128)}, f32[512,1024]{1,0:T(8,128)}, f32[512,1024]{1,0:T(8,128)}, bf16[3,512,1024]{2,1,0:T(8,128)(2,1)}) custom-call(s32[2]{0:T(128)} %fusion.cols_ref.col_ref, s32[2]{0:T(128)} %and_select_fusion.src_ref, bf16[256,4096]{1,0:T(8,128)(2,1)} %refs_0_.11, ...), custom_call_target="tpu_custom_call", output_to_operand_aliasing={{0}: (7, {}), {1}: (8, {}), {2}: (9, {}), {3}: (10, {})} | custom-call | flops 1879048192 | bytes 3670016 | tf_op jit(solution)/shard_map/pallas_call | solution.py:202
  134.9 7.9 %shard_map.69 = (bf16[512,2048]{1,0:T(8,128)(2,1)}, bf16[512,2048]{1,0:T(8,128)(2,1)}, bf16[512,2048]{1,0:T(8,128)(2,1)}) custom-call(s32[2]{0:T(128)} %fusion.cols_ref.col_ref, s32[2]{0:T(128)} %and_select_fusion.src_ref, bf16[256,4096]{1,0:T(8,128)(2,1)} %refs_0_.11, bf16[256,4096]{1,0:T(8,128)(2,1)} %refs_1_.11, bf16[256,4096]{1,0:T(8,128)(2,1)} %refs_2_.11, ...), custom_call_target="tpu_custom_call" | custom-call | flops 1879048192 | bytes 3670016 | tf_op jit(solution)/shard_map/pallas_call | solution.py:202
  142.8 3.1 %collective-permute-done.4.refs_4_ = bf16[4,256,256]{2,1,0:T(8,128)(2,1)} collective-permute-done((bf16[4,256,256]{2,1,0:T(8,128)(2,1)}, bf16[4,256,256]{2,1,0:T(8,128)(2,1)}, u32[]{:S(2)}, u32[]{:S(2)}) %collective-permute-start.4) | collective-permute-done | bytes 524320 | tf_op jit(solution)/shard_map/ppermute | solution.py:297
  145.9 5.2 %shard_map.70 = (bf16[512,2048]{1,0:T(8,128)(2,1)}, bf16[512,2048]{1,0:T(8,128)(2,1)}, bf16[512,2048]{1,0:T(8,128)(2,1)}) custom-call(s32[2]{0:T(128)} %fusion.cols_ref.col_ref, s32[2]{0:T(128)} %and_select_fusion.src_ref, bf16[256,4096]{1,0:T(8,128)(2,1)} %refs_0_.11, ...), custom_call_target="tpu_custom_call", output_to_operand_aliasing={{0}: (8, {}), {1}: (9, {}), {2}: (10, {})} | custom-call | flops 939524096 | bytes 1835008 | tf_op jit(solution)/shard_map/pallas_call | solution.py:202
  151.1 6.3 %across.1 = (bf16[512,2048]{1,0:T(8,128)(2,1)}, bf16[512,2048]{1,0:T(8,128)(2,1)}, bf16[512,2048]{1,0:T(8,128)(2,1)}) custom-call(bf16[3,512,1024]{2,1,0:T(8,128)(2,1)} %get-tuple-element.32.rows_ref, bf16[2,8,128,128]{3,2,1,0:T(8,128)(2,1)} %bitcast.4.sum_ref, ...), custom_call_target="tpu_custom_call", output_to_operand_aliasing={{0}: (5, {}), {1}: (6, {}), {2}: (7, {})} | custom-call | flops 402653184 | bytes 12582912 | tf_op jit(solution)/shard_map/across/pallas_call | solution.py:222
  157.4 5.2 %shard_map.71 = (bf16[512,2048]{1,0:T(8,128)(2,1)}, bf16[512,2048]{1,0:T(8,128)(2,1)}, bf16[512,2048]{1,0:T(8,128)(2,1)}) custom-call(s32[2]{0:T(128)} %fusion.cols_ref.col_ref, s32[2]{0:T(128)} %and_select_fusion.src_ref, bf16[256,4096]{1,0:T(8,128)(2,1)} %refs_0_.11, ...), custom_call_target="tpu_custom_call", output_to_operand_aliasing={{0}: (8, {}), {1}: (9, {}), {2}: (10, {})} | custom-call | flops 939524096 | bytes 1835008 | tf_op jit(solution)/shard_map/pallas_call | solution.py:202
  (6 shorter events, 0.0 us)
Async XLA Ops:
  5.9 16.1 %collective-permute-start.1 = (bf16[2,8,128,128]{3,2,1,0:T(8,128)(2,1)}, bf16[2,8,128,128]{3,2,1,0:T(8,128)(2,1)}, u32[]{:S(2)}, u32[]{:S(2)}) collective-permute-start(bf16[2,8,128,128]{3,2,1,0:T(8,128)(2,1)} %states.5), channel_id=1, source_target_pairs={{0,1},{1,0},{2,3},{3,2},{4,5},{5,4},{6,7},{7,6},{8,9},{9,8},{10,11... | collective-permute-start | bytes 1572872 | tf_op jit(solution)/shard_map/ppermute | solution.py:297
  13.6 55.9 %collective-permute-start.2 = (bf16[4,256,512]{2,1,0:T(8,128)(2,1)}, bf16[4,256,512]{2,1,0:T(8,128)(2,1)}, u32[]{:S(2)}, u32[]{:S(2)}) collective-permute-start(bf16[4,256,512]{2,1,0:T(8,128)(2,1)} %get-tuple-element.26), channel_id=1, source_target_pairs={{0,1},{1,0},{2,3},{3,2},{4,5},{5,4},{6,7},{7,6},{8,9},{9,8},{10,11... | collective-permute-start | bytes 3145736 | tf_op jit(solution)/shard_map/ppermute | solution.py:297
  13.7 52.4 %collective-permute-start.3 = (bf16[4,256,512]{2,1,0:T(8,128)(2,1)}, bf16[4,256,512]{2,1,0:T(8,128)(2,1)}, u32[]{:S(2)}, u32[]{:S(2)}) collective-permute-start(bf16[4,256,512]{2,1,0:T(8,128)(2,1)} %get-tuple-element.27), channel_id=1, source_target_pairs={{0,1},{1,0},{2,3},{3,2},{4,5},{5,4},{6,7},{7,6},{8,9},{9,8},{10,11... | collective-permute-start | bytes 3145736 | tf_op jit(solution)/shard_map/ppermute | solution.py:297
  24.3 48.7 %all-to-all-start = ((bf16[16,128,128]{2,1,0:T(8,128)(2,1)}), bf16[16,128,128]{2,1,0:T(8,128)(2,1)}, u32[]{:S(2)}, u32[]{:S(2)}) async-start(bf16[16,128,128]{2,1,0:T(8,128)(2,1)} %bitcast.1), calls=%async_computation | async-start | bytes 1048576 | tf_op jit(solution)/shard_map/all_to_all | solution.py:261
  73.0 20.5 %all-to-all-start.2 = ((bf16[16,128,128]{2,1,0:T(8,128)(2,1)}), bf16[16,128,128]{2,1,0:T(8,128)(2,1)S(1)}, u32[]{:S(2)}, u32[]{:S(2)}) async-start(bf16[16,128,128]{2,1,0:T(8,128)(2,1)} %bitcast.5), calls=%async_computation.2 | async-start | bytes 1048576 | tf_op jit(solution)/shard_map/all_to_all | solution.py:261
  93.4 5.8 %copy-start = (bf16[16,128,128]{2,1,0:T(8,128)(2,1)}, bf16[16,128,128]{2,1,0:T(8,128)(2,1)S(1)}, u32[]{:S(2)}) copy-start(bf16[16,128,128]{2,1,0:T(8,128)(2,1)S(1)} %all-to-all-done.2.part_ref) | copy-start | bytes 1572868
  93.4 18.5 %all-to-all-start.1 = ((bf16[16,128,128]{2,1,0:T(8,128)(2,1)}), bf16[16,128,128]{2,1,0:T(8,128)(2,1)}, u32[]{:S(2)}, u32[]{:S(2)}) async-start(bf16[16,128,128]{2,1,0:T(8,128)(2,1)} %running.2), calls=%async_computation.1 | async-start | bytes 1048576 | tf_op jit(solution)/shard_map/all_to_all | solution.py:271
  97.7 37.2 %collective-permute-start.5 = (bf16[4,256,512]{2,1,0:T(8,128)(2,1)}, bf16[4,256,512]{2,1,0:T(8,128)(2,1)}, u32[]{:S(2)}, u32[]{:S(2)}) collective-permute-start(bf16[4,256,512]{2,1,0:T(8,128)(2,1)} %get-tuple-element.37), channel_id=1, source_target_pairs={{0,1},{1,0},{2,3},{3,2},{4,5},{5,4},{6,7},{7,6},{8,9},{9,8},{10,11... | collective-permute-start | bytes 3145736 | tf_op jit(solution)/shard_map/ppermute | solution.py:297
  112.0 39.1 %all-to-all-start.3 = ((bf16[16,128,128]{2,1,0:T(8,128)(2,1)}), bf16[16,128,128]{2,1,0:T(8,128)(2,1)}, u32[]{:S(2)}, u32[]{:S(2)}) async-start(bf16[16,128,128]{2,1,0:T(8,128)(2,1)} %running.3), calls=%async_computation.3 | async-start | bytes 1048576 | tf_op jit(solution)/shard_map/all_to_all | solution.py:271
  116.4 40.9 %collective-permute-start = (bf16[4,256,256]{2,1,0:T(8,128)(2,1)}, bf16[4,256,256]{2,1,0:T(8,128)(2,1)}, u32[]{:S(2)}, u32[]{:S(2)}) collective-permute-start(bf16[4,256,256]{2,1,0:T(8,128)(2,1)} %get-tuple-element.25), channel_id=1, source_target_pairs={{0,1},{1,0},{2,3},{3,2},{4,5},{5,4},{6,7},{7,6},{8,9},{9,8},{10,11... | collective-permute-start | bytes 1572872 | tf_op jit(solution)/shard_map/ppermute | solution.py:297
  118.0 27.9 %collective-permute-start.4 = (bf16[4,256,256]{2,1,0:T(8,128)(2,1)}, bf16[4,256,256]{2,1,0:T(8,128)(2,1)}, u32[]{:S(2)}, u32[]{:S(2)}) collective-permute-start(bf16[4,256,256]{2,1,0:T(8,128)(2,1)} %get-tuple-element.36), channel_id=1, source_target_pairs={{0,1},{1,0},{2,3},{3,2},{4,5},{5,4},{6,7},{7,6},{8,9},{9,8},{10,11... | collective-permute-start | bytes 1572872 | tf_op jit(solution)/shard_map/ppermute | solution.py:297

commit v3 on v2

--- a/solution.py
+++ b/solution.py
@@ -29,7 +29,8 @@
     return pl.CostEstimate(flops=flops, bytes_accessed=size, transcendentals=0)
 
 
-def pack_kernel(sizes, first, peers, cols_ref, *refs):
+def pack_kernel(sizes, first, peers, *refs):
+    cols, refs = refs[: peers - 1], refs[peers - 1 :]
     count = len(sizes) * (peers - 1)
     ins, outs, bufs = refs[:4], refs[4 : 4 + count], refs[4 + count : 4 + 2 * count]
     in_sem, out_sem = refs[4 + 2 * count :]
@@ -37,7 +38,7 @@
     for c, n in enumerate(sizes):
         for s in range(peers - 1):
             i = c * (peers - 1) + s
-            at = pl.multiple_of((cols_ref[s + 1] + (first + sum(sizes[:c]))) * PAIR, PAIR)
+            at = pl.multiple_of((cols[s][0] + (first + sum(sizes[:c]))) * PAIR, PAIR)
             for j in range(4):
                 k = 4 * i + j
                 reads.append(
@@ -58,14 +59,14 @@
     shapes = [(4, rows, n * PAIR) for n in sizes for _ in range(1, peers)]
     flat = pl.pallas_call(
         functools.partial(pack_kernel, sizes, first, peers),
-        in_specs=[pl.BlockSpec(memory_space=pltpu.SMEM)] + [pl.BlockSpec(memory_space=pl.ANY)] * 4,
+        in_specs=[pl.BlockSpec(memory_space=pltpu.SMEM)] * (peers - 1) + [pl.BlockSpec(memory_space=pl.ANY)] * 4,
         out_specs=[pl.BlockSpec(memory_space=pl.ANY)] * len(shapes),
         out_shape=[jax.ShapeDtypeStruct(shape, BF16) for shape in shapes],
         scratch_shapes=[pltpu.VMEM(shape, BF16) for shape in shapes]
         + [pltpu.SemaphoreType.DMA((4 * len(shapes),))] * 2,
         cost_estimate=cost(0, 16 * rows * sum(sizes) * PAIR * (peers - 1)),
         name="pack",
-    )(cols, *arrays)
+    )(*cols[1:], *arrays)
     return [flat[i * (peers - 1) : (i + 1) * (peers - 1)] for i in range(len(sizes))]
 
 
@@ -84,7 +85,7 @@
 
 def states(cols, arrays, got, first, pairs, dtype=BF16, at=0, room=None, base=0, into=None):
     rows = arrays[0].shape[0]
-    own = pl.BlockSpec((rows, PAIR), lambda i, c: (0, c[at] + first + i))
+    own = pl.BlockSpec((rows, PAIR), lambda i, c: (0, c[0] + first + i))
     there = pl.BlockSpec((4, rows, PAIR), lambda i, c: (0, 0, i))
     tokens = rows * (1 + len(got))
     per = PAIR // DK
@@ -102,16 +103,16 @@
         cost_estimate=cost(4 * tokens * DK * PAIR * pairs, 8 * tokens * pairs * PAIR),
         compiler_params=pltpu.CompilerParams(vmem_limit_bytes=VMEM_LIMIT),
         name="states",
-    )(cols, *arrays, *got, *shared)
-
-
-def gather_rows(src_ref, owns, got, which, all_ref):
+    )(cols[at], *arrays, *got, *shared)
+
+
+def gather_rows(src, owns, got, which, all_ref):
     rows = owns[0].shape[0]
-    mine = pl.multiple_of(src_ref[0] * rows, rows)
+    mine = pl.multiple_of(src[0][0] * rows, rows)
     for j in which:
         all_ref[j, pl.ds(mine, rows), :] = owns[j][...]
     for p, r in enumerate(got):
-        at = pl.multiple_of(src_ref[p + 1] * rows, rows)
+        at = pl.multiple_of(src[p + 1][0] * rows, rows)
         for j in which:
             all_ref[j, pl.ds(at, rows), :] = r[j]
 
@@ -127,16 +128,21 @@
     def tri(x, keep):
         return jnp.where(keep, x, 0.0).astype(BF16)
 
-    q_a, q_b = all_ref[0, up, at], all_ref[0, down, at]
-    k_a, k_b = all_ref[1, up, at], all_ref[1, down, at]
-    v_a, v_b = all_ref[2, up, at], all_ref[2, down, at]
-    g_a, g_b = all_ref[3, up, at], all_ref[3, down, at]
-    yield 0, up, mm(tri(mm(g_a, v_a, NT), lower), k_a, NN)
-    yield 0, down, mm(mm(g_b, v_a, NT).astype(BF16), k_a, NN) + mm(tri(mm(g_b, v_b, NT), lower), k_b, NN)
-    yield 1, up, mm(tri(mm(v_a, g_a, NT), upper), q_a, NN) + mm(mm(v_a, g_b, NT).astype(BF16), q_b, NN)
-    yield 1, down, mm(tri(mm(v_b, g_b, NT), upper), q_b, NN)
-    yield 2, up, mm(tri(mm(k_a, q_a, NT), upper), g_a, NN) + mm(mm(k_a, q_b, NT).astype(BF16), g_b, NN)
-    yield 2, down, mm(tri(mm(k_b, q_b, NT), upper), g_b, NN)
+    q, k, v, g = (all_ref[j, :, at] for j in range(4))
+    probe = mm(g, v[up], NT)
+    probe = jnp.concatenate([tri(probe[up], lower), probe[down].astype(BF16)], 0)
+    first = mm(probe, k[up], NN)
+    second = mm(tri(mm(g[down], v[down], NT), lower), k[down], NN)
+    yield 0, up, first[up]
+    yield 0, down, first[down] + second
+    for grad, left, right in ((1, v, g), (2, k, q)):
+        other = q if grad == 1 else g
+        late = mm(left, right[down], NT)
+        late = jnp.concatenate([late[up].astype(BF16), tri(late[down], upper)], 0)
+        second = mm(late, other[down], NN)
+        first = mm(tri(mm(left[up], right[up], NT), upper), other[up], NN)
+        yield grad, up, first + second[up]
+        yield grad, down, second[down]
 
 
 def across(all_ref, sum_ref, j, grad, rows, at):
@@ -147,10 +153,11 @@
     return mm(all_ref[1, rows, at], sum_ref[1, j], NN)
 
 
-def whole_kernel(peers, aliased, scale, col_ref, src_ref, *refs):
+def whole_kernel(peers, aliased, scale, col_ref, *refs):
+    src, refs = refs[: peers + 1], refs[peers + 1 :]
     owns, got, sum_ref = refs[:4], refs[4 : 4 + peers], refs[4 + peers]
     outs, all_ref = refs[5 + peers + 3 * aliased : -1], refs[-1]
-    gather_rows(src_ref, owns, got, range(4), all_ref)
+    gather_rows(src, owns, got, range(4), all_ref)
     for j in range(PAIR // DK):
         at = slice(j * DK, (j + 1) * DK)
         for grad, rows, value in within(all_ref, at):
@@ -158,10 +165,11 @@
             outs[grad][rows, at] = (scale * value).astype(BF16)
 
 
-def within_kernel(peers, aliased, scale, col_ref, src_ref, *refs):
+def within_kernel(peers, aliased, scale, col_ref, *refs):
+    src, refs = refs[: peers + 1], refs[peers + 1 :]
     owns, got = refs[:4], refs[4 : 4 + peers]
     outs, rows_ref, all_ref = refs[4 + peers + 4 * aliased : -2], refs[-2], refs[-1]
-    gather_rows(src_ref, owns, got, range(4), all_ref)
+    gather_rows(src, owns, got, range(4), all_ref)
     rows_ref[...] = all_ref[1:]
     for j in range(PAIR // DK):
         at = slice(j * DK, (j + 1) * DK)
@@ -185,24 +193,24 @@
     rows = arrays[0].shape[0]
     total = rows * (1 + len(got))
     whole = kernel is whole_kernel
-    own = pl.BlockSpec((rows, PAIR), lambda i, c, s: (0, c[0] + first + i))
-    there = pl.BlockSpec((4, rows, PAIR), lambda i, c, s: (0, 0, i))
+    own = pl.BlockSpec((rows, PAIR), lambda i, c, *s: (0, c[0] + first + i))
+    there = pl.BlockSpec((4, rows, PAIR), lambda i, c, *s: (0, 0, i))
     operands, specs = [*arrays, *got], [own] * 4 + [there] * len(got)
-    here = pl.BlockSpec((total, PAIR), lambda i, c, s: (0, base + i))
+    here = pl.BlockSpec((total, PAIR), lambda i, c, *s: (0, base + i))
     outs, shapes = [here] * 3, [jax.ShapeDtypeStruct((total, room * PAIR), BF16 if whole else F32)] * 3
     if whole:
         sums, offset = sums
         operands.append(sums)
-        specs.append(pl.BlockSpec((2, PAIR // DK, DK, DK), lambda i, c, s: (0, offset + i, 0, 0)))
+        specs.append(pl.BlockSpec((2, PAIR // DK, DK, DK), lambda i, c, *s: (0, offset + i, 0, 0)))
     else:
-        outs.append(pl.BlockSpec((3, total, PAIR), lambda i, c, s: (0, 0, base + i)))
+        outs.append(pl.BlockSpec((3, total, PAIR), lambda i, c, *s: (0, 0, base + i)))
         shapes.append(jax.ShapeDtypeStruct((3, total, room * PAIR), BF16))
-    start = 2 + len(operands)
+    start = 1 + len(src) + len(operands)
     shared = [] if into is None else list(into)
     return pl.pallas_call(
         functools.partial(kernel, len(got), int(into is not None), scale),
         grid_spec=pltpu.PrefetchScalarGridSpec(
-            num_scalar_prefetch=2,
+            num_scalar_prefetch=1 + len(src),
             grid=(pairs,),
             in_specs=specs + [ANY] * len(shared),
             out_specs=outs,
@@ -212,7 +220,7 @@
         input_output_aliases={start + j: j for j in range(len(shared))},
         cost_estimate=cost(14 * total * total * PAIR * pairs, 14 * total * PAIR * pairs),
         compiler_params=pltpu.CompilerParams(vmem_limit_bytes=VMEM_LIMIT),
-    )(cols, src, *operands, *shared)
+    )(cols[0], *src, *operands, *shared)
 
 
 def finish(parts, sums, pairs, room, scale, into):
@@ -289,8 +297,8 @@
     sizes += [n for n in (late - 2 * (late // 4), late // 4, late // 4) if n]
     firsts = [sum(sizes[:i]) for i in range(len(sizes))]
     shifts = range(1, peers)
-    cols = ((place + jnp.arange(peers)) % peers * pairs_here).astype(jnp.int32)
-    src = ((place - jnp.arange(peers)) % peers).astype(jnp.int32)
+    cols = [jnp.reshape((place + s) % peers * pairs_here, (1,)).astype(jnp.int32) for s in range(peers)]
+    src = [jnp.reshape((place - s) % peers, (1,)).astype(jnp.int32) for s in range(peers)]
 
     def move(values):
         return [

time: 164 us -> 158 us (0.963)
  Pallas kernels: 65.4 us -> 52.9 us
  waiting for transfers between devices: 63 us -> 71.2 us
    pallas_call x5, Pallas kernels: 34.1 us -> 25 us  [outputs(): pl.pallas_call(functools.partial(kernel, len(got), int(into is not None),...]
    ppermute x6, waiting for transfers between devices: 39.8 us -> 48 us  [move(): lax.ppermute(value, 'head', [(i, (i + s) % peers) for i in range(peers)])]
    pallas_call x4, Pallas kernels: 16.5 us -> 13.8 us  [states(): pl.pallas_call(functools.partial(state_kernel, len(got)), grid_spec=pltpu...]
  transfers between devices with their start and end apart: 10 -> 10, of which waited for: 5 -> 5; matrix products, arithmetic and copies ran while one was open for 2% -> 1% of each run, Pallas kernels for 34% -> 29%
where the time goes in v3:
time: 158 us; the launch traced here: 157 us
  waiting for transfers between devices  71.2 us (45%)
  Pallas kernels  52.9 us (33%)
  starting transfers between devices  30.1 us (19%)
  other arithmetic  2.31 us (1%)
    ppermute x6, waiting for transfers between devices, move(): lax.ppermute(value, 'head', [(i, (i + s) % peers) for i in range(peers)])  48 us
    pallas_call x5, Pallas kernels, outputs(): pl.pallas_call(functools.partial(kernel, len(got), int(into is not None),...  25 us
    pallas_call x4, Pallas kernels, states(): pl.pallas_call(functools.partial(state_kernel, len(got)), grid_spec=pltpu...  13.8 us
    all_to_all x2, starting transfers between devices, scan(): parts = lax.all_to_all(part, 'seq', 0, 0, tiled=True)  12.7 us
    all_to_all x2, waiting for transfers between devices, scan(): parts = lax.all_to_all(part, 'seq', 0, 0, tiled=True)  12.3 us
    all_to_all x2, waiting for transfers between devices, scan(): return lax.all_to_all(mine, 'seq', 0, 0, tiled=True).reshape(own.shape)  10.8 us
    ppermute x6, starting transfers between devices, move(): lax.ppermute(value, 'head', [(i, (i + s) % peers) for i in range(peers)])  8.69 us
    all_to_all x2, starting transfers between devices, scan(): return lax.all_to_all(mine, 'seq', 0, 0, tiled=True).reshape(own.shape)  8.68 us
  transfers between devices with their start and end apart: 10, of which 5 were waited for; matrix products, arithmetic and copies ran while one was open for 1% of the time, Pallas kernels for 29%

profile of v3, /device:TPU:0, one launch (start us, length us, event | category | flops | bytes accessed | tf_op | source)
XLA Modules:
  0.0 157.2 jit_solution(17353251636497214254)
XLA Ops:
  0.6 4.1 %states.5 = bf16[2,8,128,128]{3,2,1,0:T(8,128)(2,1)} custom-call(s32[1]{0:T(128)} %bitcast.3.refs_0_.col_ref, bf16[256,4096]{1,0:T(8,128)(2,1)} %refs_2_.11, bf16[256,4096]{1,0:T(8,128)(2,1)} %refs_3_.11, bf16[256,4096]{1,0:T(8,128)(2,1)} %refs_4_.11, bf16[256,4096]{1,0:T(8,128)(2,1)} %refs_5_.9), custom_call_target="tpu_custom_call" | custom-call | flops 134217728 | bytes 2097152 | tf_op jit(solution)/shard_map/states/pallas_call | solution.py:93
  4.7 3.0 %collective-permute-start.1 = (bf16[2,8,128,128]{3,2,1,0:T(8,128)(2,1)}, bf16[2,8,128,128]{3,2,1,0:T(8,128)(2,1)}, u32[]{:S(2)}, u32[]{:S(2)}) collective-permute-start(bf16[2,8,128,128]{3,2,1,0:T(8,128)(2,1)} %states.5), channel_id=1, source_target_pairs={{0,1},{1,0},{2,3},{3,2},{4,5},{5,4},{6,7},{7,6},{8,9},{9,8},{10,11... | collective-permute-start | bytes 1572872 | tf_op jit(solution)/shard_map/ppermute | solution.py:305
  7.7 4.0 %pack.1 = (bf16[4,256,512]{2,1,0:T(8,128)(2,1)}, bf16[4,256,512]{2,1,0:T(8,128)(2,1)}, bf16[4,256,512]{2,1,0:T(8,128)(2,1)}, bf16[4,256,256]{2,1,0:T(8,128)(2,1)}, bf16[4,256,256]{2,1,0:T(8,128)(2,1)}) custom-call(s32[1]{0:T(128)} %bitcast.3.refs_0_.col_ref, bf16[256,4096]{1,0:T(8,128)(2,1)} %refs_2_.11, bf16[256,4096]{1,0:T(8,128)(2,1)} %refs_3_.11, ...), custom_call_target="tpu_custom_call" | custom-call | bytes 8388608 | tf_op jit(solution)/shard_map/pack/pallas_call | solution.py:60
  11.7 0.1 collective-permute-start.2
  11.8 2.0 %collective-permute-start.3 = (bf16[4,256,512]{2,1,0:T(8,128)(2,1)}, bf16[4,256,512]{2,1,0:T(8,128)(2,1)}, u32[]{:S(2)}, u32[]{:S(2)}) collective-permute-start(bf16[4,256,512]{2,1,0:T(8,128)(2,1)} %get-tuple-element.27), channel_id=1, source_target_pairs={{0,1},{1,0},{2,3},{3,2},{4,5},{5,4},{6,7},{7,6},{8,9},{9,8},{10,11... | collective-permute-start | bytes 3145736 | tf_op jit(solution)/shard_map/ppermute | solution.py:305
  13.8 4.2 %states.4 = f32[2,8,128,128]{3,2,1,0:T(8,128)} custom-call(s32[1]{0:T(128)} %bitcast.col_ref, bf16[256,4096]{1,0:T(8,128)(2,1)} %refs_2_.11, bf16[256,4096]{1,0:T(8,128)(2,1)} %refs_3_.11, bf16[256,4096]{1,0:T(8,128)(2,1)} %refs_4_.11, bf16[256,4096]{1,0:T(8,128)(2,1)} %refs_5_.9), custom_call_target="tpu_custom_call" | custom-call | flops 134217728 | bytes 2097152 | tf_op jit(solution)/shard_map/states/pallas_call | solution.py:93
  18.0 2.8 %collective-permute-done.1 = bf16[2,8,128,128]{3,2,1,0:T(8,128)(2,1)} collective-permute-done((bf16[2,8,128,128]{3,2,1,0:T(8,128)(2,1)}, bf16[2,8,128,128]{3,2,1,0:T(8,128)(2,1)}, u32[]{:S(2)}, u32[]{:S(2)}) %collective-permute-start.1) | collective-permute-done | bytes 524320 | tf_op jit(solution)/shard_map/ppermute | solution.py:305
  20.8 2.3 %add_convert_fusion = bf16[2,8,128,128]{3,2,1,0:T(8,128)(2,1)} fusion(f32[2,8,128,128]{3,2,1,0:T(8,128)} %states.4, bf16[2,8,128,128]{3,2,1,0:T(8,128)(2,1)} %collective-permute-done.1), kind=kLoop, calls=%fused_computation | loop fusion | flops 786432 | bytes 2097152 | tf_op jit(solution)/shard_map/convert_element_type | solution.py:317
  23.1 6.5 %all-to-all-start = ((bf16[16,128,128]{2,1,0:T(8,128)(2,1)}), bf16[16,128,128]{2,1,0:T(8,128)(2,1)}, u32[]{:S(2)}, u32[]{:S(2)}) async-start(bf16[16,128,128]{2,1,0:T(8,128)(2,1)} %bitcast.5), calls=%async_computation | async-start | bytes 1048576 | tf_op jit(solution)/shard_map/all_to_all | solution.py:269
  29.6 35.2 %collective-permute-done.3.refs_6_.rest_0_ = bf16[4,256,512]{2,1,0:T(8,128)(2,1)} collective-permute-done((bf16[4,256,512]{2,1,0:T(8,128)(2,1)}, bf16[4,256,512]{2,1,0:T(8,128)(2,1)}, u32[]{:S(2)}, u32[]{:S(2)}) %collective-permute-start.3) | collective-permute-done | bytes 1048608 | tf_op jit(solution)/shard_map/ppermute | solution.py:305
  64.9 2.7 %states.6.rest_1_ = bf16[2,8,128,128]{3,2,1,0:T(8,128)(2,1)} custom-call(s32[1]{0:T(128)} %bitcast.col_ref, bf16[256,4096]{1,0:T(8,128)(2,1)} %refs_2_.11, bf16[256,4096]{1,0:T(8,128)(2,1)} %refs_3_.11, bf16[256,4096]{1,0:T(8,128)(2,1)} %refs_4_.11, bf16[256,4096]{1,0:T(8,128)(2,1)} %refs_5_.9, bf16[4,256,512]{2,1,0:T(8,128)(2,1)} %collective-permute-done.3.refs_6_.rest_0_), custom_call_target="tpu_custom_call" | custom-call | flops 134217728 | bytes 2097152 | tf_op jit(solution)/shard_map/states/pallas_call | solution.py:93
  67.6 2.8 %states.7 = bf16[2,8,128,128]{3,2,1,0:T(8,128)(2,1)} custom-call(s32[1]{0:T(128)} %bitcast.col_ref, bf16[256,4096]{1,0:T(8,128)(2,1)} %refs_2_.11, bf16[256,4096]{1,0:T(8,128)(2,1)} %refs_3_.11, bf16[256,4096]{1,0:T(8,128)(2,1)} %refs_4_.11, bf16[256,4096]{1,0:T(8,128)(2,1)} %refs_5_.9, ...), custom_call_target="tpu_custom_call", output_to_operand_aliasing={{}: (6, {})} | custom-call | flops 134217728 | bytes 2097152 | tf_op jit(solution)/shard_map/states/pallas_call | solution.py:93
  70.4 0.0 all-to-all-done.part_ref
  70.4 6.2 %all-to-all-start.2 = ((bf16[16,128,128]{2,1,0:T(8,128)(2,1)}), bf16[16,128,128]{2,1,0:T(8,128)(2,1)S(1)}, u32[]{:S(2)}, u32[]{:S(2)}) async-start(bf16[16,128,128]{2,1,0:T(8,128)(2,1)} %bitcast.9), calls=%async_computation.2 | async-start | bytes 1048576 | tf_op jit(solution)/shard_map/all_to_all | solution.py:269
  76.6 1.9 %running.2 = bf16[16,128,128]{2,1,0:T(8,128)(2,1)} custom-call(s32[1]{0:T(128)} %bitcast.4.up_ref, bf16[16,128,128]{2,1,0:T(8,128)(2,1)} %all-to-all-done.part_ref), custom_call_target="tpu_custom_call" | custom-call | flops 262144 | bytes 1048576 | tf_op jit(solution)/shard_map/running/pallas_call | solution.py:271
  78.6 12.3 %all-to-all-done.2.part_ref = bf16[16,128,128]{2,1,0:T(8,128)(2,1)S(1)} async-done(((bf16[16,128,128]{2,1,0:T(8,128)(2,1)}), bf16[16,128,128]{2,1,0:T(8,128)(2,1)S(1)}, u32[]{:S(2)}, u32[]{:S(2)}) %all-to-all-start.2) | async-done | bytes 524320 | tf_op jit(solution)/shard_map/all_to_all | solution.py:269
  90.9 4.2 %all-to-all-start.1 = ((bf16[16,128,128]{2,1,0:T(8,128)(2,1)}), bf16[16,128,128]{2,1,0:T(8,128)(2,1)}, u32[]{:S(2)}, u32[]{:S(2)}) async-start(bf16[16,128,128]{2,1,0:T(8,128)(2,1)} %running.2), calls=%async_computation.1 | async-start | bytes 1048576 | tf_op jit(solution)/shard_map/all_to_all | solution.py:279
  95.2 1.6 collective-permute-start.5
  96.7 1.9 %running.3 = bf16[16,128,128]{2,1,0:T(8,128)(2,1)} custom-call(s32[1]{0:T(128)} %bitcast.4.up_ref, bf16[16,128,128]{2,1,0:T(8,128)(2,1)} %copy-done), custom_call_target="tpu_custom_call" | custom-call | flops 262144 | bytes 1048576 | tf_op jit(solution)/shard_map/running/pallas_call | solution.py:271
  98.6 10.8 %all-to-all-done.1 = bf16[16,128,128]{2,1,0:T(8,128)(2,1)} async-done(((bf16[16,128,128]{2,1,0:T(8,128)(2,1)}), bf16[16,128,128]{2,1,0:T(8,128)(2,1)}, u32[]{:S(2)}, u32[]{:S(2)}) %all-to-all-start.1) | async-done | bytes 524320 | tf_op jit(solution)/shard_map/all_to_all | solution.py:279
  109.4 4.4 %all-to-all-start.3 = ((bf16[16,128,128]{2,1,0:T(8,128)(2,1)}), bf16[16,128,128]{2,1,0:T(8,128)(2,1)}, u32[]{:S(2)}, u32[]{:S(2)}) async-start(bf16[16,128,128]{2,1,0:T(8,128)(2,1)} %running.3), calls=%async_computation.3 | async-start | bytes 1048576 | tf_op jit(solution)/shard_map/all_to_all | solution.py:279
  113.9 1.6 collective-permute-start
  115.4 0.5 collective-permute-start.4
  116.0 5.8 %shard_map.67 = (f32[512,1024]{1,0:T(8,128)}, f32[512,1024]{1,0:T(8,128)}, f32[512,1024]{1,0:T(8,128)}, bf16[3,512,1024]{2,1,0:T(8,128)(2,1)}) custom-call(s32[1]{0:T(128)} %bitcast.col_ref, s32[1]{0:T(128)} %bitcast.1.refs_0_, s32[1]{0:T(128)} %bitcast.2.refs_1_, bf16[256,4096]{1,0:T(8,128)(2,1)} %refs_2_.11, bf16[256,4096]{1,0:T(8,128)(2,1)} %refs_3_.11, ...), custom_call_target="tpu_custom_call" | custom-call | flops 1879048192 | bytes 3670016 | tf_op jit(solution)/shard_map/pallas_call | solution.py:210
  121.8 5.8 %shard_map.68 = (f32[512,1024]{1,0:T(8,128)}, f32[512,1024]{1,0:T(8,128)}, f32[512,1024]{1,0:T(8,128)}, bf16[3,512,1024]{2,1,0:T(8,128)(2,1)}) custom-call(s32[1]{0:T(128)} %bitcast.col_ref, s32[1]{0:T(128)} %bitcast.1.refs_0_, s32[1]{0:T(128)} %bitcast.2.refs_1_, ...), custom_call_target="tpu_custom_call", output_to_operand_aliasing={{0}: (8, {}), {1}: (9, {}), {2}: (10, {}), {3}: (11, {})} | custom-call | flops 1879048192 | bytes 3670016 | tf_op jit(solution)/shard_map/pallas_call | solution.py:210
  127.7 0.0 collective-permute-done.5.refs_6_
  127.7 5.7 %shard_map.69 = (bf16[512,2048]{1,0:T(8,128)(2,1)}, bf16[512,2048]{1,0:T(8,128)(2,1)}, bf16[512,2048]{1,0:T(8,128)(2,1)}) custom-call(s32[1]{0:T(128)} %bitcast.col_ref, s32[1]{0:T(128)} %bitcast.1.refs_0_, s32[1]{0:T(128)} %bitcast.2.refs_1_, bf16[256,4096]{1,0:T(8,128)(2,1)} %refs_2_.11, bf16[256,4096]{1,0:T(8,128)(2,1)} %refs_3_.11, ...), custom_call_target="tpu_custom_call" | custom-call | flops 1879048192 | bytes 3670016 | tf_op jit(solution)/shard_map/pallas_call | solution.py:210
  133.4 10.0 %collective-permute-done.4.refs_6_ = bf16[4,256,256]{2,1,0:T(8,128)(2,1)} collective-permute-done((bf16[4,256,256]{2,1,0:T(8,128)(2,1)}, bf16[4,256,256]{2,1,0:T(8,128)(2,1)}, u32[]{:S(2)}, u32[]{:S(2)}) %collective-permute-start.4) | collective-permute-done | bytes 524320 | tf_op jit(solution)/shard_map/ppermute | solution.py:305
  143.3 3.8 %shard_map.70 = (bf16[512,2048]{1,0:T(8,128)(2,1)}, bf16[512,2048]{1,0:T(8,128)(2,1)}, bf16[512,2048]{1,0:T(8,128)(2,1)}) custom-call(s32[1]{0:T(128)} %bitcast.col_ref, s32[1]{0:T(128)} %bitcast.1.refs_0_, s32[1]{0:T(128)} %bitcast.2.refs_1_, bf16[256,4096]{1,0:T(8,128)(2,1)} %refs_2_.11, ...), custom_call_target="tpu_custom_call", output_to_operand_aliasing={{0}: (9, {}), {1}: (10, {}), {2}: (11, {})} | custom-call | flops 939524096 | bytes 1835008 | tf_op jit(solution)/shard_map/pallas_call | solution.py:210
  147.1 0.0 all-to-all-done.3
  147.1 6.3 %across.1 = (bf16[512,2048]{1,0:T(8,128)(2,1)}, bf16[512,2048]{1,0:T(8,128)(2,1)}, bf16[512,2048]{1,0:T(8,128)(2,1)}) custom-call(bf16[3,512,1024]{2,1,0:T(8,128)(2,1)} %get-tuple-element.32.rows_ref, bf16[2,8,128,128]{3,2,1,0:T(8,128)(2,1)} %bitcast.8.sum_ref, ...), custom_call_target="tpu_custom_call", output_to_operand_aliasing={{0}: (5, {}), {1}: (6, {}), {2}: (7, {})} | custom-call | flops 402653184 | bytes 12582912 | tf_op jit(solution)/shard_map/across/pallas_call | solution.py:230
  153.4 3.8 %shard_map.71 = (bf16[512,2048]{1,0:T(8,128)(2,1)}, bf16[512,2048]{1,0:T(8,128)(2,1)}, bf16[512,2048]{1,0:T(8,128)(2,1)}) custom-call(s32[1]{0:T(128)} %bitcast.col_ref, s32[1]{0:T(128)} %bitcast.1.refs_0_, s32[1]{0:T(128)} %bitcast.2.refs_1_, bf16[256,4096]{1,0:T(8,128)(2,1)} %refs_2_.11, ...), custom_call_target="tpu_custom_call", output_to_operand_aliasing={{0}: (9, {}), {1}: (10, {}), {2}: (11, {})} | custom-call | flops 939524096 | bytes 1835008 | tf_op jit(solution)/shard_map/pallas_call | solution.py:210
  (4 shorter events, 0.0 us)
Async XLA Ops:
  4.7 16.1 %collective-permute-start.1 = (bf16[2,8,128,128]{3,2,1,0:T(8,128)(2,1)}, bf16[2,8,128,128]{3,2,1,0:T(8,128)(2,1)}, u32[]{:S(2)}, u32[]{:S(2)}) collective-permute-start(bf16[2,8,128,128]{3,2,1,0:T(8,128)(2,1)} %states.5), channel_id=1, source_target_pairs={{0,1},{1,0},{2,3},{3,2},{4,5},{5,4},{6,7},{7,6},{8,9},{9,8},{10,11... | collective-permute-start | bytes 1572872 | tf_op jit(solution)/shard_map/ppermute | solution.py:305
  11.7 55.9 %collective-permute-start.2 = (bf16[4,256,512]{2,1,0:T(8,128)(2,1)}, bf16[4,256,512]{2,1,0:T(8,128)(2,1)}, u32[]{:S(2)}, u32[]{:S(2)}) collective-permute-start(bf16[4,256,512]{2,1,0:T(8,128)(2,1)} %get-tuple-element.26), channel_id=1, source_target_pairs={{0,1},{1,0},{2,3},{3,2},{4,5},{5,4},{6,7},{7,6},{8,9},{9,8},{10,11... | collective-permute-start | bytes 3145736 | tf_op jit(solution)/shard_map/ppermute | solution.py:305
  11.8 53.1 %collective-permute-start.3 = (bf16[4,256,512]{2,1,0:T(8,128)(2,1)}, bf16[4,256,512]{2,1,0:T(8,128)(2,1)}, u32[]{:S(2)}, u32[]{:S(2)}) collective-permute-start(bf16[4,256,512]{2,1,0:T(8,128)(2,1)} %get-tuple-element.27), channel_id=1, source_target_pairs={{0,1},{1,0},{2,3},{3,2},{4,5},{5,4},{6,7},{7,6},{8,9},{9,8},{10,11... | collective-permute-start | bytes 3145736 | tf_op jit(solution)/shard_map/ppermute | solution.py:305
  23.1 47.3 %all-to-all-start = ((bf16[16,128,128]{2,1,0:T(8,128)(2,1)}), bf16[16,128,128]{2,1,0:T(8,128)(2,1)}, u32[]{:S(2)}, u32[]{:S(2)}) async-start(bf16[16,128,128]{2,1,0:T(8,128)(2,1)} %bitcast.5), calls=%async_computation | async-start | bytes 1048576 | tf_op jit(solution)/shard_map/all_to_all | solution.py:269
  70.4 20.5 %all-to-all-start.2 = ((bf16[16,128,128]{2,1,0:T(8,128)(2,1)}), bf16[16,128,128]{2,1,0:T(8,128)(2,1)S(1)}, u32[]{:S(2)}, u32[]{:S(2)}) async-start(bf16[16,128,128]{2,1,0:T(8,128)(2,1)} %bitcast.9), calls=%async_computation.2 | async-start | bytes 1048576 | tf_op jit(solution)/shard_map/all_to_all | solution.py:269
  90.9 5.8 %copy-start = (bf16[16,128,128]{2,1,0:T(8,128)(2,1)}, bf16[16,128,128]{2,1,0:T(8,128)(2,1)S(1)}, u32[]{:S(2)}) copy-start(bf16[16,128,128]{2,1,0:T(8,128)(2,1)S(1)} %all-to-all-done.2.part_ref) | copy-start | bytes 1572868
  90.9 18.5 %all-to-all-start.1 = ((bf16[16,128,128]{2,1,0:T(8,128)(2,1)}), bf16[16,128,128]{2,1,0:T(8,128)(2,1)}, u32[]{:S(2)}, u32[]{:S(2)}) async-start(bf16[16,128,128]{2,1,0:T(8,128)(2,1)} %running.2), calls=%async_computation.1 | async-start | bytes 1048576 | tf_op jit(solution)/shard_map/all_to_all | solution.py:279
  95.2 32.5 %collective-permute-start.5 = (bf16[4,256,512]{2,1,0:T(8,128)(2,1)}, bf16[4,256,512]{2,1,0:T(8,128)(2,1)}, u32[]{:S(2)}, u32[]{:S(2)}) collective-permute-start(bf16[4,256,512]{2,1,0:T(8,128)(2,1)} %get-tuple-element.37), channel_id=1, source_target_pairs={{0,1},{1,0},{2,3},{3,2},{4,5},{5,4},{6,7},{7,6},{8,9},{9,8},{10,11... | collective-permute-start | bytes 3145736 | tf_op jit(solution)/shard_map/ppermute | solution.py:305
  109.4 37.7 %all-to-all-start.3 = ((bf16[16,128,128]{2,1,0:T(8,128)(2,1)}), bf16[16,128,128]{2,1,0:T(8,128)(2,1)}, u32[]{:S(2)}, u32[]{:S(2)}) async-start(bf16[16,128,128]{2,1,0:T(8,128)(2,1)} %running.3), calls=%async_computation.3 | async-start | bytes 1048576 | tf_op jit(solution)/shard_map/all_to_all | solution.py:279
  113.9 39.5 %collective-permute-start = (bf16[4,256,256]{2,1,0:T(8,128)(2,1)}, bf16[4,256,256]{2,1,0:T(8,128)(2,1)}, u32[]{:S(2)}, u32[]{:S(2)}) collective-permute-start(bf16[4,256,256]{2,1,0:T(8,128)(2,1)} %get-tuple-element.25), channel_id=1, source_target_pairs={{0,1},{1,0},{2,3},{3,2},{4,5},{5,4},{6,7},{7,6},{8,9},{9,8},{10,11... | collective-permute-start | bytes 1572872 | tf_op jit(solution)/shard_map/ppermute | solution.py:305
  115.4 27.9 %collective-permute-start.4 = (bf16[4,256,256]{2,1,0:T(8,128)(2,1)}, bf16[4,256,256]{2,1,0:T(8,128)(2,1)}, u32[]{:S(2)}, u32[]{:S(2)}) collective-permute-start(bf16[4,256,256]{2,1,0:T(8,128)(2,1)} %get-tuple-element.36), channel_id=1, source_target_pairs={{0,1},{1,0},{2,3},{3,2},{4,5},{5,4},{6,7},{7,6},{8,9},{9,8},{10,11... | collective-permute-start | bytes 1572872 | tf_op jit(solution)/shard_map/ppermute | solution.py:305

commit v4 on v3

--- a/solution.py
+++ b/solution.py
@@ -106,6 +106,43 @@
     )(cols[at], *arrays, *got, *shared)
 
 
+def split_kernel(peers, col_ref, core_ref, q_ref, k_ref, v_ref, g_ref, *rest):
+    keep_ref, give_ref = rest[-2:]
+    first = core_ref[0] == 0
+    for j in range(PAIR // DK):
+        at = slice(j * DK, (j + 1) * DK)
+        kv = mm(k_ref[:, at], v_ref[:, at], TN)
+        qg = mm(q_ref[:, at], g_ref[:, at], TN)
+        for r in rest[:peers]:
+            kv = kv + mm(r[1, :, at], r[2, :, at], TN)
+            qg = qg + mm(r[0, :, at], r[3, :, at], TN)
+        keep_ref[j] = jnp.where(first, kv, qg)
+        give_ref[j] = jnp.where(first, qg, kv)
+
+
+def split_states(cols, core, arrays, got, first, pairs, base, room, into):
+    rows = arrays[0].shape[0]
+    own = pl.BlockSpec((rows, PAIR), lambda i, c, d: (0, c[0] + first + i))
+    there = pl.BlockSpec((4, rows, PAIR), lambda i, c, d: (0, 0, i))
+    tokens = rows * (1 + len(got))
+    per = PAIR // DK
+    shared = [] if into is None else list(into)
+    return pl.pallas_call(
+        functools.partial(split_kernel, len(got)),
+        grid_spec=pltpu.PrefetchScalarGridSpec(
+            num_scalar_prefetch=2,
+            grid=(pairs,),
+            in_specs=[own] * 4 + [there] * len(got) + [pl.BlockSpec(memory_space=pl.ANY)] * len(shared),
+            out_specs=[pl.BlockSpec((per, DK, DK), lambda i, c, d: (base + i, 0, 0))] * 2,
+        ),
+        out_shape=[jax.ShapeDtypeStruct((per * room, DK, DK), F32)] * 2,
+        input_output_aliases={6 + len(got) + j: j for j in range(len(shared))},
+        cost_estimate=cost(4 * tokens * DK * PAIR * pairs, 8 * tokens * pairs * PAIR),
+        compiler_params=pltpu.CompilerParams(vmem_limit_bytes=VMEM_LIMIT),
+        name="split_states",
+    )(cols[0], core, *arrays, *got, *shared)
+
+
 def gather_rows(src, owns, got, which, all_ref):
     rows = owns[0].shape[0]
     mine = pl.multiple_of(src[0][0] * rows, rows)
@@ -145,27 +182,26 @@
         yield grad, down, second[down]
 
 
-def across(all_ref, sum_ref, j, grad, rows, at):
-    if grad == 0:
-        return mm(all_ref[3, rows, at], sum_ref[0, j], NT)
-    if grad == 1:
-        return mm(all_ref[2, rows, at], sum_ref[1, j], NT)
-    return mm(all_ref[1, rows, at], sum_ref[1, j], NN)
-
-
-def whole_kernel(peers, aliased, scale, col_ref, *refs):
+def prefix_suffix(core_ref, mine_ref, other_ref, j):
+    first, mine, other = core_ref[0] == 0, mine_ref[j], other_ref[j]
+    return jnp.where(first, mine, other), jnp.where(first, other, mine)
+
+
+def whole_kernel(peers, aliased, scale, col_ref, core_ref, *refs):
     src, refs = refs[: peers + 1], refs[peers + 1 :]
-    owns, got, sum_ref = refs[:4], refs[4 : 4 + peers], refs[4 + peers]
-    outs, all_ref = refs[5 + peers + 3 * aliased : -1], refs[-1]
+    owns, got, sums = refs[:4], refs[4 : 4 + peers], refs[4 + peers : 6 + peers]
+    outs, all_ref = refs[6 + peers + 3 * aliased : -1], refs[-1]
     gather_rows(src, owns, got, range(4), all_ref)
     for j in range(PAIR // DK):
         at = slice(j * DK, (j + 1) * DK)
+        prefix, suffix = prefix_suffix(core_ref, *sums, j)
         for grad, rows, value in within(all_ref, at):
-            value = value + across(all_ref, sum_ref, j, grad, rows, at)
+            which, state, dims = ((3, prefix, NT), (2, suffix, NT), (1, suffix, NN))[grad]
+            value = value + mm(all_ref[which, rows, at], state, dims)
             outs[grad][rows, at] = (scale * value).astype(BF16)
 
 
-def within_kernel(peers, aliased, scale, col_ref, *refs):
+def within_kernel(peers, aliased, scale, col_ref, core_ref, *refs):
     src, refs = refs[: peers + 1], refs[peers + 1 :]
     owns, got = refs[:4], refs[4 : 4 + peers]
     outs, rows_ref, all_ref = refs[4 + peers + 4 * aliased : -2], refs[-2], refs[-1]
@@ -177,19 +213,20 @@
             outs[grad][rows, at] = value
 
 
-def across_kernel(aliased, scale, rows_ref, sum_ref, *refs):
+def across_kernel(aliased, scale, core_ref, rows_ref, mine_ref, other_ref, *refs):
     parts, outs = refs[:3], refs[3 + 3 * aliased :]
     for j in range(PAIR // DK):
         at = slice(j * DK, (j + 1) * DK)
-        for grad, (which, state, dims) in enumerate(((2, 0, NT), (1, 1, NT), (0, 1, NN))):
-            value = parts[grad][:, at] + mm(rows_ref[which, :, at], sum_ref[state, j], dims)
+        prefix, suffix = prefix_suffix(core_ref, mine_ref, other_ref, j)
+        for grad, (which, state, dims) in enumerate(((2, prefix, NT), (1, suffix, NT), (0, suffix, NN))):
+            value = parts[grad][:, at] + mm(rows_ref[which, :, at], state, dims)
             outs[grad][:, at] = (scale * value).astype(BF16)
 
 
 ANY = pl.BlockSpec(memory_space=pl.ANY)
 
 
-def outputs(kernel, cols, src, arrays, got, sums, first, pairs, base, room, scale, into):
+def outputs(kernel, cols, core, src, arrays, got, sums, first, pairs, base, room, scale, into):
     rows = arrays[0].shape[0]
     total = rows * (1 + len(got))
     whole = kernel is whole_kernel
@@ -200,17 +237,17 @@
     outs, shapes = [here] * 3, [jax.ShapeDtypeStruct((total, room * PAIR), BF16 if whole else F32)] * 3
     if whole:
         sums, offset = sums
-        operands.append(sums)
-        specs.append(pl.BlockSpec((2, PAIR // DK, DK, DK), lambda i, c, *s: (0, offset + i, 0, 0)))
+        operands += sums
+        specs += [pl.BlockSpec((PAIR // DK, DK, DK), lambda i, c, *s: (offset + i, 0, 0))] * 2
     else:
         outs.append(pl.BlockSpec((3, total, PAIR), lambda i, c, *s: (0, 0, base + i)))
         shapes.append(jax.ShapeDtypeStruct((3, total, room * PAIR), BF16))
-    start = 1 + len(src) + len(operands)
+    start = 2 + len(src) + len(operands)
     shared = [] if into is None else list(into)
     return pl.pallas_call(
         functools.partial(kernel, len(got), int(into is not None), scale),
         grid_spec=pltpu.PrefetchScalarGridSpec(
-            num_scalar_prefetch=1 + len(src),
+            num_scalar_prefetch=2 + len(src),
             grid=(pairs,),
             in_specs=specs + [ANY] * len(shared),
             out_specs=outs,
@@ -220,29 +257,32 @@
         input_output_aliases={start + j: j for j in range(len(shared))},
         cost_estimate=cost(14 * total * total * PAIR * pairs, 14 * total * PAIR * pairs),
         compiler_params=pltpu.CompilerParams(vmem_limit_bytes=VMEM_LIMIT),
-    )(cols[0], *src, *operands, *shared)
-
-
-def finish(parts, sums, pairs, room, scale, into):
+    )(cols[0], core, *src, *operands, *shared)
+
+
+def finish(parts, core, sums, pairs, room, scale, into):
     total = parts[0].shape[0]
-    here = pl.BlockSpec((total, PAIR), lambda i: (0, i))
+    here = pl.BlockSpec((total, PAIR), lambda i, d: (0, i))
     shared = [] if into is None else list(into)
     return pl.pallas_call(
         functools.partial(across_kernel, int(into is not None), scale),
-        grid=(pairs,),
-        in_specs=[
-            pl.BlockSpec((3, total, PAIR), lambda i: (0, 0, i)),
-            pl.BlockSpec((2, PAIR // DK, DK, DK), lambda i: (0, i, 0, 0)),
-            *[here] * 3,
-            *[ANY] * len(shared),
-        ],
-        out_specs=[here] * 3,
+        grid_spec=pltpu.PrefetchScalarGridSpec(
+            num_scalar_prefetch=1,
+            grid=(pairs,),
+            in_specs=[
+                pl.BlockSpec((3, total, PAIR), lambda i, d: (0, 0, i)),
+                *[pl.BlockSpec((PAIR // DK, DK, DK), lambda i, d: (i, 0, 0))] * 2,
+                *[here] * 3,
+                *[ANY] * len(shared),
+            ],
+            out_specs=[here] * 3,
+        ),
         out_shape=[jax.ShapeDtypeStruct((total, room * PAIR), BF16)] * 3,
-        input_output_aliases={5 + j: j for j in range(len(shared))},
+        input_output_aliases={7 + j: j for j in range(len(shared))},
         cost_estimate=cost(6 * total * DK * PAIR * pairs, 24 * total * PAIR * pairs),
         compiler_params=pltpu.CompilerParams(vmem_limit_bytes=VMEM_LIMIT),
         name="across",
-    )(parts[3], sums, *parts[:3], *shared)
+    )(core, parts[3], *sums, *parts[:3], *shared)
 
 
 def running_kernel(up_ref, part_ref, out_ref):
@@ -263,11 +303,9 @@
         run(reversed(range(count)))
 
 
-def scan(own):
-    count = lax.axis_size("seq")
-    part = own.reshape(count, -1, DK)
-    parts = lax.all_to_all(part, "seq", 0, 0, tiled=True)
-    up = (lax.axis_index("seq") < count // 2).astype(jnp.int32).reshape(1)
+def deal_and_sum(own, up, groups):
+    count = len(groups[0])
+    parts = lax.all_to_all(own.reshape(count, -1, DK), "seq", 0, 0, tiled=True, axis_index_groups=groups)
     mine = pl.pallas_call(
         running_kernel,
         in_specs=[pl.BlockSpec(memory_space=pltpu.SMEM), pl.BlockSpec(memory_space=pltpu.VMEM)],
@@ -275,8 +313,18 @@
         out_shape=jax.ShapeDtypeStruct(parts.shape, BF16),
         cost_estimate=cost(parts.size, 4 * parts.size),
         name="running",
-    )(up, parts)
-    return lax.all_to_all(mine, "seq", 0, 0, tiled=True).reshape(own.shape)
+    )(up.astype(jnp.int32).reshape(1), parts)
+    mine = lax.all_to_all(mine, "seq", 0, 0, tiled=True, axis_index_groups=groups)
+    return mine.reshape(own.shape)
+
+
+def scan_chips(keep, give):
+    count = lax.axis_size("seq")
+    swap = [(i, i ^ 1) for i in range(count)]
+    chip = keep + lax.ppermute(give, "seq", swap)
+    groups = [list(range(core, count, 2)) for core in (0, 1)]
+    mine = deal_and_sum(chip.astype(BF16), lax.axis_index("seq") % 2 == 0, groups)
+    return mine, lax.ppermute((mine.astype(F32) + keep).astype(BF16), "seq", swap)
 
 
 def local(queries, key_vectors, value_vectors, out_grads):
@@ -292,7 +340,7 @@
     scale = 1.0 / math.sqrt(DK * total_tokens)
     late = pairs_here // 2
     early = pairs_here - late
-    sizes = [early - early // 2, early // 2]
+    sizes = [n for n in (1, (early - 1) // 2, early - 1 - (early - 1) // 2) if n]
     split = len(sizes)
     sizes += [n for n in (late - 2 * (late // 4), late // 4, late // 4) if n]
     firsts = [sum(sizes[:i]) for i in range(len(sizes))]
@@ -306,33 +354,33 @@
             for s, value in zip(shifts, values)
         ]
 
+    got = [move(pack(cols, peers, arrays, 0, sizes[:1])[0])]
     late_sent = [states(cols, arrays, [], early, late, BF16, s) for s in shifts]
     late_got = move(late_sent)
-    got = []
-    for packed in pack(cols, peers, arrays, 0, sizes):
+    for c, packed in enumerate(pack(cols, peers, arrays, sizes[0], sizes[1:]), 1):
         got.append(move(packed))
-    late_sums = states(cols, arrays, [], early, late, F32)
+    core = (lax.axis_index("seq") % 2).astype(jnp.int32).reshape(1)
+    keep, give = split_states(cols, core, arrays, [], early, late, 0, late, None)
     for piece in late_got:
-        late_sums = late_sums + piece.astype(F32)
-    late_sums = scan(late_sums.astype(BF16))
-    early_sums = parts = None
+        first, second = jnp.where(core[0] == 0, piece[0], piece[1]), jnp.where(core[0] == 0, piece[1], piece[0])
+        keep, give = keep + first.astype(F32), give + second.astype(F32)
+    late_sums = scan_chips(keep, give)
+    own = parts = None
     for c in range(split):
-        early_sums = states(
-            cols, arrays, got[c], firsts[c], sizes[c], room=early, base=firsts[c], into=early_sums
-        )
+        own = split_states(cols, core, arrays, got[c], firsts[c], sizes[c], firsts[c], early, own)
     for c in range(split):
         parts = outputs(
-            within_kernel, cols, src, arrays, got[c], None, firsts[c], sizes[c], firsts[c], early, scale, parts
+            within_kernel, cols, core, src, arrays, got[c], None, firsts[c], sizes[c], firsts[c], early, scale, parts
         )
-    early_sums = scan(early_sums)
+    early_sums = scan_chips(*own)
 
     outs = None
     for c in range(split, len(sizes)):
         if c == len(sizes) - 1:
-            outs = finish(parts, early_sums, early, pairs_here, scale, outs)
+            outs = finish(parts, core, early_sums, early, pairs_here, scale, outs)
         sums = (late_sums, firsts[c] - early)
         outs = outputs(
-            whole_kernel, cols, src, arrays, got[c], sums, firsts[c], sizes[c], firsts[c], pairs_here, scale, outs
+            whole_kernel, cols, core, src, arrays, got[c], sums, firsts[c], sizes[c], firsts[c], pairs_here, scale, outs
         )
     return tuple(outs)
 

time: 158 us -> 169 us (1.070)
  other arithmetic: 2.31 us -> 8.97 us
  Pallas kernels: 52.9 us -> 58.5 us
    pallas_call x2 -> x6, Pallas kernels: 3.85 us -> 15.1 us  [the longest x4 11.7 us: split_states(): pl.pallas_call(functools.partial(split_kernel, len(got)), grid_spec=pltpu...]
    pallas_call x4 -> x1, Pallas kernels: 13.8 us -> 4.06 us  [states(): pl.pallas_call(functools.partial(state_kernel, len(got)), grid_spec=pltpu...]
    all_to_all x4, waiting for transfers between devices: 23.1 us -> 15.8 us  [the longest x2 15.8 us: deal_and_sum(): lax.all_to_all(own.reshape(count, -1, DK), 'seq', 0, 0, tiled=True, axis_...]
    ppermute x6 -> x7, waiting for transfers between devices: 48 us -> 54.3 us  [move(): lax.ppermute(value, 'head', [(i, (i + s) % peers) for i in range(peers)])]
    convert_element_type x1 -> x4, other arithmetic: 2.31 us -> 6.93 us  [the longest x2 3.97 us: scan_chips(): (mine.astype(F32) + keep).astype(BF16)]
    pallas_call x5 -> x6, Pallas kernels: 25 us -> 27.5 us  [outputs(): pl.pallas_call(functools.partial(kernel, len(got), int(into is not None),...]
    add x0 -> x1, other arithmetic: none -> 2.05 us  [grads(): keep, give = (keep + first.astype(F32), give + second.astype(F32))]
    pallas_call x1 -> x2, Pallas kernels: 3.99 us -> 5.59 us  [pack(): pl.pallas_call(functools.partial(pack_kernel, sizes, first, peers), in_sp...]
  transfers between devices with their start and end apart: 10 -> 15, of which waited for: 5 -> 5; matrix products, arithmetic and copies ran while one was open for 1% -> 5% of each run, Pallas kernels for 29% -> 30%
where the time goes in v4:
time: 169 us; the launch traced here: 168 us
  waiting for transfers between devices  70.1 us (41%)
  Pallas kernels  58.5 us (35%)
  starting transfers between devices  29.3 us (17%)
  other arithmetic  8.97 us (5%)
    ppermute x7, waiting for transfers between devices, move(): lax.ppermute(value, 'head', [(i, (i + s) % peers) for i in range(peers)])  54.3 us
    pallas_call x6, Pallas kernels, outputs(): pl.pallas_call(functools.partial(kernel, len(got), int(into is not None),...  27.5 us
    all_to_all x2, waiting for transfers between devices, deal_and_sum(): lax.all_to_all(own.reshape(count, -1, DK), 'seq', 0, 0, tiled=True, axis_...  15.8 us
    pallas_call x4, Pallas kernels, split_states(): pl.pallas_call(functools.partial(split_kernel, len(got)), grid_spec=pltpu...  11.7 us
    all_to_all x2, starting transfers between devices, deal_and_sum(): lax.all_to_all(own.reshape(count, -1, DK), 'seq', 0, 0, tiled=True, axis_...  10.1 us
    all_to_all x2, starting transfers between devices, deal_and_sum(): lax.all_to_all(mine, 'seq', 0, 0, tiled=True, axis_index_groups=groups)  9.88 us
    ppermute x7, starting transfers between devices, move(): lax.ppermute(value, 'head', [(i, (i + s) % peers) for i in range(peers)])  8.78 us
    pallas_call x1, Pallas kernels, finish(): pl.pallas_call(functools.partial(across_kernel, int(into is not None), sc...  6.3 us
  transfers between devices with their start and end apart: 15, of which 5 were waited for; matrix products, arithmetic and copies ran while one was open for 5% of the time, Pallas kernels for 30%

profile of v4, /device:TPU:0, one launch (start us, length us, event | category | flops | bytes accessed | tf_op | source)
XLA Modules:
  0.0 167.7 jit_solution(10529762463517562617)
XLA Ops:
  0.6 4.1 %states.1 = bf16[2,8,128,128]{3,2,1,0:T(8,128)(2,1)} custom-call(s32[1]{0:T(128)} %bitcast.4.refs_0_.col_ref, bf16[256,4096]{1,0:T(8,128)(2,1)} %refs_2_.15, bf16[256,4096]{1,0:T(8,128)(2,1)} %refs_3_.15, bf16[256,4096]{1,0:T(8,128)(2,1)} %refs_4_.15, bf16[256,4096]{1,0:T(8,128)(2,1)} %refs_5_.11), custom_call_target="tpu_custom_call" | custom-call | flops 134217728 | bytes 2097152 | tf_op jit(solution)/shard_map/states/pallas_call | solution.py:93
  4.7 3.0 %collective-permute-start.1 = (bf16[2,8,128,128]{3,2,1,0:T(8,128)(2,1)}, bf16[2,8,128,128]{3,2,1,0:T(8,128)(2,1)}, u32[]{:S(2)}, u32[]{:S(2)}) collective-permute-start(bf16[2,8,128,128]{3,2,1,0:T(8,128)(2,1)} %states.1), channel_id=1, source_target_pairs={{0,1},{1,0},{2,3},{3,2},{4,5},{5,4},{6,7},{7,6},{8,9},{9,8},{10,11... | collective-permute-start | bytes 1572872 | tf_op jit(solution)/shard_map/ppermute | solution.py:353
  7.7 3.8 %pack.2 = (bf16[4,256,256]{2,1,0:T(8,128)(2,1)}, bf16[4,256,512]{2,1,0:T(8,128)(2,1)}, bf16[4,256,512]{2,1,0:T(8,128)(2,1)}, bf16[4,256,256]{2,1,0:T(8,128)(2,1)}, bf16[4,256,256]{2,1,0:T(8,128)(2,1)}) custom-call(s32[1]{0:T(128)} %bitcast.4.refs_0_.col_ref, bf16[256,4096]{1,0:T(8,128)(2,1)} %refs_2_.15, bf16[256,4096]{1,0:T(8,128)(2,1)} %refs_3_.15, ...), custom_call_target="tpu_custom_call" | custom-call | bytes 7340032 | tf_op jit(solution)/shard_map/pack/pallas_call | solution.py:60
  11.5 2.0 %collective-permute-start.5 = (bf16[4,256,256]{2,1,0:T(8,128)(2,1)}, bf16[4,256,256]{2,1,0:T(8,128)(2,1)}, u32[]{:S(2)}, u32[]{:S(2)}) collective-permute-start(bf16[4,256,256]{2,1,0:T(8,128)(2,1)} %get-tuple-element.41), channel_id=1, source_target_pairs={{0,1},{1,0},{2,3},{3,2},{4,5},{5,4},{6,7},{7,6},{8,9},{9,8},{10,11... | collective-permute-start | bytes 1572872 | tf_op jit(solution)/shard_map/ppermute | solution.py:353
  13.6 1.8 %pack.3 = bf16[4,256,256]{2,1,0:T(8,128)(2,1)} custom-call(s32[1]{0:T(128)} %bitcast.4.refs_0_.col_ref, bf16[256,4096]{1,0:T(8,128)(2,1)} %refs_2_.15, bf16[256,4096]{1,0:T(8,128)(2,1)} %refs_3_.15, bf16[256,4096]{1,0:T(8,128)(2,1)} %refs_4_.15, bf16[256,4096]{1,0:T(8,128)(2,1)} %refs_5_.11), custom_call_target="tpu_custom_call" | custom-call | bytes 1048576 | tf_op jit(solution)/shard_map/pack/pallas_call | solution.py:60
  15.5 4.1 %split_states.4 = (f32[8,128,128]{2,1,0:T(8,128)}, f32[8,128,128]{2,1,0:T(8,128)}) custom-call(s32[1]{0:T(128)} %bitcast.col_ref, s32[1]{0:T(128)} %bitcast.1.core_ref, bf16[256,4096]{1,0:T(8,128)(2,1)} %refs_2_.15, bf16[256,4096]{1,0:T(8,128)(2,1)} %refs_3_.15, bf16[256,4096]{1,0:T(8,128)(2,1)} %refs_4_.15, bf16[256,4096]{1,0:T(8,128)(2,1)} %refs_5_.11), custom_call_target="tpu_custom_call" | custom-call | flops 134217728 | bytes 2097152 | tf_op jit(solution)/shard_map/split_states/pallas_call | solution.py:130
  20.8 2.0 %convert_add_fusion = f32[8,128,128]{2,1,0:T(8,128)} fusion(f32[8,128,128]{2,1,0:T(8,128)} %get-tuple-element.39, pred[]{:T(512)S(6)} %eq.14, bf16[2,8,128,128]{3,2,1,0:T(8,128)(2,1)} %collective-permute-done.1), kind=kLoop, calls=%fused_computation | loop fusion | flops 393216 | bytes 1572865 | tf_op jit(solution)/shard_map/add | solution.py:366
  22.8 42.0 %collective-permute-done.6.refs_6_.rest_0_ = bf16[4,256,256]{2,1,0:T(8,128)(2,1)} collective-permute-done((bf16[4,256,256]{2,1,0:T(8,128)(2,1)}, bf16[4,256,256]{2,1,0:T(8,128)(2,1)}, u32[]{:S(2)}, u32[]{:S(2)}) %collective-permute-start.6) | collective-permute-done | bytes 524320 | tf_op jit(solution)/shard_map/ppermute | solution.py:353
  64.8 2.4 %split_states.5 = (f32[8,128,128]{2,1,0:T(8,128)}, f32[8,128,128]{2,1,0:T(8,128)}) custom-call(s32[1]{0:T(128)} %bitcast.col_ref, s32[1]{0:T(128)} %bitcast.1.core_ref, bf16[256,4096]{1,0:T(8,128)(2,1)} %refs_2_.15, bf16[256,4096]{1,0:T(8,128)(2,1)} %refs_3_.15, bf16[256,4096]{1,0:T(8,128)(2,1)} %refs_4_.15, bf16[256,4096]{1,0:T(8,128)(2,1)} %refs_5_.11, ...), custom_call_target="tpu_custom_call" | custom-call | flops 67108864 | bytes 1048576 | tf_op jit(solution)/shard_map/split_states/pallas_call | solution.py:130
  67.2 2.4 %split_states.6 = (f32[8,128,128]{2,1,0:T(8,128)}, f32[8,128,128]{2,1,0:T(8,128)}) custom-call(s32[1]{0:T(128)} %bitcast.col_ref, s32[1]{0:T(128)} %bitcast.1.core_ref, bf16[256,4096]{1,0:T(8,128)(2,1)} %refs_2_.15, bf16[256,4096]{1,0:T(8,128)(2,1)} %refs_3_.15, bf16[256,4096]{1,0:T(8,128)(2,1)} %refs_4_.15, ...), custom_call_target="tpu_custom_call", output_to_operand_aliasing={{0}: (7, {}), {1}: (8, {})} | custom-call | flops 67108864 | bytes 1048576 | tf_op jit(solution)/shard_map/split_states/pallas_call | solution.py:130
  69.6 2.8 %split_states.7 = (f32[8,128,128]{2,1,0:T(8,128)}, f32[8,128,128]{2,1,0:T(8,128)}) custom-call(s32[1]{0:T(128)} %bitcast.col_ref, s32[1]{0:T(128)} %bitcast.1.core_ref, bf16[256,4096]{1,0:T(8,128)(2,1)} %refs_2_.15, bf16[256,4096]{1,0:T(8,128)(2,1)} %refs_3_.15, bf16[256,4096]{1,0:T(8,128)(2,1)} %refs_4_.15, ...), custom_call_target="tpu_custom_call", output_to_operand_aliasing={{0}: (7, {}), {1}: (8, {})} | custom-call | flops 134217728 | bytes 2097152 | tf_op jit(solution)/shard_map/split_states/pallas_call | solution.py:130
  72.5 2.2 %add_convert_fusion.3 = bf16[8,128,128]{2,1,0:T(8,128)(2,1)} fusion(f32[8,128,128]{2,1,0:T(8,128)} %collective-permute-done.2, f32[8,128,128]{2,1,0:T(8,128)} %get-tuple-element.38, bf16[2,8,128,128]{3,2,1,0:T(8,128)(2,1)} %collective-permute-done.1, pred[]{:T(512)S(6)} %eq.14), kind=kLoop, calls=%fused_computation.5 | loop fusion | flops 655360 | bytes 1835009 | tf_op jit(solution)/shard_map/convert_element_type | solution.py:326
  74.7 6.1 %all-to-all-start = ((bf16[8,128,128]{2,1,0:T(8,128)(2,1)}), bf16[8,128,128]{2,1,0:T(8,128)(2,1)S(1)}, u32[]{:S(2)}, u32[]{:S(2)}) async-start(bf16[8,128,128]{2,1,0:T(8,128)(2,1)} %add_convert_fusion.3), calls=%async_computation | async-start | bytes 524288 | tf_op jit(solution)/shard_map/all_to_all | solution.py:308
  81.5 8.8 %all-to-all-done.part_ref = bf16[8,128,128]{2,1,0:T(8,128)(2,1)S(1)} async-done(((bf16[8,128,128]{2,1,0:T(8,128)(2,1)}), bf16[8,128,128]{2,1,0:T(8,128)(2,1)S(1)}, u32[]{:S(2)}, u32[]{:S(2)}) %all-to-all-start) | async-done | bytes 262176 | tf_op jit(solution)/shard_map/all_to_all | solution.py:308
  90.3 4.0 %all-to-all-start.2 = ((bf16[8,128,128]{2,1,0:T(8,128)(2,1)}), bf16[8,128,128]{2,1,0:T(8,128)(2,1)}, u32[]{:S(2)}, u32[]{:S(2)}) async-start(bf16[8,128,128]{2,1,0:T(8,128)(2,1)} %add_convert_fusion.1), calls=%async_computation.2 | async-start | bytes 524288 | tf_op jit(solution)/shard_map/all_to_all | solution.py:308
  94.4 1.7 %running.2 = bf16[8,128,128]{2,1,0:T(8,128)(2,1)} custom-call(s32[1]{0:T(128)} %bitcast.5.up_ref, bf16[8,128,128]{2,1,0:T(8,128)(2,1)} %copy-done.1), custom_call_target="tpu_custom_call" | custom-call | flops 131072 | bytes 524288 | tf_op jit(solution)/shard_map/running/pallas_call | solution.py:309
  96.1 7.0 %all-to-all-done.2.part_ref = bf16[8,128,128]{2,1,0:T(8,128)(2,1)} async-done(((bf16[8,128,128]{2,1,0:T(8,128)(2,1)}), bf16[8,128,128]{2,1,0:T(8,128)(2,1)}, u32[]{:S(2)}, u32[]{:S(2)}) %all-to-all-start.2) | async-done | bytes 262176 | tf_op jit(solution)/shard_map/all_to_all | solution.py:308
  103.1 4.0 %all-to-all-start.1 = ((bf16[8,128,128]{2,1,0:T(8,128)(2,1)}), bf16[8,128,128]{2,1,0:T(8,128)(2,1)}, u32[]{:S(2)}, u32[]{:S(2)}) async-start(bf16[8,128,128]{2,1,0:T(8,128)(2,1)} %running.2), calls=%async_computation.1 | async-start | bytes 524288 | tf_op jit(solution)/shard_map/all_to_all | solution.py:317
  107.1 1.6 collective-permute-start.10
  109.2 1.5 collective-permute-start.9
  110.7 4.1 %shard_map.67 = (f32[512,1024]{1,0:T(8,128)}, f32[512,1024]{1,0:T(8,128)}, f32[512,1024]{1,0:T(8,128)}, bf16[3,512,1024]{2,1,0:T(8,128)(2,1)}) custom-call(s32[1]{0:T(128)} %bitcast.col_ref, s32[1]{0:T(128)} %bitcast.1.core_ref, s32[1]{0:T(128)} %bitcast.2.refs_0_, s32[1]{0:T(128)} %bitcast.3.refs_1_, bf16[256,4096]{1,0:T(8,128)(2,1)} %refs_2_.15, ...), custom_call_target="tpu_custom_call" | custom-call | flops 939524096 | bytes 1835008 | tf_op jit(solution)/shard_map/pallas_call | solution.py:247
  114.8 1.7 %running.3 = bf16[8,128,128]{2,1,0:T(8,128)(2,1)} custom-call(s32[1]{0:T(128)} %bitcast.5.up_ref, bf16[8,128,128]{2,1,0:T(8,128)(2,1)} %all-to-all-done.2.part_ref), custom_call_target="tpu_custom_call" | custom-call | flops 131072 | bytes 524288 | tf_op jit(solution)/shard_map/running/pallas_call | solution.py:309
  116.5 5.8 %all-to-all-start.3 = ((bf16[8,128,128]{2,1,0:T(8,128)(2,1)}), bf16[8,128,128]{2,1,0:T(8,128)(2,1)}, u32[]{:S(2)}, u32[]{:S(2)}) async-start(bf16[8,128,128]{2,1,0:T(8,128)(2,1)} %running.3), calls=%async_computation.3 | async-start | bytes 524288 | tf_op jit(solution)/shard_map/all_to_all | solution.py:317
  122.4 4.1 %shard_map.68 = (f32[512,1024]{1,0:T(8,128)}, f32[512,1024]{1,0:T(8,128)}, f32[512,1024]{1,0:T(8,128)}, bf16[3,512,1024]{2,1,0:T(8,128)(2,1)}) custom-call(s32[1]{0:T(128)} %bitcast.col_ref, s32[1]{0:T(128)} %bitcast.1.core_ref, s32[1]{0:T(128)} %bitcast.2.refs_0_, ...), custom_call_target="tpu_custom_call", output_to_operand_aliasing={{0}: (9, {}), {1}: (10, {}), {2}: (11, {}), {3}: (12, {})} | custom-call | flops 939524096 | bytes 1835008 | tf_op jit(solution)/shard_map/pallas_call | solution.py:247
  126.5 2.1 %add_convert_fusion.2 = bf16[8,128,128]{2,1,0:T(8,128)(2,1)} fusion(bf16[8,128,128]{2,1,0:T(8,128)(2,1)} %all-to-all-done.1.refs_7_, f32[8,128,128]{2,1,0:T(8,128)} %get-tuple-element.38, bf16[2,8,128,128]{3,2,1,0:T(8,128)(2,1)} %collective-permute-done.1, pred[]{:T(512)S(6)} %eq.14), kind=kLoop, calls=%fused_computation.4 | loop fusion | flops 786432 | bytes 1572865 | tf_op jit(solution)/shard_map/convert_element_type | solution.py:327
  128.6 5.9 %shard_map.69 = (f32[512,1024]{1,0:T(8,128)}, f32[512,1024]{1,0:T(8,128)}, f32[512,1024]{1,0:T(8,128)}, bf16[3,512,1024]{2,1,0:T(8,128)(2,1)}) custom-call(s32[1]{0:T(128)} %bitcast.col_ref, s32[1]{0:T(128)} %bitcast.1.core_ref, s32[1]{0:T(128)} %bitcast.2.refs_0_, ...), custom_call_target="tpu_custom_call", output_to_operand_aliasing={{0}: (9, {}), {1}: (10, {}), {2}: (11, {}), {3}: (12, {})} | custom-call | flops 1879048192 | bytes 3670016 | tf_op jit(solution)/shard_map/pallas_call | solution.py:247
  134.4 1.9 %add_convert_fusion = bf16[8,128,128]{2,1,0:T(8,128)(2,1)} fusion(f32[8,128,128]{2,1,0:T(8,128)} %get-tuple-element.55, bf16[8,128,128]{2,1,0:T(8,128)(2,1)} %all-to-all-done.3.mine_ref), kind=kLoop, calls=%fused_computation.2 | loop fusion | flops 393216 | bytes 1048576 | tf_op jit(solution)/shard_map/convert_element_type | solution.py:327
  136.8 5.7 %shard_map.70 = (bf16[512,2048]{1,0:T(8,128)(2,1)}, bf16[512,2048]{1,0:T(8,128)(2,1)}, bf16[512,2048]{1,0:T(8,128)(2,1)}) custom-call(s32[1]{0:T(128)} %bitcast.col_ref, s32[1]{0:T(128)} %bitcast.1.core_ref, s32[1]{0:T(128)} %bitcast.2.refs_0_, s32[1]{0:T(128)} %bitcast.3.refs_1_, bf16[256,4096]{1,0:T(8,128)(2,1)} %refs_2_.15, bf16[256,4096]{1,0:T(8,128)(2,1)} %refs_3_.15, ...), custom_call_target="tpu_custom_call" | custom-call | flops 1879048192 | bytes 3670016 | tf_op jit(solution)/shard_map/pallas_call | solution.py:247
  142.5 11.2 %collective-permute-done.9.refs_6_ = bf16[4,256,256]{2,1,0:T(8,128)(2,1)} collective-permute-done((bf16[4,256,256]{2,1,0:T(8,128)(2,1)}, bf16[4,256,256]{2,1,0:T(8,128)(2,1)}, u32[]{:S(2)}, u32[]{:S(2)}) %collective-permute-start.9) | collective-permute-done | bytes 524320 | tf_op jit(solution)/shard_map/ppermute | solution.py:353
  153.7 3.8 %shard_map.71 = (bf16[512,2048]{1,0:T(8,128)(2,1)}, bf16[512,2048]{1,0:T(8,128)(2,1)}, bf16[512,2048]{1,0:T(8,128)(2,1)}) custom-call(s32[1]{0:T(128)} %bitcast.col_ref, s32[1]{0:T(128)} %bitcast.1.core_ref, s32[1]{0:T(128)} %bitcast.2.refs_0_, s32[1]{0:T(128)} %bitcast.3.refs_1_, ...), custom_call_target="tpu_custom_call", output_to_operand_aliasing={{0}: (11, {}), {1}: (12, {}), {2}: (13, {})} | custom-call | flops 939524096 | bytes 1835008 | tf_op jit(solution)/shard_map/pallas_call | solution.py:247
  157.6 6.3 %across.1 = (bf16[512,2048]{1,0:T(8,128)(2,1)}, bf16[512,2048]{1,0:T(8,128)(2,1)}, bf16[512,2048]{1,0:T(8,128)(2,1)}) custom-call(s32[1]{0:T(128)} %bitcast.1.core_ref, bf16[3,512,1024]{2,1,0:T(8,128)(2,1)} %get-tuple-element.50.rows_ref, bf16[8,128,128]{2,1,0:T(8,128)(2,1)} %all-to-all-done.3.mine_ref, ...), custom_call_target="tpu_custom_call", output_to_operand_aliasing={{0}: (7, {}), {1}: (8, {}), {2}: (9, {})} | custom-call | flops 402653184 | bytes 12582912 | tf_op jit(solution)/shard_map/across/pallas_call | solution.py:267
  163.9 3.8 %shard_map.72 = (bf16[512,2048]{1,0:T(8,128)(2,1)}, bf16[512,2048]{1,0:T(8,128)(2,1)}, bf16[512,2048]{1,0:T(8,128)(2,1)}) custom-call(s32[1]{0:T(128)} %bitcast.col_ref, s32[1]{0:T(128)} %bitcast.1.core_ref, s32[1]{0:T(128)} %bitcast.2.refs_0_, s32[1]{0:T(128)} %bitcast.3.refs_1_, ...), custom_call_target="tpu_custom_call", output_to_operand_aliasing={{0}: (11, {}), {1}: (12, {}), {2}: (13, {})} | custom-call | flops 939524096 | bytes 1835008 | tf_op jit(solution)/shard_map/pallas_call | solution.py:247
  (23 shorter events, 3.2 us)
Async XLA Ops:
  4.7 16.1 %collective-permute-start.1 = (bf16[2,8,128,128]{3,2,1,0:T(8,128)(2,1)}, bf16[2,8,128,128]{3,2,1,0:T(8,128)(2,1)}, u32[]{:S(2)}, u32[]{:S(2)}) collective-permute-start(bf16[2,8,128,128]{3,2,1,0:T(8,128)(2,1)} %states.1), channel_id=1, source_target_pairs={{0,1},{1,0},{2,3},{3,2},{4,5},{5,4},{6,7},{7,6},{8,9},{9,8},{10,11... | collective-permute-start | bytes 1572872 | tf_op jit(solution)/shard_map/ppermute | solution.py:353
  11.5 58.1 %collective-permute-start.4 = (bf16[4,256,512]{2,1,0:T(8,128)(2,1)}, bf16[4,256,512]{2,1,0:T(8,128)(2,1)}, u32[]{:S(2)}, u32[]{:S(2)}) collective-permute-start(bf16[4,256,512]{2,1,0:T(8,128)(2,1)} %get-tuple-element.40), channel_id=1, source_target_pairs={{0,1},{1,0},{2,3},{3,2},{4,5},{5,4},{6,7},{7,6},{8,9},{9,8},{10,11... | collective-permute-start | bytes 3145736 | tf_op jit(solution)/shard_map/ppermute | solution.py:353
  11.5 55.7 %collective-permute-start.5 = (bf16[4,256,256]{2,1,0:T(8,128)(2,1)}, bf16[4,256,256]{2,1,0:T(8,128)(2,1)}, u32[]{:S(2)}, u32[]{:S(2)}) collective-permute-start(bf16[4,256,256]{2,1,0:T(8,128)(2,1)} %get-tuple-element.41), channel_id=1, source_target_pairs={{0,1},{1,0},{2,3},{3,2},{4,5},{5,4},{6,7},{7,6},{8,9},{9,8},{10,11... | collective-permute-start | bytes 1572872 | tf_op jit(solution)/shard_map/ppermute | solution.py:353
  15.4 49.5 %collective-permute-start.6 = (bf16[4,256,256]{2,1,0:T(8,128)(2,1)}, bf16[4,256,256]{2,1,0:T(8,128)(2,1)}, u32[]{:S(2)}, u32[]{:S(2)}) collective-permute-start(bf16[4,256,256]{2,1,0:T(8,128)(2,1)} %pack.3), channel_id=1, source_target_pairs={{0,1},{1,0},{2,3},{3,2},{4,5},{5,4},{6,7},{7,6},{8,9},{9,8},{10,11... | collective-permute-start | bytes 1572872 | tf_op jit(solution)/shard_map/ppermute | solution.py:353
  22.8 49.7 %collective-permute-start.2 = (f32[8,128,128]{2,1,0:T(8,128)}, f32[8,128,128]{2,1,0:T(8,128)}, u32[]{:S(2)}, u32[]{:S(2)}) collective-permute-start(f32[8,128,128]{2,1,0:T(8,128)} %convert_add_fusion), channel_id=1, source_target_pairs={{0,2},{2,0},{4,6},{6,4},{8,10},{10,8},{12,14},{14,12},{16,18},{18,... | collective-permute-start | bytes 1572872 | tf_op jit(solution)/shard_map/ppermute | solution.py:324
  72.4 8.4 %copy-start = (f32[8,128,128]{2,1,0:T(8,128)S(1)}, f32[8,128,128]{2,1,0:T(8,128)}, u32[]{:S(2)}) copy-start(f32[8,128,128]{2,1,0:T(8,128)} %get-tuple-element.55) | copy-start | bytes 1572868
  72.4 8.4 %collective-permute-start.7 = (f32[8,128,128]{2,1,0:T(8,128)}, f32[8,128,128]{2,1,0:T(8,128)S(1)}, u32[]{:S(2)}, u32[]{:S(2)}) collective-permute-start(f32[8,128,128]{2,1,0:T(8,128)} %get-tuple-element.56), channel_id=1, source_target_pairs={{0,2},{2,0},{4,6},{6,4},{8,10},{10,8},{12,14},{14,12},{16,18},{18,... | collective-permute-start | bytes 1572872 | tf_op jit(solution)/shard_map/ppermute | solution.py:324
  74.7 15.6 %all-to-all-start = ((bf16[8,128,128]{2,1,0:T(8,128)(2,1)}), bf16[8,128,128]{2,1,0:T(8,128)(2,1)S(1)}, u32[]{:S(2)}, u32[]{:S(2)}) async-start(bf16[8,128,128]{2,1,0:T(8,128)(2,1)} %add_convert_fusion.3), calls=%async_computation | async-start | bytes 524288 | tf_op jit(solution)/shard_map/all_to_all | solution.py:308
  90.3 4.1 %copy-start.1 = (bf16[8,128,128]{2,1,0:T(8,128)(2,1)}, bf16[8,128,128]{2,1,0:T(8,128)(2,1)S(1)}, u32[]{:S(2)}) copy-start(bf16[8,128,128]{2,1,0:T(8,128)(2,1)S(1)} %all-to-all-done.part_ref) | copy-start | bytes 786436
  90.3 12.8 %all-to-all-start.2 = ((bf16[8,128,128]{2,1,0:T(8,128)(2,1)}), bf16[8,128,128]{2,1,0:T(8,128)(2,1)}, u32[]{:S(2)}, u32[]{:S(2)}) async-start(bf16[8,128,128]{2,1,0:T(8,128)(2,1)} %add_convert_fusion.1), calls=%async_computation.2 | async-start | bytes 524288 | tf_op jit(solution)/shard_map/all_to_all | solution.py:308
  103.1 13.4 %all-to-all-start.1 = ((bf16[8,128,128]{2,1,0:T(8,128)(2,1)}), bf16[8,128,128]{2,1,0:T(8,128)(2,1)}, u32[]{:S(2)}, u32[]{:S(2)}) async-start(bf16[8,128,128]{2,1,0:T(8,128)(2,1)} %running.2), calls=%async_computation.1 | async-start | bytes 524288 | tf_op jit(solution)/shard_map/all_to_all | solution.py:317
  107.1 29.7 %collective-permute-start.10 = (bf16[4,256,512]{2,1,0:T(8,128)(2,1)}, bf16[4,256,512]{2,1,0:T(8,128)(2,1)}, u32[]{:S(2)}, u32[]{:S(2)}) collective-permute-start(bf16[4,256,512]{2,1,0:T(8,128)(2,1)} %get-tuple-element.61), channel_id=1, source_target_pairs={{0,1},{1,0},{2,3},{3,2},{4,5},{5,4},{6,7},{7,6},{8,9},{9,8},{10,11... | collective-permute-start | bytes 3145736 | tf_op jit(solution)/shard_map/ppermute | solution.py:353
  108.7 55.2 %collective-permute-start = (bf16[4,256,256]{2,1,0:T(8,128)(2,1)}, bf16[4,256,256]{2,1,0:T(8,128)(2,1)}, u32[]{:S(2)}, u32[]{:S(2)}) collective-permute-start(bf16[4,256,256]{2,1,0:T(8,128)(2,1)} %get-tuple-element.37), channel_id=1, source_target_pairs={{0,1},{1,0},{2,3},{3,2},{4,5},{5,4},{6,7},{7,6},{8,9},{9,8},{10,11... | collective-permute-start | bytes 1572872 | tf_op jit(solution)/shard_map/ppermute | solution.py:353
  109.2 44.5 %collective-permute-start.9 = (bf16[4,256,256]{2,1,0:T(8,128)(2,1)}, bf16[4,256,256]{2,1,0:T(8,128)(2,1)}, u32[]{:S(2)}, u32[]{:S(2)}) collective-permute-start(bf16[4,256,256]{2,1,0:T(8,128)(2,1)} %get-tuple-element.60), channel_id=1, source_target_pairs={{0,1},{1,0},{2,3},{3,2},{4,5},{5,4},{6,7},{7,6},{8,9},{9,8},{10,11... | collective-permute-start | bytes 1572872 | tf_op jit(solution)/shard_map/ppermute | solution.py:353
  116.5 17.9 %all-to-all-start.3 = ((bf16[8,128,128]{2,1,0:T(8,128)(2,1)}), bf16[8,128,128]{2,1,0:T(8,128)(2,1)}, u32[]{:S(2)}, u32[]{:S(2)}) async-start(bf16[8,128,128]{2,1,0:T(8,128)(2,1)} %running.3), calls=%async_computation.3 | async-start | bytes 524288 | tf_op jit(solution)/shard_map/all_to_all | solution.py:317
  128.5 8.3 %collective-permute-start.3 = (bf16[8,128,128]{2,1,0:T(8,128)(2,1)}, bf16[8,128,128]{2,1,0:T(8,128)(2,1)}, u32[]{:S(2)}, u32[]{:S(2)}) collective-permute-start(bf16[8,128,128]{2,1,0:T(8,128)(2,1)} %add_convert_fusion.2), channel_id=1, source_target_pairs={{0,2},{2,0},{4,6},{6,4},{8,10},{10,8},{12,14},{14,12},{16,18},{18,... | collective-permute-start | bytes 786440 | tf_op jit(solution)/shard_map/ppermute | solution.py:327
  136.3 21.2 %collective-permute-start.8 = (bf16[8,128,128]{2,1,0:T(8,128)(2,1)}, bf16[8,128,128]{2,1,0:T(8,128)(2,1)}, u32[]{:S(2)}, u32[]{:S(2)}) collective-permute-start(bf16[8,128,128]{2,1,0:T(8,128)(2,1)} %add_convert_fusion), channel_id=1, source_target_pairs={{0,2},{2,0},{4,6},{6,4},{8,10},{10,8},{12,14},{14,12},{16,18},{18,... | collective-permute-start | bytes 786440 | tf_op jit(solution)/shard_map/ppermute | solution.py:327

commit v5 on v4

--- a/solution.py
+++ b/solution.py
@@ -182,15 +182,16 @@
         yield grad, down, second[down]
 
 
-def prefix_suffix(core_ref, mine_ref, other_ref, j):
-    first, mine, other = core_ref[0] == 0, mine_ref[j], other_ref[j]
+def prefix_suffix(core_ref, mine_ref, other_ref, theirs_ref, j):
+    first, mine = core_ref[0] == 0, mine_ref[j]
+    other = (other_ref[j].astype(F32) + theirs_ref[j]).astype(BF16)
     return jnp.where(first, mine, other), jnp.where(first, other, mine)
 
 
 def whole_kernel(peers, aliased, scale, col_ref, core_ref, *refs):
     src, refs = refs[: peers + 1], refs[peers + 1 :]
-    owns, got, sums = refs[:4], refs[4 : 4 + peers], refs[4 + peers : 6 + peers]
-    outs, all_ref = refs[6 + peers + 3 * aliased : -1], refs[-1]
+    owns, got, sums = refs[:4], refs[4 : 4 + peers], refs[4 + peers : 7 + peers]
+    outs, all_ref = refs[7 + peers + 3 * aliased : -1], refs[-1]
     gather_rows(src, owns, got, range(4), all_ref)
     for j in range(PAIR // DK):
         at = slice(j * DK, (j + 1) * DK)
@@ -210,16 +211,16 @@
     for j in range(PAIR // DK):
         at = slice(j * DK, (j + 1) * DK)
         for grad, rows, value in within(all_ref, at):
-            outs[grad][rows, at] = value
-
-
-def across_kernel(aliased, scale, core_ref, rows_ref, mine_ref, other_ref, *refs):
-    parts, outs = refs[:3], refs[3 + 3 * aliased :]
-    for j in range(PAIR // DK):
-        at = slice(j * DK, (j + 1) * DK)
-        prefix, suffix = prefix_suffix(core_ref, mine_ref, other_ref, j)
+            outs[grad][rows, at] = value.astype(BF16)
+
+
+def across_kernel(aliased, scale, core_ref, rows_ref, *refs):
+    sums, parts, outs = refs[:3], refs[3:6], refs[6 + 3 * aliased :]
+    for j in range(PAIR // DK):
+        at = slice(j * DK, (j + 1) * DK)
+        prefix, suffix = prefix_suffix(core_ref, *sums, j)
         for grad, (which, state, dims) in enumerate(((2, prefix, NT), (1, suffix, NT), (0, suffix, NN))):
-            value = parts[grad][:, at] + mm(rows_ref[which, :, at], state, dims)
+            value = parts[grad][:, at].astype(F32) + mm(rows_ref[which, :, at], state, dims)
             outs[grad][:, at] = (scale * value).astype(BF16)
 
 
@@ -234,11 +235,11 @@
     there = pl.BlockSpec((4, rows, PAIR), lambda i, c, *s: (0, 0, i))
     operands, specs = [*arrays, *got], [own] * 4 + [there] * len(got)
     here = pl.BlockSpec((total, PAIR), lambda i, c, *s: (0, base + i))
-    outs, shapes = [here] * 3, [jax.ShapeDtypeStruct((total, room * PAIR), BF16 if whole else F32)] * 3
+    outs, shapes = [here] * 3, [jax.ShapeDtypeStruct((total, room * PAIR), BF16)] * 3
     if whole:
         sums, offset = sums
         operands += sums
-        specs += [pl.BlockSpec((PAIR // DK, DK, DK), lambda i, c, *s: (offset + i, 0, 0))] * 2
+        specs += [pl.BlockSpec((PAIR // DK, DK, DK), lambda i, c, *s: (offset + i, 0, 0))] * 3
     else:
         outs.append(pl.BlockSpec((3, total, PAIR), lambda i, c, *s: (0, 0, base + i)))
         shapes.append(jax.ShapeDtypeStruct((3, total, room * PAIR), BF16))
@@ -271,14 +272,14 @@
             grid=(pairs,),
             in_specs=[
                 pl.BlockSpec((3, total, PAIR), lambda i, d: (0, 0, i)),
-                *[pl.BlockSpec((PAIR // DK, DK, DK), lambda i, d: (i, 0, 0))] * 2,
+                *[pl.BlockSpec((PAIR // DK, DK, DK), lambda i, d: (i, 0, 0))] * 3,
                 *[here] * 3,
                 *[ANY] * len(shared),
             ],
             out_specs=[here] * 3,
         ),
         out_shape=[jax.ShapeDtypeStruct((total, room * PAIR), BF16)] * 3,
-        input_output_aliases={7 + j: j for j in range(len(shared))},
+        input_output_aliases={8 + j: j for j in range(len(shared))},
         cost_estimate=cost(6 * total * DK * PAIR * pairs, 24 * total * PAIR * pairs),
         compiler_params=pltpu.CompilerParams(vmem_limit_bytes=VMEM_LIMIT),
         name="across",
@@ -322,9 +323,10 @@
     count = lax.axis_size("seq")
     swap = [(i, i ^ 1) for i in range(count)]
     chip = keep + lax.ppermute(give, "seq", swap)
+    theirs = lax.ppermute(keep, "seq", swap)
     groups = [list(range(core, count, 2)) for core in (0, 1)]
     mine = deal_and_sum(chip.astype(BF16), lax.axis_index("seq") % 2 == 0, groups)
-    return mine, lax.ppermute((mine.astype(F32) + keep).astype(BF16), "seq", swap)
+    return mine, lax.ppermute(mine, "seq", swap), theirs
 
 
 def local(queries, key_vectors, value_vectors, out_grads):
@@ -340,9 +342,9 @@
     scale = 1.0 / math.sqrt(DK * total_tokens)
     late = pairs_here // 2
     early = pairs_here - late
-    sizes = [n for n in (1, (early - 1) // 2, early - 1 - (early - 1) // 2) if n]
+    sizes = [1] * early
     split = len(sizes)
-    sizes += [n for n in (late - 2 * (late // 4), late // 4, late // 4) if n]
+    sizes += [n for n in (late - 3 * (late // 4), late // 4, late // 4, late // 4) if n]
     firsts = [sum(sizes[:i]) for i in range(len(sizes))]
     shifts = range(1, peers)
     cols = [jnp.reshape((place + s) % peers * pairs_here, (1,)).astype(jnp.int32) for s in range(peers)]

time: 169 us -> 169 us (level)
  Pallas kernels: 58.5 us -> 63.7 us
  other arithmetic: 8.97 us -> 5.21 us
  waiting for transfers between devices: 70.1 us -> 67.1 us
    ppermute x7 -> x9, waiting for transfers between devices: 54.3 us -> 45.9 us  [move(): lax.ppermute(value, 'head', [(i, (i + s) % peers) for i in range(peers)])]
    all_to_all x2, waiting for transfers between devices: 0.01 us -> 5.08 us  [deal_and_sum(): lax.all_to_all(mine, 'seq', 0, 0, tiled=True, axis_index_groups=groups)]
    convert_element_type x2 -> x0, other arithmetic: 3.97 us -> none  [scan_chips(): (mine.astype(F32) + keep).astype(BF16)]
    pallas_call x6 -> x8, Pallas kernels: 27.5 us -> 31 us  [outputs(): pl.pallas_call(functools.partial(kernel, len(got), int(into is not None),...]
    ppermute x7 -> x9, starting transfers between devices: 8.78 us -> 12.3 us  [move(): lax.ppermute(value, 'head', [(i, (i + s) % peers) for i in range(peers)])]
    pallas_call x4 -> x5, Pallas kernels: 11.7 us -> 13.7 us  [split_states(): pl.pallas_call(functools.partial(split_kernel, len(got)), grid_spec=pltpu...]
  transfers between devices with their start and end apart: 15 -> 19, of which waited for: 5 -> 6; matrix products, arithmetic and copies ran while one was open for 5% -> 3% of each run, Pallas kernels for 30% -> 33%
where the time goes in v5:
time: 169 us; the launch traced here: 168 us
  waiting for transfers between devices  67.1 us (40%)
  Pallas kernels  63.7 us (38%)
  starting transfers between devices  30.9 us (18%)
  other arithmetic  5.21 us (3%)
    ppermute x9, waiting for transfers between devices, move(): lax.ppermute(value, 'head', [(i, (i + s) % peers) for i in range(peers)])  45.9 us
    pallas_call x8, Pallas kernels, outputs(): pl.pallas_call(functools.partial(kernel, len(got), int(into is not None),...  31 us
    all_to_all x2, waiting for transfers between devices, deal_and_sum(): lax.all_to_all(own.reshape(count, -1, DK), 'seq', 0, 0, tiled=True, axis_...  16.1 us
    pallas_call x5, Pallas kernels, split_states(): pl.pallas_call(functools.partial(split_kernel, len(got)), grid_spec=pltpu...  13.7 us
    ppermute x9, starting transfers between devices, move(): lax.ppermute(value, 'head', [(i, (i + s) % peers) for i in range(peers)])  12.3 us
    all_to_all x2, starting transfers between devices, deal_and_sum(): lax.all_to_all(own.reshape(count, -1, DK), 'seq', 0, 0, tiled=True, axis_...  9.68 us
    all_to_all x2, starting transfers between devices, deal_and_sum(): lax.all_to_all(mine, 'seq', 0, 0, tiled=True, axis_index_groups=groups)  8.28 us
    pallas_call x2, Pallas kernels, pack(): pl.pallas_call(functools.partial(pack_kernel, sizes, first, peers), in_sp...  5.91 us
  transfers between devices with their start and end apart: 19, of which 6 were waited for; matrix products, arithmetic and copies ran while one was open for 3% of the time, Pallas kernels for 33%

profile of v5, /device:TPU:0, one launch (start us, length us, event | category | flops | bytes accessed | tf_op | source)
XLA Modules:
  0.0 167.7 jit_solution(15925672927224396058)
XLA Ops:
  0.6 4.1 %states.1 = bf16[2,8,128,128]{3,2,1,0:T(8,128)(2,1)} custom-call(s32[1]{0:T(128)} %bitcast.4.refs_0_.col_ref, bf16[256,4096]{1,0:T(8,128)(2,1)} %refs_2_.19, bf16[256,4096]{1,0:T(8,128)(2,1)} %refs_3_.19, bf16[256,4096]{1,0:T(8,128)(2,1)} %refs_4_.19, bf16[256,4096]{1,0:T(8,128)(2,1)} %refs_5_.15), custom_call_target="tpu_custom_call" | custom-call | flops 134217728 | bytes 2097152 | tf_op jit(solution)/shard_map/states/pallas_call | solution.py:93
  4.7 3.0 %collective-permute-start.1 = (bf16[2,8,128,128]{3,2,1,0:T(8,128)(2,1)}, bf16[2,8,128,128]{3,2,1,0:T(8,128)(2,1)}, u32[]{:S(2)}, u32[]{:S(2)}) collective-permute-start(bf16[2,8,128,128]{3,2,1,0:T(8,128)(2,1)} %states.1), channel_id=1, source_target_pairs={{0,1},{1,0},{2,3},{3,2},{4,5},{5,4},{6,7},{7,6},{8,9},{9,8},{10,11... | collective-permute-start | bytes 1572872 | tf_op jit(solution)/shard_map/ppermute | solution.py:355
  7.7 1.8 %pack.3 = bf16[4,256,256]{2,1,0:T(8,128)(2,1)} custom-call(s32[1]{0:T(128)} %bitcast.4.refs_0_.col_ref, bf16[256,4096]{1,0:T(8,128)(2,1)} %refs_2_.19, bf16[256,4096]{1,0:T(8,128)(2,1)} %refs_3_.19, bf16[256,4096]{1,0:T(8,128)(2,1)} %refs_4_.19, bf16[256,4096]{1,0:T(8,128)(2,1)} %refs_5_.15), custom_call_target="tpu_custom_call" | custom-call | bytes 1048576 | tf_op jit(solution)/shard_map/pack/pallas_call | solution.py:60
  9.6 4.1 %pack.2 = (bf16[4,256,256]{2,1,0:T(8,128)(2,1)}, bf16[4,256,256]{2,1,0:T(8,128)(2,1)}, bf16[4,256,256]{2,1,0:T(8,128)(2,1)}, bf16[4,256,256]{2,1,0:T(8,128)(2,1)...) custom-call(s32[1]{0:T(128)} %bitcast.4.refs_0_.col_ref, ...), custom_call_target="tpu_custom_call" | custom-call | bytes 7340032 | tf_op jit(solution)/shard_map/pack/pallas_call | solution.py:60
  13.7 2.1 %collective-permute-start.5 = (bf16[4,256,256]{2,1,0:T(8,128)(2,1)}, bf16[4,256,256]{2,1,0:T(8,128)(2,1)}, u32[]{:S(2)}, u32[]{:S(2)}) collective-permute-start(bf16[4,256,256]{2,1,0:T(8,128)(2,1)} %get-tuple-element.51), channel_id=1, source_target_pairs={{0,1},{1,0},{2,3},{3,2},{4,5},{5,4},{6,7},{7,6},{8,9},{9,8},{10,11... | collective-permute-start | bytes 1572872 | tf_op jit(solution)/shard_map/ppermute | solution.py:355
  15.8 1.9 %collective-permute-start.7 = (bf16[4,256,256]{2,1,0:T(8,128)(2,1)}, bf16[4,256,256]{2,1,0:T(8,128)(2,1)}, u32[]{:S(2)}, u32[]{:S(2)}) collective-permute-start(bf16[4,256,256]{2,1,0:T(8,128)(2,1)} %get-tuple-element.53), channel_id=1, source_target_pairs={{0,1},{1,0},{2,3},{3,2},{4,5},{5,4},{6,7},{7,6},{8,9},{9,8},{10,11... | collective-permute-start | bytes 1572872 | tf_op jit(solution)/shard_map/ppermute | solution.py:355
  17.8 4.2 %split_states.5 = (f32[8,128,128]{2,1,0:T(8,128)}, f32[8,128,128]{2,1,0:T(8,128)}) custom-call(s32[1]{0:T(128)} %bitcast.col_ref, s32[1]{0:T(128)} %bitcast.1.core_ref, bf16[256,4096]{1,0:T(8,128)(2,1)} %refs_2_.19, bf16[256,4096]{1,0:T(8,128)(2,1)} %refs_3_.19, bf16[256,4096]{1,0:T(8,128)(2,1)} %refs_4_.19, bf16[256,4096]{1,0:T(8,128)(2,1)} %refs_5_.15), custom_call_target="tpu_custom_call" | custom-call | flops 134217728 | bytes 2097152 | tf_op jit(solution)/shard_map/split_states/pallas_call | solution.py:130
  21.9 2.1 %convert_add_fusion = f32[8,128,128]{2,1,0:T(8,128)} fusion(f32[8,128,128]{2,1,0:T(8,128)} %get-tuple-element.50, pred[]{:T(512)S(6)} %eq.14, bf16[2,8,128,128]{3,2,1,0:T(8,128)(2,1)} %collective-permute-done.1), kind=kLoop, calls=%fused_computation | loop fusion | flops 393216 | bytes 1572865 | tf_op jit(solution)/shard_map/add | solution.py:368
  24.0 8.0 %collective-permute-done.8.refs_6_.rest_0_ = bf16[4,256,256]{2,1,0:T(8,128)(2,1)} collective-permute-done((bf16[4,256,256]{2,1,0:T(8,128)(2,1)}, bf16[4,256,256]{2,1,0:T(8,128)(2,1)}, u32[]{:S(2)}, u32[]{:S(2)}) %collective-permute-start.8) | collective-permute-done | bytes 524320 | tf_op jit(solution)/shard_map/ppermute | solution.py:355
  32.0 2.4 %split_states.6 = (f32[8,128,128]{2,1,0:T(8,128)}, f32[8,128,128]{2,1,0:T(8,128)}) custom-call(s32[1]{0:T(128)} %bitcast.col_ref, s32[1]{0:T(128)} %bitcast.1.core_ref, bf16[256,4096]{1,0:T(8,128)(2,1)} %refs_2_.19, bf16[256,4096]{1,0:T(8,128)(2,1)} %refs_3_.19, bf16[256,4096]{1,0:T(8,128)(2,1)} %refs_4_.19, bf16[256,4096]{1,0:T(8,128)(2,1)} %refs_5_.15, ...), custom_call_target="tpu_custom_call" | custom-call | flops 67108864 | bytes 1048576 | tf_op jit(solution)/shard_map/split_states/pallas_call | solution.py:130
  34.4 30.5 %collective-permute-done.7.refs_6_.rest_0_ = bf16[4,256,256]{2,1,0:T(8,128)(2,1)} collective-permute-done((bf16[4,256,256]{2,1,0:T(8,128)(2,1)}, bf16[4,256,256]{2,1,0:T(8,128)(2,1)}, u32[]{:S(2)}, u32[]{:S(2)}) %collective-permute-start.7) | collective-permute-done | bytes 524320 | tf_op jit(solution)/shard_map/ppermute | solution.py:355
  64.9 2.4 %split_states.7 = (f32[8,128,128]{2,1,0:T(8,128)}, f32[8,128,128]{2,1,0:T(8,128)}) custom-call(s32[1]{0:T(128)} %bitcast.col_ref, s32[1]{0:T(128)} %bitcast.1.core_ref, bf16[256,4096]{1,0:T(8,128)(2,1)} %refs_2_.19, bf16[256,4096]{1,0:T(8,128)(2,1)} %refs_3_.19, bf16[256,4096]{1,0:T(8,128)(2,1)} %refs_4_.19, ...), custom_call_target="tpu_custom_call", output_to_operand_aliasing={{0}: (7, {}), {1}: (8, {})} | custom-call | flops 67108864 | bytes 1048576 | tf_op jit(solution)/shard_map/split_states/pallas_call | solution.py:130
  67.2 2.4 %split_states.8 = (f32[8,128,128]{2,1,0:T(8,128)}, f32[8,128,128]{2,1,0:T(8,128)}) custom-call(s32[1]{0:T(128)} %bitcast.col_ref, s32[1]{0:T(128)} %bitcast.1.core_ref, bf16[256,4096]{1,0:T(8,128)(2,1)} %refs_2_.19, bf16[256,4096]{1,0:T(8,128)(2,1)} %refs_3_.19, bf16[256,4096]{1,0:T(8,128)(2,1)} %refs_4_.19, ...), custom_call_target="tpu_custom_call", output_to_operand_aliasing={{0}: (7, {}), {1}: (8, {})} | custom-call | flops 67108864 | bytes 1048576 | tf_op jit(solution)/shard_map/split_states/pallas_call | solution.py:130
  69.6 2.4 %split_states.9 = (f32[8,128,128]{2,1,0:T(8,128)}, f32[8,128,128]{2,1,0:T(8,128)}) custom-call(s32[1]{0:T(128)} %bitcast.col_ref, s32[1]{0:T(128)} %bitcast.1.core_ref, bf16[256,4096]{1,0:T(8,128)(2,1)} %refs_2_.19, bf16[256,4096]{1,0:T(8,128)(2,1)} %refs_3_.19, bf16[256,4096]{1,0:T(8,128)(2,1)} %refs_4_.19, ...), custom_call_target="tpu_custom_call", output_to_operand_aliasing={{0}: (7, {}), {1}: (8, {})} | custom-call | flops 67108864 | bytes 1048576 | tf_op jit(solution)/shard_map/split_states/pallas_call | solution.py:130
  72.0 2.4 %add_convert_fusion.1 = (bf16[8,128,128]{2,1,0:T(8,128)(2,1)}, f32[8,128,128]{2,1,0:T(8,128)}) fusion(f32[8,128,128]{2,1,0:T(8,128)} %collective-permute-done.2, f32[8,128,128]{2,1,0:T(8,128)} %get-tuple-element.49, bf16[2,8,128,128]{3,2,1,0:T(8,128)(2,1)} %collective-permute-done.1, pred[]{:T(512)S(6)} %eq.14), kind=kLoop, calls=%fused_computation.3 | loop fusion | flops 655360 | bytes 2359297 | tf_op jit(solution)/shard_map/convert_element_type | solution.py:328
  74.4 6.1 %all-to-all-start = ((bf16[8,128,128]{2,1,0:T(8,128)(2,1)}), bf16[8,128,128]{2,1,0:T(8,128)(2,1)S(1)}, u32[]{:S(2)}, u32[]{:S(2)}) async-start(bf16[8,128,128]{2,1,0:T(8,128)(2,1)} %get-tuple-element.93), calls=%async_computation | async-start | bytes 524288 | tf_op jit(solution)/shard_map/all_to_all | solution.py:309
  81.3 8.8 %all-to-all-done.part_ref = bf16[8,128,128]{2,1,0:T(8,128)(2,1)S(1)} async-done(((bf16[8,128,128]{2,1,0:T(8,128)(2,1)}), bf16[8,128,128]{2,1,0:T(8,128)(2,1)S(1)}, u32[]{:S(2)}, u32[]{:S(2)}) %all-to-all-start) | async-done | bytes 262176 | tf_op jit(solution)/shard_map/all_to_all | solution.py:309
  90.0 3.6 %all-to-all-start.2 = ((bf16[8,128,128]{2,1,0:T(8,128)(2,1)}), bf16[8,128,128]{2,1,0:T(8,128)(2,1)S(1)}, u32[]{:S(2)}, u32[]{:S(2)}) async-start(bf16[8,128,128]{2,1,0:T(8,128)(2,1)} %add_convert_fusion), calls=%async_computation.2 | async-start | bytes 524288 | tf_op jit(solution)/shard_map/all_to_all | solution.py:309
  95.3 7.4 %all-to-all-done.2.part_ref = bf16[8,128,128]{2,1,0:T(8,128)(2,1)S(1)} async-done(((bf16[8,128,128]{2,1,0:T(8,128)(2,1)}), bf16[8,128,128]{2,1,0:T(8,128)(2,1)S(1)}, u32[]{:S(2)}, u32[]{:S(2)}) %all-to-all-start.2) | async-done | bytes 262176 | tf_op jit(solution)/shard_map/all_to_all | solution.py:309
  102.7 4.1 %all-to-all-start.1 = ((bf16[8,128,128]{2,1,0:T(8,128)(2,1)}), bf16[8,128,128]{2,1,0:T(8,128)(2,1)}, u32[]{:S(2)}, u32[]{:S(2)}) async-start(bf16[8,128,128]{2,1,0:T(8,128)(2,1)} %running.2), calls=%async_computation.1 | async-start | bytes 524288 | tf_op jit(solution)/shard_map/all_to_all | solution.py:318
  110.0 5.1 %all-to-all-done.1.refs_7_ = bf16[8,128,128]{2,1,0:T(8,128)(2,1)} async-done(((bf16[8,128,128]{2,1,0:T(8,128)(2,1)}), bf16[8,128,128]{2,1,0:T(8,128)(2,1)}, u32[]{:S(2)}, u32[]{:S(2)}) %all-to-all-start.1) | async-done | bytes 262176 | tf_op jit(solution)/shard_map/all_to_all | solution.py:318
  115.1 4.2 %all-to-all-start.3 = ((bf16[8,128,128]{2,1,0:T(8,128)(2,1)}), bf16[8,128,128]{2,1,0:T(8,128)(2,1)}, u32[]{:S(2)}, u32[]{:S(2)}) async-start(bf16[8,128,128]{2,1,0:T(8,128)(2,1)} %running.3), calls=%async_computation.3 | async-start | bytes 524288 | tf_op jit(solution)/shard_map/all_to_all | solution.py:318
  122.9 3.9 %shard_map.67 = (bf16[512,1024]{1,0:T(8,128)(2,1)}, bf16[512,1024]{1,0:T(8,128)(2,1)}, bf16[512,1024]{1,0:T(8,128)(2,1)}, bf16[3,512,1024]{2,1,0:T(8,128)(2,1)}) custom-call(s32[1]{0:T(128)} %bitcast.col_ref, s32[1]{0:T(128)} %bitcast.1.core_ref, s32[1]{0:T(128)} %bitcast.2.refs_0_, s32[1]{0:T(128)} %bitcast.3.refs_1_, bf16[256,4096]{1,0:T(8,128)(2,1)} %refs_2_.19, ...), custom_call_target="tpu_custom_call" | custom-call | flops 939524096 | bytes 1835008 | tf_op jit(solution)/shard_map/pallas_call | solution.py:248
  127.3 3.9 %shard_map.68 = (bf16[512,1024]{1,0:T(8,128)(2,1)}, bf16[512,1024]{1,0:T(8,128)(2,1)}, bf16[512,1024]{1,0:T(8,128)(2,1)}, bf16[3,512,1024]{2,1,0:T(8,128)(2,1)}) custom-call(s32[1]{0:T(128)} %bitcast.col_ref, s32[1]{0:T(128)} %bitcast.1.core_ref, s32[1]{0:T(128)} %bitcast.2.refs_0_, ...), custom_call_target="tpu_custom_call", output_to_operand_aliasing={{0}: (9, {}), {1}: (10, {}), {2}: (11, {}), {3}: (12, {})} | custom-call | flops 939524096 | bytes 1835008 | tf_op jit(solution)/shard_map/pallas_call | solution.py:248
  131.2 3.9 %shard_map.69 = (bf16[512,1024]{1,0:T(8,128)(2,1)}, bf16[512,1024]{1,0:T(8,128)(2,1)}, bf16[512,1024]{1,0:T(8,128)(2,1)}, bf16[3,512,1024]{2,1,0:T(8,128)(2,1)}) custom-call(s32[1]{0:T(128)} %bitcast.col_ref, s32[1]{0:T(128)} %bitcast.1.core_ref, s32[1]{0:T(128)} %bitcast.2.refs_0_, ...), custom_call_target="tpu_custom_call", output_to_operand_aliasing={{0}: (9, {}), {1}: (10, {}), {2}: (11, {}), {3}: (12, {})} | custom-call | flops 939524096 | bytes 1835008 | tf_op jit(solution)/shard_map/pallas_call | solution.py:248
  135.1 3.9 %shard_map.70 = (bf16[512,1024]{1,0:T(8,128)(2,1)}, bf16[512,1024]{1,0:T(8,128)(2,1)}, bf16[512,1024]{1,0:T(8,128)(2,1)}, bf16[3,512,1024]{2,1,0:T(8,128)(2,1)}) custom-call(s32[1]{0:T(128)} %bitcast.col_ref, s32[1]{0:T(128)} %bitcast.1.core_ref, s32[1]{0:T(128)} %bitcast.2.refs_0_, ...), custom_call_target="tpu_custom_call", output_to_operand_aliasing={{0}: (9, {}), {1}: (10, {}), {2}: (11, {}), {3}: (12, {})} | custom-call | flops 939524096 | bytes 1835008 | tf_op jit(solution)/shard_map/pallas_call | solution.py:248
  139.2 3.9 %shard_map.71 = (bf16[512,2048]{1,0:T(8,128)(2,1)}, bf16[512,2048]{1,0:T(8,128)(2,1)}, bf16[512,2048]{1,0:T(8,128)(2,1)}) custom-call(s32[1]{0:T(128)} %bitcast.col_ref, s32[1]{0:T(128)} %bitcast.1.core_ref, s32[1]{0:T(128)} %bitcast.2.refs_0_, s32[1]{0:T(128)} %bitcast.3.refs_1_, bf16[256,4096]{1,0:T(8,128)(2,1)} %refs_2_.19, bf16[256,4096]{1,0:T(8,128)(2,1)} %refs_3_.19, ...), custom_call_target="tpu_custom_call" | custom-call | flops 939524096 | bytes 1835008 | tf_op jit(solution)/shard_map/pallas_call | solution.py:248
  143.0 3.9 %shard_map.72 = (bf16[512,2048]{1,0:T(8,128)(2,1)}, bf16[512,2048]{1,0:T(8,128)(2,1)}, bf16[512,2048]{1,0:T(8,128)(2,1)}) custom-call(s32[1]{0:T(128)} %bitcast.col_ref, s32[1]{0:T(128)} %bitcast.1.core_ref, s32[1]{0:T(128)} %bitcast.2.refs_0_, s32[1]{0:T(128)} %bitcast.3.refs_1_, ...), custom_call_target="tpu_custom_call", output_to_operand_aliasing={{0}: (12, {}), {1}: (13, {}), {2}: (14, {})} | custom-call | flops 939524096 | bytes 1835008 | tf_op jit(solution)/shard_map/pallas_call | solution.py:248
  146.9 7.4 %collective-permute-done.12.refs_6_ = bf16[4,256,256]{2,1,0:T(8,128)(2,1)} collective-permute-done((bf16[4,256,256]{2,1,0:T(8,128)(2,1)}, bf16[4,256,256]{2,1,0:T(8,128)(2,1)}, u32[]{:S(2)}, u32[]{:S(2)}) %collective-permute-start.12) | collective-permute-done | bytes 524320 | tf_op jit(solution)/shard_map/ppermute | solution.py:355
  154.3 3.9 %shard_map.73 = (bf16[512,2048]{1,0:T(8,128)(2,1)}, bf16[512,2048]{1,0:T(8,128)(2,1)}, bf16[512,2048]{1,0:T(8,128)(2,1)}) custom-call(s32[1]{0:T(128)} %bitcast.col_ref, s32[1]{0:T(128)} %bitcast.1.core_ref, s32[1]{0:T(128)} %bitcast.2.refs_0_, s32[1]{0:T(128)} %bitcast.3.refs_1_, ...), custom_call_target="tpu_custom_call", output_to_operand_aliasing={{0}: (12, {}), {1}: (13, {}), {2}: (14, {})} | custom-call | flops 939524096 | bytes 1835008 | tf_op jit(solution)/shard_map/pallas_call | solution.py:248
  158.2 5.7 %across.1 = (bf16[512,2048]{1,0:T(8,128)(2,1)}, bf16[512,2048]{1,0:T(8,128)(2,1)}, bf16[512,2048]{1,0:T(8,128)(2,1)}) custom-call(s32[1]{0:T(128)} %bitcast.1.core_ref, bf16[3,512,1024]{2,1,0:T(8,128)(2,1)} %get-tuple-element.66.rows_ref, bf16[8,128,128]{2,1,0:T(8,128)(2,1)} %all-to-all-done.3.refs_0_, ...), custom_call_target="tpu_custom_call", output_to_operand_aliasing={{0}: (8, {}), {1}: (9, {}), {2}: (10, {})} | custom-call | flops 402653184 | bytes 12582912 | tf_op jit(solution)/shard_map/across/pallas_call | solution.py:268
  163.8 3.9 %shard_map.74 = (bf16[512,2048]{1,0:T(8,128)(2,1)}, bf16[512,2048]{1,0:T(8,128)(2,1)}, bf16[512,2048]{1,0:T(8,128)(2,1)}) custom-call(s32[1]{0:T(128)} %bitcast.col_ref, s32[1]{0:T(128)} %bitcast.1.core_ref, s32[1]{0:T(128)} %bitcast.2.refs_0_, s32[1]{0:T(128)} %bitcast.3.refs_1_, ...), custom_call_target="tpu_custom_call", output_to_operand_aliasing={{0}: (12, {}), {1}: (13, {}), {2}: (14, {})} | custom-call | flops 939524096 | bytes 1835008 | tf_op jit(solution)/shard_map/pallas_call | solution.py:248
  (34 shorter events, 10.1 us)
Async XLA Ops:
  4.7 17.2 %collective-permute-start.1 = (bf16[2,8,128,128]{3,2,1,0:T(8,128)(2,1)}, bf16[2,8,128,128]{3,2,1,0:T(8,128)(2,1)}, u32[]{:S(2)}, u32[]{:S(2)}) collective-permute-start(bf16[2,8,128,128]{3,2,1,0:T(8,128)(2,1)} %states.1), channel_id=1, source_target_pairs={{0,1},{1,0},{2,3},{3,2},{4,5},{5,4},{6,7},{7,6},{8,9},{9,8},{10,11... | collective-permute-start | bytes 1572872 | tf_op jit(solution)/shard_map/ppermute | solution.py:355
  9.5 22.5 %collective-permute-start.8 = (bf16[4,256,256]{2,1,0:T(8,128)(2,1)}, bf16[4,256,256]{2,1,0:T(8,128)(2,1)}, u32[]{:S(2)}, u32[]{:S(2)}) collective-permute-start(bf16[4,256,256]{2,1,0:T(8,128)(2,1)} %pack.3), channel_id=1, source_target_pairs={{0,1},{1,0},{2,3},{3,2},{4,5},{5,4},{6,7},{7,6},{8,9},{9,8},{10,11... | collective-permute-start | bytes 1572872 | tf_op jit(solution)/shard_map/ppermute | solution.py:355
  13.7 55.9 %collective-permute-start.5 = (bf16[4,256,256]{2,1,0:T(8,128)(2,1)}, bf16[4,256,256]{2,1,0:T(8,128)(2,1)}, u32[]{:S(2)}, u32[]{:S(2)}) collective-permute-start(bf16[4,256,256]{2,1,0:T(8,128)(2,1)} %get-tuple-element.51), channel_id=1, source_target_pairs={{0,1},{1,0},{2,3},{3,2},{4,5},{5,4},{6,7},{7,6},{8,9},{9,8},{10,11... | collective-permute-start | bytes 1572872 | tf_op jit(solution)/shard_map/ppermute | solution.py:355
  15.8 51.5 %collective-permute-start.6 = (bf16[4,256,256]{2,1,0:T(8,128)(2,1)}, bf16[4,256,256]{2,1,0:T(8,128)(2,1)}, u32[]{:S(2)}, u32[]{:S(2)}) collective-permute-start(bf16[4,256,256]{2,1,0:T(8,128)(2,1)} %get-tuple-element.52), channel_id=1, source_target_pairs={{0,1},{1,0},{2,3},{3,2},{4,5},{5,4},{6,7},{7,6},{8,9},{9,8},{10,11... | collective-permute-start | bytes 1572872 | tf_op jit(solution)/shard_map/ppermute | solution.py:355
  15.8 49.0 %collective-permute-start.7 = (bf16[4,256,256]{2,1,0:T(8,128)(2,1)}, bf16[4,256,256]{2,1,0:T(8,128)(2,1)}, u32[]{:S(2)}, u32[]{:S(2)}) collective-permute-start(bf16[4,256,256]{2,1,0:T(8,128)(2,1)} %get-tuple-element.53), channel_id=1, source_target_pairs={{0,1},{1,0},{2,3},{3,2},{4,5},{5,4},{6,7},{7,6},{8,9},{9,8},{10,11... | collective-permute-start | bytes 1572872 | tf_op jit(solution)/shard_map/ppermute | solution.py:355
  24.0 48.0 %collective-permute-start.2 = (f32[8,128,128]{2,1,0:T(8,128)}, f32[8,128,128]{2,1,0:T(8,128)}, u32[]{:S(2)}, u32[]{:S(2)}) collective-permute-start(f32[8,128,128]{2,1,0:T(8,128)} %convert_add_fusion), channel_id=1, source_target_pairs={{0,2},{2,0},{4,6},{6,4},{8,10},{10,8},{12,14},{14,12},{16,18},{18,... | collective-permute-start | bytes 1572872 | tf_op jit(solution)/shard_map/ppermute | solution.py:325
  72.0 8.5 %copy-start = (f32[8,128,128]{2,1,0:T(8,128)S(1)}, f32[8,128,128]{2,1,0:T(8,128)}, u32[]{:S(2)}) copy-start(f32[8,128,128]{2,1,0:T(8,128)} %get-tuple-element.73) | copy-start | bytes 1572868
  72.0 8.5 %collective-permute-start.9 = (f32[8,128,128]{2,1,0:T(8,128)}, f32[8,128,128]{2,1,0:T(8,128)S(1)}, u32[]{:S(2)}, u32[]{:S(2)}) collective-permute-start(f32[8,128,128]{2,1,0:T(8,128)} %get-tuple-element.74), channel_id=1, source_target_pairs={{0,2},{2,0},{4,6},{6,4},{8,10},{10,8},{12,14},{14,12},{16,18},{18,... | collective-permute-start | bytes 1572872 | tf_op jit(solution)/shard_map/ppermute | solution.py:325
  74.4 15.6 %all-to-all-start = ((bf16[8,128,128]{2,1,0:T(8,128)(2,1)}), bf16[8,128,128]{2,1,0:T(8,128)(2,1)S(1)}, u32[]{:S(2)}, u32[]{:S(2)}) async-start(bf16[8,128,128]{2,1,0:T(8,128)(2,1)} %get-tuple-element.93), calls=%async_computation | async-start | bytes 524288 | tf_op jit(solution)/shard_map/all_to_all | solution.py:309
  90.0 3.6 %copy-start.2 = (bf16[8,128,128]{2,1,0:T(8,128)(2,1)}, bf16[8,128,128]{2,1,0:T(8,128)(2,1)S(1)}, u32[]{:S(2)}) copy-start(bf16[8,128,128]{2,1,0:T(8,128)(2,1)S(1)} %all-to-all-done.part_ref) | copy-start | bytes 786436
  90.0 12.7 %all-to-all-start.2 = ((bf16[8,128,128]{2,1,0:T(8,128)(2,1)}), bf16[8,128,128]{2,1,0:T(8,128)(2,1)S(1)}, u32[]{:S(2)}, u32[]{:S(2)}) async-start(bf16[8,128,128]{2,1,0:T(8,128)(2,1)} %add_convert_fusion), calls=%async_computation.2 | async-start | bytes 524288 | tf_op jit(solution)/shard_map/all_to_all | solution.py:309
  102.7 5.6 %copy-start.1 = (bf16[8,128,128]{2,1,0:T(8,128)(2,1)}, bf16[8,128,128]{2,1,0:T(8,128)(2,1)S(1)}, u32[]{:S(2)}) copy-start(bf16[8,128,128]{2,1,0:T(8,128)(2,1)S(1)} %all-to-all-done.2.part_ref) | copy-start | bytes 786436
  102.7 12.4 %all-to-all-start.1 = ((bf16[8,128,128]{2,1,0:T(8,128)(2,1)}), bf16[8,128,128]{2,1,0:T(8,128)(2,1)}, u32[]{:S(2)}, u32[]{:S(2)}) async-start(bf16[8,128,128]{2,1,0:T(8,128)(2,1)} %running.2), calls=%async_computation.1 | async-start | bytes 524288 | tf_op jit(solution)/shard_map/all_to_all | solution.py:318
  106.8 20.0 %collective-permute-start.14 = (bf16[4,256,256]{2,1,0:T(8,128)(2,1)}, bf16[4,256,256]{2,1,0:T(8,128)(2,1)}, u32[]{:S(2)}, u32[]{:S(2)}) collective-permute-start(bf16[4,256,256]{2,1,0:T(8,128)(2,1)} %get-tuple-element.80), channel_id=1, source_target_pairs={{0,1},{1,0},{2,3},{3,2},{4,5},{5,4},{6,7},{7,6},{8,9},{9,8},{10,11... | collective-permute-start | bytes 1572872 | tf_op jit(solution)/shard_map/ppermute | solution.py:355
  108.3 18.5 %collective-permute-start.4 = (f32[8,128,128]{2,1,0:T(8,128)}, f32[8,128,128]{2,1,0:T(8,128)}, u32[]{:S(2)}, u32[]{:S(2)}) collective-permute-start(f32[8,128,128]{2,1,0:T(8,128)} %get-tuple-element.94), channel_id=1, source_target_pairs={{0,2},{2,0},{4,6},{6,4},{8,10},{10,8},{12,14},{14,12},{16,18},{18,... | collective-permute-start | bytes 1572872 | tf_op jit(solution)/shard_map/ppermute | solution.py:326
  115.1 23.9 %all-to-all-start.3 = ((bf16[8,128,128]{2,1,0:T(8,128)(2,1)}), bf16[8,128,128]{2,1,0:T(8,128)(2,1)}, u32[]{:S(2)}, u32[]{:S(2)}) async-start(bf16[8,128,128]{2,1,0:T(8,128)(2,1)} %running.3), calls=%async_computation.3 | async-start | bytes 524288 | tf_op jit(solution)/shard_map/all_to_all | solution.py:318
  119.3 23.7 %collective-permute-start.13 = (bf16[4,256,256]{2,1,0:T(8,128)(2,1)}, bf16[4,256,256]{2,1,0:T(8,128)(2,1)}, u32[]{:S(2)}, u32[]{:S(2)}) collective-permute-start(bf16[4,256,256]{2,1,0:T(8,128)(2,1)} %get-tuple-element.79), channel_id=1, source_target_pairs={{0,1},{1,0},{2,3},{3,2},{4,5},{5,4},{6,7},{7,6},{8,9},{9,8},{10,11... | collective-permute-start | bytes 1572872 | tf_op jit(solution)/shard_map/ppermute | solution.py:355
  120.9 42.9 %collective-permute-start = (bf16[4,256,256]{2,1,0:T(8,128)(2,1)}, bf16[4,256,256]{2,1,0:T(8,128)(2,1)}, u32[]{:S(2)}, u32[]{:S(2)}) collective-permute-start(bf16[4,256,256]{2,1,0:T(8,128)(2,1)} %get-tuple-element.48), channel_id=1, source_target_pairs={{0,1},{1,0},{2,3},{3,2},{4,5},{5,4},{6,7},{7,6},{8,9},{9,8},{10,11... | collective-permute-start | bytes 1572872 | tf_op jit(solution)/shard_map/ppermute | solution.py:355
  121.4 32.9 %collective-permute-start.12 = (bf16[4,256,256]{2,1,0:T(8,128)(2,1)}, bf16[4,256,256]{2,1,0:T(8,128)(2,1)}, u32[]{:S(2)}, u32[]{:S(2)}) collective-permute-start(bf16[4,256,256]{2,1,0:T(8,128)(2,1)} %get-tuple-element.78), channel_id=1, source_target_pairs={{0,1},{1,0},{2,3},{3,2},{4,5},{5,4},{6,7},{7,6},{8,9},{9,8},{10,11... | collective-permute-start | bytes 1572872 | tf_op jit(solution)/shard_map/ppermute | solution.py:355
  126.8 31.4 %collective-permute-start.11 = (f32[8,128,128]{2,1,0:T(8,128)}, f32[8,128,128]{2,1,0:T(8,128)}, u32[]{:S(2)}, u32[]{:S(2)}) collective-permute-start(f32[8,128,128]{2,1,0:T(8,128)} %get-tuple-element.73), channel_id=1, source_target_pairs={{0,2},{2,0},{4,6},{6,4},{8,10},{10,8},{12,14},{14,12},{16,18},{18,... | collective-permute-start | bytes 1572872 | tf_op jit(solution)/shard_map/ppermute | solution.py:326
  126.8 12.2 %collective-permute-start.3 = (bf16[8,128,128]{2,1,0:T(8,128)(2,1)}, bf16[8,128,128]{2,1,0:T(8,128)(2,1)}, u32[]{:S(2)}, u32[]{:S(2)}) collective-permute-start(bf16[8,128,128]{2,1,0:T(8,128)(2,1)} %all-to-all-done.1.refs_7_), channel_id=1, source_target_pairs={{0,2},{2,0},{4,6},{6,4},{8,10},{10,8},{12,14},{14,12},{16,18},{18,... | collective-permute-start | bytes 786440 | tf_op jit(solution)/shard_map/ppermute | solution.py:329
  139.0 19.1 %collective-permute-start.10 = (bf16[8,128,128]{2,1,0:T(8,128)(2,1)}, bf16[8,128,128]{2,1,0:T(8,128)(2,1)}, u32[]{:S(2)}, u32[]{:S(2)}) collective-permute-start(bf16[8,128,128]{2,1,0:T(8,128)(2,1)} %all-to-all-done.3.refs_0_), channel_id=1, source_target_pairs={{0,2},{2,0},{4,6},{6,4},{8,10},{10,8},{12,14},{14,12},{16,18},{18,... | collective-permute-start | bytes 786440 | tf_op jit(solution)/shard_map/ppermute | solution.py:329

commit v6 on v5

--- a/solution.py
+++ b/solution.py
@@ -116,11 +116,11 @@
         for r in rest[:peers]:
             kv = kv + mm(r[1, :, at], r[2, :, at], TN)
             qg = qg + mm(r[0, :, at], r[3, :, at], TN)
-        keep_ref[j] = jnp.where(first, kv, qg)
-        give_ref[j] = jnp.where(first, qg, kv)
-
-
-def split_states(cols, core, arrays, got, first, pairs, base, room, into):
+        keep_ref[j] = jnp.where(first, kv, qg).astype(keep_ref.dtype)
+        give_ref[j] = jnp.where(first, qg, kv).astype(give_ref.dtype)
+
+
+def split_states(cols, core, arrays, got, first, pairs, base, room, into, dtype):
     rows = arrays[0].shape[0]
     own = pl.BlockSpec((rows, PAIR), lambda i, c, d: (0, c[0] + first + i))
     there = pl.BlockSpec((4, rows, PAIR), lambda i, c, d: (0, 0, i))
@@ -135,7 +135,7 @@
             in_specs=[own] * 4 + [there] * len(got) + [pl.BlockSpec(memory_space=pl.ANY)] * len(shared),
             out_specs=[pl.BlockSpec((per, DK, DK), lambda i, c, d: (base + i, 0, 0))] * 2,
         ),
-        out_shape=[jax.ShapeDtypeStruct((per * room, DK, DK), F32)] * 2,
+        out_shape=[jax.ShapeDtypeStruct((per * room, DK, DK), dtype)] * 2,
         input_output_aliases={6 + len(got) + j: j for j in range(len(shared))},
         cost_estimate=cost(4 * tokens * DK * PAIR * pairs, 8 * tokens * pairs * PAIR),
         compiler_params=pltpu.CompilerParams(vmem_limit_bytes=VMEM_LIMIT),
@@ -184,7 +184,7 @@
 
 def prefix_suffix(core_ref, mine_ref, other_ref, theirs_ref, j):
     first, mine = core_ref[0] == 0, mine_ref[j]
-    other = (other_ref[j].astype(F32) + theirs_ref[j]).astype(BF16)
+    other = (other_ref[j].astype(F32) + theirs_ref[j].astype(F32)).astype(BF16)
     return jnp.where(first, mine, other), jnp.where(first, other, mine)
 
 
@@ -322,7 +322,7 @@
 def scan_chips(keep, give):
     count = lax.axis_size("seq")
     swap = [(i, i ^ 1) for i in range(count)]
-    chip = keep + lax.ppermute(give, "seq", swap)
+    chip = keep.astype(F32) + lax.ppermute(give, "seq", swap).astype(F32)
     theirs = lax.ppermute(keep, "seq", swap)
     groups = [list(range(core, count, 2)) for core in (0, 1)]
     mine = deal_and_sum(chip.astype(BF16), lax.axis_index("seq") % 2 == 0, groups)
@@ -344,7 +344,7 @@
     early = pairs_here - late
     sizes = [1] * early
     split = len(sizes)
-    sizes += [n for n in (late - 3 * (late // 4), late // 4, late // 4, late // 4) if n]
+    sizes += [n for n in (late - 2 * (late // 4), late // 4, late // 4) if n]
     firsts = [sum(sizes[:i]) for i in range(len(sizes))]
     shifts = range(1, peers)
     cols = [jnp.reshape((place + s) % peers * pairs_here, (1,)).astype(jnp.int32) for s in range(peers)]
@@ -362,14 +362,14 @@
     for c, packed in enumerate(pack(cols, peers, arrays, sizes[0], sizes[1:]), 1):
         got.append(move(packed))
     core = (lax.axis_index("seq") % 2).astype(jnp.int32).reshape(1)
-    keep, give = split_states(cols, core, arrays, [], early, late, 0, late, None)
+    keep, give = split_states(cols, core, arrays, [], early, late, 0, late, None, F32)
     for piece in late_got:
         first, second = jnp.where(core[0] == 0, piece[0], piece[1]), jnp.where(core[0] == 0, piece[1], piece[0])
         keep, give = keep + first.astype(F32), give + second.astype(F32)
     late_sums = scan_chips(keep, give)
     own = parts = None
     for c in range(split):
-        own = split_states(cols, core, arrays, got[c], firsts[c], sizes[c], firsts[c], early, own)
+        own = split_states(cols, core, arrays, got[c], firsts[c], sizes[c], firsts[c], early, own, BF16)
     for c in range(split):
         parts = outputs(
             within_kernel, cols, core, src, arrays, got[c], None, firsts[c], sizes[c], firsts[c], early, scale, parts

time: 169 us -> 160 us (0.947)
  waiting for transfers between devices: 67.1 us -> 62.1 us
  Pallas kernels: 63.7 us -> 61.7 us
    ppermute x9 -> x8, waiting for transfers between devices: 45.9 us -> 40.9 us  [move(): lax.ppermute(value, 'head', [(i, (i + s) % peers) for i in range(peers)])]
    pallas_call x8 -> x7, Pallas kernels: 31 us -> 29.3 us  [outputs(): pl.pallas_call(functools.partial(kernel, len(got), int(into is not None),...]
    ppermute x9 -> x8, starting transfers between devices: 12.3 us -> 10.7 us  [move(): lax.ppermute(value, 'head', [(i, (i + s) % peers) for i in range(peers)])]
  transfers between devices with their start and end apart: 19 -> 18, of which waited for: 6 -> 4; matrix products, arithmetic and copies ran while one was open for 3% -> 3% of each run, Pallas kernels for 33% -> 34%
where the time goes in v6:
time: 160 us; the launch traced here: 159 us
  waiting for transfers between devices  62.1 us (39%)
  Pallas kernels  61.7 us (39%)
  starting transfers between devices  29.4 us (18%)
  other arithmetic  5.24 us (3%)
    ppermute x8, waiting for transfers between devices, move(): lax.ppermute(value, 'head', [(i, (i + s) % peers) for i in range(peers)])  40.9 us
    pallas_call x7, Pallas kernels, outputs(): pl.pallas_call(functools.partial(kernel, len(got), int(into is not None),...  29.3 us
    all_to_all x2, waiting for transfers between devices, deal_and_sum(): lax.all_to_all(own.reshape(count, -1, DK), 'seq', 0, 0, tiled=True, axis_...  14.6 us
    pallas_call x5, Pallas kernels, split_states(): pl.pallas_call(functools.partial(split_kernel, len(got)), grid_spec=pltpu...  13.5 us
    ppermute x8, starting transfers between devices, move(): lax.ppermute(value, 'head', [(i, (i + s) % peers) for i in range(peers)])  10.7 us
    all_to_all x2, starting transfers between devices, deal_and_sum(): lax.all_to_all(own.reshape(count, -1, DK), 'seq', 0, 0, tiled=True, axis_...  9.67 us
    all_to_all x2, starting transfers between devices, deal_and_sum(): lax.all_to_all(mine, 'seq', 0, 0, tiled=True, axis_index_groups=groups)  8.3 us
    all_to_all x2, waiting for transfers between devices, deal_and_sum(): lax.all_to_all(mine, 'seq', 0, 0, tiled=True, axis_index_groups=groups)  6.53 us
  transfers between devices with their start and end apart: 18, of which 4 were waited for; matrix products, arithmetic and copies ran while one was open for 3% of the time, Pallas kernels for 34%

profile of v6, /device:TPU:0, one launch (start us, length us, event | category | flops | bytes accessed | tf_op | source)
XLA Modules:
  0.0 159.2 jit_solution(15061571847684907519)
XLA Ops:
  0.6 4.1 %states.1 = bf16[2,8,128,128]{3,2,1,0:T(8,128)(2,1)} custom-call(s32[1]{0:T(128)} %bitcast.4.refs_0_.col_ref, bf16[256,4096]{1,0:T(8,128)(2,1)} %refs_2_.17, bf16[256,4096]{1,0:T(8,128)(2,1)} %refs_3_.17, bf16[256,4096]{1,0:T(8,128)(2,1)} %refs_4_.17, bf16[256,4096]{1,0:T(8,128)(2,1)} %refs_5_.13), custom_call_target="tpu_custom_call" | custom-call | flops 134217728 | bytes 2097152 | tf_op jit(solution)/shard_map/states/pallas_call | solution.py:93
  4.7 3.0 %collective-permute-start.1 = (bf16[2,8,128,128]{3,2,1,0:T(8,128)(2,1)}, bf16[2,8,128,128]{3,2,1,0:T(8,128)(2,1)}, u32[]{:S(2)}, u32[]{:S(2)}) collective-permute-start(bf16[2,8,128,128]{3,2,1,0:T(8,128)(2,1)} %states.1), channel_id=1, source_target_pairs={{0,1},{1,0},{2,3},{3,2},{4,5},{5,4},{6,7},{7,6},{8,9},{9,8},{10,11... | collective-permute-start | bytes 1572872 | tf_op jit(solution)/shard_map/ppermute | solution.py:355
  7.7 4.0 %pack.2 = (bf16[4,256,256]{2,1,0:T(8,128)(2,1)}, bf16[4,256,256]{2,1,0:T(8,128)(2,1)}, bf16[4,256,256]{2,1,0:T(8,128)(2,1)}, bf16[4,256,512]{2,1,0:T(8,128)(2,1)...) custom-call(s32[1]{0:T(128)} %bitcast.4.refs_0_.col_ref, bf16[256,4096]{1,0:T(8,128)(2,1)} %refs_2_.17, ...), custom_call_target="tpu_custom_call" | custom-call | bytes 7340032 | tf_op jit(solution)/shard_map/pack/pallas_call | solution.py:60
  11.8 2.0 %collective-permute-start.6 = (bf16[4,256,256]{2,1,0:T(8,128)(2,1)}, bf16[4,256,256]{2,1,0:T(8,128)(2,1)}, u32[]{:S(2)}, u32[]{:S(2)}) collective-permute-start(bf16[4,256,256]{2,1,0:T(8,128)(2,1)} %get-tuple-element.48), channel_id=1, source_target_pairs={{0,1},{1,0},{2,3},{3,2},{4,5},{5,4},{6,7},{7,6},{8,9},{9,8},{10,11... | collective-permute-start | bytes 1572872 | tf_op jit(solution)/shard_map/ppermute | solution.py:355
  13.9 1.8 %pack.3 = bf16[4,256,256]{2,1,0:T(8,128)(2,1)} custom-call(s32[1]{0:T(128)} %bitcast.4.refs_0_.col_ref, bf16[256,4096]{1,0:T(8,128)(2,1)} %refs_2_.17, bf16[256,4096]{1,0:T(8,128)(2,1)} %refs_3_.17, bf16[256,4096]{1,0:T(8,128)(2,1)} %refs_4_.17, bf16[256,4096]{1,0:T(8,128)(2,1)} %refs_5_.13), custom_call_target="tpu_custom_call" | custom-call | bytes 1048576 | tf_op jit(solution)/shard_map/pack/pallas_call | solution.py:60
  15.7 2.0 %collective-permute-start.8 = (bf16[4,256,256]{2,1,0:T(8,128)(2,1)}, bf16[4,256,256]{2,1,0:T(8,128)(2,1)}, u32[]{:S(2)}, u32[]{:S(2)}) collective-permute-start(bf16[4,256,256]{2,1,0:T(8,128)(2,1)} %pack.3), channel_id=1, source_target_pairs={{0,1},{1,0},{2,3},{3,2},{4,5},{5,4},{6,7},{7,6},{8,9},{9,8},{10,11... | collective-permute-start | bytes 1572872 | tf_op jit(solution)/shard_map/ppermute | solution.py:355
  17.7 4.2 %split_states.5 = (f32[8,128,128]{2,1,0:T(8,128)}, f32[8,128,128]{2,1,0:T(8,128)}) custom-call(s32[1]{0:T(128)} %bitcast.col_ref, s32[1]{0:T(128)} %bitcast.1.core_ref, bf16[256,4096]{1,0:T(8,128)(2,1)} %refs_2_.17, bf16[256,4096]{1,0:T(8,128)(2,1)} %refs_3_.17, bf16[256,4096]{1,0:T(8,128)(2,1)} %refs_4_.17, bf16[256,4096]{1,0:T(8,128)(2,1)} %refs_5_.13), custom_call_target="tpu_custom_call" | custom-call | flops 134217728 | bytes 2097152 | tf_op jit(solution)/shard_map/split_states/pallas_call | solution.py:130
  21.9 2.1 %convert_add_fusion = f32[8,128,128]{2,1,0:T(8,128)} fusion(f32[8,128,128]{2,1,0:T(8,128)} %get-tuple-element.46, pred[]{:T(512)S(6)} %eq.14, bf16[2,8,128,128]{3,2,1,0:T(8,128)(2,1)} %collective-permute-done.1), kind=kLoop, calls=%fused_computation | loop fusion | flops 393216 | bytes 1572865 | tf_op jit(solution)/shard_map/add | solution.py:368
  23.9 40.9 %collective-permute-done.8.refs_6_.rest_0_ = bf16[4,256,256]{2,1,0:T(8,128)(2,1)} collective-permute-done((bf16[4,256,256]{2,1,0:T(8,128)(2,1)}, bf16[4,256,256]{2,1,0:T(8,128)(2,1)}, u32[]{:S(2)}, u32[]{:S(2)}) %collective-permute-start.8) | collective-permute-done | bytes 524320 | tf_op jit(solution)/shard_map/ppermute | solution.py:355
  64.9 2.3 %split_states.6 = (bf16[8,128,128]{2,1,0:T(8,128)(2,1)}, bf16[8,128,128]{2,1,0:T(8,128)(2,1)}) custom-call(s32[1]{0:T(128)} %bitcast.col_ref, s32[1]{0:T(128)} %bitcast.1.core_ref, bf16[256,4096]{1,0:T(8,128)(2,1)} %refs_2_.17, bf16[256,4096]{1,0:T(8,128)(2,1)} %refs_3_.17, bf16[256,4096]{1,0:T(8,128)(2,1)} %refs_4_.17, bf16[256,4096]{1,0:T(8,128)(2,1)} %refs_5_.13, ...), custom_call_target="tpu_custom_call" | custom-call | flops 67108864 | bytes 1048576 | tf_op jit(solution)/shard_map/split_states/pallas_call | solution.py:130
  67.2 2.3 %split_states.7 = (bf16[8,128,128]{2,1,0:T(8,128)(2,1)}, bf16[8,128,128]{2,1,0:T(8,128)(2,1)}) custom-call(s32[1]{0:T(128)} %bitcast.col_ref, s32[1]{0:T(128)} %bitcast.1.core_ref, bf16[256,4096]{1,0:T(8,128)(2,1)} %refs_2_.17, bf16[256,4096]{1,0:T(8,128)(2,1)} %refs_3_.17, ...), custom_call_target="tpu_custom_call", output_to_operand_aliasing={{0}: (7, {}), {1}: (8, {})} | custom-call | flops 67108864 | bytes 1048576 | tf_op jit(solution)/shard_map/split_states/pallas_call | solution.py:130
  69.6 2.3 %split_states.8 = (bf16[8,128,128]{2,1,0:T(8,128)(2,1)}, bf16[8,128,128]{2,1,0:T(8,128)(2,1)}) custom-call(s32[1]{0:T(128)} %bitcast.col_ref, s32[1]{0:T(128)} %bitcast.1.core_ref, bf16[256,4096]{1,0:T(8,128)(2,1)} %refs_2_.17, bf16[256,4096]{1,0:T(8,128)(2,1)} %refs_3_.17, ...), custom_call_target="tpu_custom_call", output_to_operand_aliasing={{0}: (7, {}), {1}: (8, {})} | custom-call | flops 67108864 | bytes 1048576 | tf_op jit(solution)/shard_map/split_states/pallas_call | solution.py:130
  71.9 2.3 %split_states.9 = (bf16[8,128,128]{2,1,0:T(8,128)(2,1)}, bf16[8,128,128]{2,1,0:T(8,128)(2,1)}) custom-call(s32[1]{0:T(128)} %bitcast.col_ref, s32[1]{0:T(128)} %bitcast.1.core_ref, bf16[256,4096]{1,0:T(8,128)(2,1)} %refs_2_.17, bf16[256,4096]{1,0:T(8,128)(2,1)} %refs_3_.17, ...), custom_call_target="tpu_custom_call", output_to_operand_aliasing={{0}: (7, {}), {1}: (8, {})} | custom-call | flops 67108864 | bytes 1048576 | tf_op jit(solution)/shard_map/split_states/pallas_call | solution.py:130
  74.2 2.4 %add_convert_fusion.1 = (bf16[8,128,128]{2,1,0:T(8,128)(2,1)}, f32[8,128,128]{2,1,0:T(8,128)}) fusion(f32[8,128,128]{2,1,0:T(8,128)} %collective-permute-done.2, f32[8,128,128]{2,1,0:T(8,128)} %get-tuple-element.45, bf16[2,8,128,128]{3,2,1,0:T(8,128)(2,1)} %collective-permute-done.1, pred[]{:T(512)S(6)} %eq.14), kind=kLoop, calls=%fused_computation.3 | loop fusion | flops 655360 | bytes 2359297 | tf_op jit(solution)/shard_map/convert_element_type | solution.py:328
  76.6 6.1 %all-to-all-start = ((bf16[8,128,128]{2,1,0:T(8,128)(2,1)}), bf16[8,128,128]{2,1,0:T(8,128)(2,1)S(1)}, u32[]{:S(2)}, u32[]{:S(2)}) async-start(bf16[8,128,128]{2,1,0:T(8,128)(2,1)} %get-tuple-element.85), calls=%async_computation | async-start | bytes 524288 | tf_op jit(solution)/shard_map/all_to_all | solution.py:309
  83.5 8.7 %all-to-all-done.part_ref = bf16[8,128,128]{2,1,0:T(8,128)(2,1)S(1)} async-done(((bf16[8,128,128]{2,1,0:T(8,128)(2,1)}), bf16[8,128,128]{2,1,0:T(8,128)(2,1)S(1)}, u32[]{:S(2)}, u32[]{:S(2)}) %all-to-all-start) | async-done | bytes 262176 | tf_op jit(solution)/shard_map/all_to_all | solution.py:309
  92.2 3.6 %all-to-all-start.2 = ((bf16[8,128,128]{2,1,0:T(8,128)(2,1)}), bf16[8,128,128]{2,1,0:T(8,128)(2,1)S(1)}, u32[]{:S(2)}, u32[]{:S(2)}) async-start(bf16[8,128,128]{2,1,0:T(8,128)(2,1)} %add_convert_fusion), calls=%async_computation.2 | async-start | bytes 524288 | tf_op jit(solution)/shard_map/all_to_all | solution.py:309
  97.3 1.7 %running.2 = bf16[8,128,128]{2,1,0:T(8,128)(2,1)} custom-call(s32[1]{0:T(128)} %bitcast.5.up_ref, bf16[8,128,128]{2,1,0:T(8,128)(2,1)} %copy-done.1), custom_call_target="tpu_custom_call" | custom-call | flops 131072 | bytes 524288 | tf_op jit(solution)/shard_map/running/pallas_call | solution.py:310
  99.0 5.9 %all-to-all-done.2.part_ref = bf16[8,128,128]{2,1,0:T(8,128)(2,1)S(1)} async-done(((bf16[8,128,128]{2,1,0:T(8,128)(2,1)}), bf16[8,128,128]{2,1,0:T(8,128)(2,1)S(1)}, u32[]{:S(2)}, u32[]{:S(2)}) %all-to-all-start.2) | async-done | bytes 262176 | tf_op jit(solution)/shard_map/all_to_all | solution.py:309
  104.9 4.1 %all-to-all-start.1 = ((bf16[8,128,128]{2,1,0:T(8,128)(2,1)}), bf16[8,128,128]{2,1,0:T(8,128)(2,1)}, u32[]{:S(2)}, u32[]{:S(2)}) async-start(bf16[8,128,128]{2,1,0:T(8,128)(2,1)} %running.2), calls=%async_computation.1 | async-start | bytes 524288 | tf_op jit(solution)/shard_map/all_to_all | solution.py:318
  109.1 1.7 %running.3 = bf16[8,128,128]{2,1,0:T(8,128)(2,1)} custom-call(s32[1]{0:T(128)} %bitcast.5.up_ref, bf16[8,128,128]{2,1,0:T(8,128)(2,1)} %copy-done.2), custom_call_target="tpu_custom_call" | custom-call | flops 131072 | bytes 524288 | tf_op jit(solution)/shard_map/running/pallas_call | solution.py:310
  110.8 6.5 %all-to-all-done.1.refs_7_ = bf16[8,128,128]{2,1,0:T(8,128)(2,1)} async-done(((bf16[8,128,128]{2,1,0:T(8,128)(2,1)}), bf16[8,128,128]{2,1,0:T(8,128)(2,1)}, u32[]{:S(2)}, u32[]{:S(2)}) %all-to-all-start.1) | async-done | bytes 262176 | tf_op jit(solution)/shard_map/all_to_all | solution.py:318
  117.3 4.2 %all-to-all-start.3 = ((bf16[8,128,128]{2,1,0:T(8,128)(2,1)}), bf16[8,128,128]{2,1,0:T(8,128)(2,1)}, u32[]{:S(2)}, u32[]{:S(2)}) async-start(bf16[8,128,128]{2,1,0:T(8,128)(2,1)} %running.3), calls=%async_computation.3 | async-start | bytes 524288 | tf_op jit(solution)/shard_map/all_to_all | solution.py:318
  121.6 1.6 collective-permute-start
  123.7 4.0 %shard_map.67 = (bf16[512,1024]{1,0:T(8,128)(2,1)}, bf16[512,1024]{1,0:T(8,128)(2,1)}, bf16[512,1024]{1,0:T(8,128)(2,1)}, bf16[3,512,1024]{2,1,0:T(8,128)(2,1)}) custom-call(s32[1]{0:T(128)} %bitcast.col_ref, s32[1]{0:T(128)} %bitcast.1.core_ref, s32[1]{0:T(128)} %bitcast.2.refs_0_, s32[1]{0:T(128)} %bitcast.3.refs_1_, bf16[256,4096]{1,0:T(8,128)(2,1)} %refs_2_.17, ...), custom_call_target="tpu_custom_call" | custom-call | flops 939524096 | bytes 1835008 | tf_op jit(solution)/shard_map/pallas_call | solution.py:248
  127.6 3.9 %shard_map.68 = (bf16[512,1024]{1,0:T(8,128)(2,1)}, bf16[512,1024]{1,0:T(8,128)(2,1)}, bf16[512,1024]{1,0:T(8,128)(2,1)}, bf16[3,512,1024]{2,1,0:T(8,128)(2,1)}) custom-call(s32[1]{0:T(128)} %bitcast.col_ref, s32[1]{0:T(128)} %bitcast.1.core_ref, s32[1]{0:T(128)} %bitcast.2.refs_0_, ...), custom_call_target="tpu_custom_call", output_to_operand_aliasing={{0}: (9, {}), {1}: (10, {}), {2}: (11, {}), {3}: (12, {})} | custom-call | flops 939524096 | bytes 1835008 | tf_op jit(solution)/shard_map/pallas_call | solution.py:248
  131.5 3.9 %shard_map.69 = (bf16[512,1024]{1,0:T(8,128)(2,1)}, bf16[512,1024]{1,0:T(8,128)(2,1)}, bf16[512,1024]{1,0:T(8,128)(2,1)}, bf16[3,512,1024]{2,1,0:T(8,128)(2,1)}) custom-call(s32[1]{0:T(128)} %bitcast.col_ref, s32[1]{0:T(128)} %bitcast.1.core_ref, s32[1]{0:T(128)} %bitcast.2.refs_0_, ...), custom_call_target="tpu_custom_call", output_to_operand_aliasing={{0}: (9, {}), {1}: (10, {}), {2}: (11, {}), {3}: (12, {})} | custom-call | flops 939524096 | bytes 1835008 | tf_op jit(solution)/shard_map/pallas_call | solution.py:248
  135.5 3.9 %shard_map.70 = (bf16[512,1024]{1,0:T(8,128)(2,1)}, bf16[512,1024]{1,0:T(8,128)(2,1)}, bf16[512,1024]{1,0:T(8,128)(2,1)}, bf16[3,512,1024]{2,1,0:T(8,128)(2,1)}) custom-call(s32[1]{0:T(128)} %bitcast.col_ref, s32[1]{0:T(128)} %bitcast.1.core_ref, s32[1]{0:T(128)} %bitcast.2.refs_0_, ...), custom_call_target="tpu_custom_call", output_to_operand_aliasing={{0}: (9, {}), {1}: (10, {}), {2}: (11, {}), {3}: (12, {})} | custom-call | flops 939524096 | bytes 1835008 | tf_op jit(solution)/shard_map/pallas_call | solution.py:248
  140.1 5.8 %shard_map.71 = (bf16[512,2048]{1,0:T(8,128)(2,1)}, bf16[512,2048]{1,0:T(8,128)(2,1)}, bf16[512,2048]{1,0:T(8,128)(2,1)}) custom-call(s32[1]{0:T(128)} %bitcast.col_ref, s32[1]{0:T(128)} %bitcast.1.core_ref, s32[1]{0:T(128)} %bitcast.2.refs_0_, s32[1]{0:T(128)} %bitcast.3.refs_1_, bf16[256,4096]{1,0:T(8,128)(2,1)} %refs_2_.17, bf16[256,4096]{1,0:T(8,128)(2,1)} %refs_3_.17, ...), custom_call_target="tpu_custom_call" | custom-call | flops 1879048192 | bytes 3670016 | tf_op jit(solution)/shard_map/pallas_call | solution.py:248
  145.8 3.9 %shard_map.72 = (bf16[512,2048]{1,0:T(8,128)(2,1)}, bf16[512,2048]{1,0:T(8,128)(2,1)}, bf16[512,2048]{1,0:T(8,128)(2,1)}) custom-call(s32[1]{0:T(128)} %bitcast.col_ref, s32[1]{0:T(128)} %bitcast.1.core_ref, s32[1]{0:T(128)} %bitcast.2.refs_0_, s32[1]{0:T(128)} %bitcast.3.refs_1_, ...), custom_call_target="tpu_custom_call", output_to_operand_aliasing={{0}: (12, {}), {1}: (13, {}), {2}: (14, {})} | custom-call | flops 939524096 | bytes 1835008 | tf_op jit(solution)/shard_map/pallas_call | solution.py:248
  149.7 5.6 %across.1 = (bf16[512,2048]{1,0:T(8,128)(2,1)}, bf16[512,2048]{1,0:T(8,128)(2,1)}, bf16[512,2048]{1,0:T(8,128)(2,1)}) custom-call(s32[1]{0:T(128)} %bitcast.1.core_ref, bf16[3,512,1024]{2,1,0:T(8,128)(2,1)} %get-tuple-element.62.rows_ref, bf16[8,128,128]{2,1,0:T(8,128)(2,1)} %all-to-all-done.3.refs_0_, ...), custom_call_target="tpu_custom_call", output_to_operand_aliasing={{0}: (8, {}), {1}: (9, {}), {2}: (10, {})} | custom-call | flops 402653184 | bytes 12582912 | tf_op jit(solution)/shard_map/across/pallas_call | solution.py:268
  155.3 3.9 %shard_map.73 = (bf16[512,2048]{1,0:T(8,128)(2,1)}, bf16[512,2048]{1,0:T(8,128)(2,1)}, bf16[512,2048]{1,0:T(8,128)(2,1)}) custom-call(s32[1]{0:T(128)} %bitcast.col_ref, s32[1]{0:T(128)} %bitcast.1.core_ref, s32[1]{0:T(128)} %bitcast.2.refs_0_, s32[1]{0:T(128)} %bitcast.3.refs_1_, ...), custom_call_target="tpu_custom_call", output_to_operand_aliasing={{0}: (12, {}), {1}: (13, {}), {2}: (14, {})} | custom-call | flops 939524096 | bytes 1835008 | tf_op jit(solution)/shard_map/pallas_call | solution.py:248
  (31 shorter events, 3.7 us)
Async XLA Ops:
  4.7 17.1 %collective-permute-start.1 = (bf16[2,8,128,128]{3,2,1,0:T(8,128)(2,1)}, bf16[2,8,128,128]{3,2,1,0:T(8,128)(2,1)}, u32[]{:S(2)}, u32[]{:S(2)}) collective-permute-start(bf16[2,8,128,128]{3,2,1,0:T(8,128)(2,1)} %states.1), channel_id=1, source_target_pairs={{0,1},{1,0},{2,3},{3,2},{4,5},{5,4},{6,7},{7,6},{8,9},{9,8},{10,11... | collective-permute-start | bytes 1572872 | tf_op jit(solution)/shard_map/ppermute | solution.py:355
  11.7 60.2 %collective-permute-start.5 = (bf16[4,256,256]{2,1,0:T(8,128)(2,1)}, bf16[4,256,256]{2,1,0:T(8,128)(2,1)}, u32[]{:S(2)}, u32[]{:S(2)}) collective-permute-start(bf16[4,256,256]{2,1,0:T(8,128)(2,1)} %get-tuple-element.47), channel_id=1, source_target_pairs={{0,1},{1,0},{2,3},{3,2},{4,5},{5,4},{6,7},{7,6},{8,9},{9,8},{10,11... | collective-permute-start | bytes 1572872 | tf_op jit(solution)/shard_map/ppermute | solution.py:355
  11.8 57.8 %collective-permute-start.6 = (bf16[4,256,256]{2,1,0:T(8,128)(2,1)}, bf16[4,256,256]{2,1,0:T(8,128)(2,1)}, u32[]{:S(2)}, u32[]{:S(2)}) collective-permute-start(bf16[4,256,256]{2,1,0:T(8,128)(2,1)} %get-tuple-element.48), channel_id=1, source_target_pairs={{0,1},{1,0},{2,3},{3,2},{4,5},{5,4},{6,7},{7,6},{8,9},{9,8},{10,11... | collective-permute-start | bytes 1572872 | tf_op jit(solution)/shard_map/ppermute | solution.py:355
  13.8 53.4 %collective-permute-start.7 = (bf16[4,256,256]{2,1,0:T(8,128)(2,1)}, bf16[4,256,256]{2,1,0:T(8,128)(2,1)}, u32[]{:S(2)}, u32[]{:S(2)}) collective-permute-start(bf16[4,256,256]{2,1,0:T(8,128)(2,1)} %get-tuple-element.49), channel_id=1, source_target_pairs={{0,1},{1,0},{2,3},{3,2},{4,5},{5,4},{6,7},{7,6},{8,9},{9,8},{10,11... | collective-permute-start | bytes 1572872 | tf_op jit(solution)/shard_map/ppermute | solution.py:355
  15.7 49.2 %collective-permute-start.8 = (bf16[4,256,256]{2,1,0:T(8,128)(2,1)}, bf16[4,256,256]{2,1,0:T(8,128)(2,1)}, u32[]{:S(2)}, u32[]{:S(2)}) collective-permute-start(bf16[4,256,256]{2,1,0:T(8,128)(2,1)} %pack.3), channel_id=1, source_target_pairs={{0,1},{1,0},{2,3},{3,2},{4,5},{5,4},{6,7},{7,6},{8,9},{9,8},{10,11... | collective-permute-start | bytes 1572872 | tf_op jit(solution)/shard_map/ppermute | solution.py:355
  23.9 50.3 %collective-permute-start.2 = (f32[8,128,128]{2,1,0:T(8,128)}, f32[8,128,128]{2,1,0:T(8,128)}, u32[]{:S(2)}, u32[]{:S(2)}) collective-permute-start(f32[8,128,128]{2,1,0:T(8,128)} %convert_add_fusion), channel_id=1, source_target_pairs={{0,2},{2,0},{4,6},{6,4},{8,10},{10,8},{12,14},{14,12},{16,18},{18,... | collective-permute-start | bytes 1572872 | tf_op jit(solution)/shard_map/ppermute | solution.py:325
  74.2 8.5 %copy-start = (bf16[8,128,128]{2,1,0:T(8,128)(2,1)S(1)}, bf16[8,128,128]{2,1,0:T(8,128)(2,1)}, u32[]{:S(2)}) copy-start(bf16[8,128,128]{2,1,0:T(8,128)(2,1)} %get-tuple-element.69) | copy-start | bytes 786436
  74.2 8.5 %collective-permute-start.9 = (bf16[8,128,128]{2,1,0:T(8,128)(2,1)}, bf16[8,128,128]{2,1,0:T(8,128)(2,1)S(1)}, u32[]{:S(2)}, u32[]{:S(2)}) collective-permute-start(bf16[8,128,128]{2,1,0:T(8,128)(2,1)} %get-tuple-element.70), channel_id=1, source_target_pairs={{0,2},{2,0},{4,6},{6,4},{8,10},{10,8},{12,14},{14,12},{16,18},{18,... | collective-permute-start | bytes 786440 | tf_op jit(solution)/shard_map/ppermute | solution.py:325
  76.6 15.6 %all-to-all-start = ((bf16[8,128,128]{2,1,0:T(8,128)(2,1)}), bf16[8,128,128]{2,1,0:T(8,128)(2,1)S(1)}, u32[]{:S(2)}, u32[]{:S(2)}) async-start(bf16[8,128,128]{2,1,0:T(8,128)(2,1)} %get-tuple-element.85), calls=%async_computation | async-start | bytes 524288 | tf_op jit(solution)/shard_map/all_to_all | solution.py:309
  92.2 5.1 %copy-start.1 = (bf16[8,128,128]{2,1,0:T(8,128)(2,1)}, bf16[8,128,128]{2,1,0:T(8,128)(2,1)S(1)}, u32[]{:S(2)}) copy-start(bf16[8,128,128]{2,1,0:T(8,128)(2,1)S(1)} %all-to-all-done.part_ref) | copy-start | bytes 786436
  92.2 12.7 %all-to-all-start.2 = ((bf16[8,128,128]{2,1,0:T(8,128)(2,1)}), bf16[8,128,128]{2,1,0:T(8,128)(2,1)S(1)}, u32[]{:S(2)}, u32[]{:S(2)}) async-start(bf16[8,128,128]{2,1,0:T(8,128)(2,1)} %add_convert_fusion), calls=%async_computation.2 | async-start | bytes 524288 | tf_op jit(solution)/shard_map/all_to_all | solution.py:309
  95.8 43.6 %collective-permute-start.13 = (bf16[4,256,512]{2,1,0:T(8,128)(2,1)}, bf16[4,256,512]{2,1,0:T(8,128)(2,1)}, u32[]{:S(2)}, u32[]{:S(2)}) collective-permute-start(bf16[4,256,512]{2,1,0:T(8,128)(2,1)} %get-tuple-element.75), channel_id=1, source_target_pairs={{0,1},{1,0},{2,3},{3,2},{4,5},{5,4},{6,7},{7,6},{8,9},{9,8},{10,11... | collective-permute-start | bytes 3145736 | tf_op jit(solution)/shard_map/ppermute | solution.py:355
  104.9 4.1 %copy-start.2 = (bf16[8,128,128]{2,1,0:T(8,128)(2,1)}, bf16[8,128,128]{2,1,0:T(8,128)(2,1)S(1)}, u32[]{:S(2)}) copy-start(bf16[8,128,128]{2,1,0:T(8,128)(2,1)S(1)} %all-to-all-done.2.part_ref) | copy-start | bytes 786436
  104.9 12.4 %all-to-all-start.1 = ((bf16[8,128,128]{2,1,0:T(8,128)(2,1)}), bf16[8,128,128]{2,1,0:T(8,128)(2,1)}, u32[]{:S(2)}, u32[]{:S(2)}) async-start(bf16[8,128,128]{2,1,0:T(8,128)(2,1)} %running.2), calls=%async_computation.1 | async-start | bytes 524288 | tf_op jit(solution)/shard_map/all_to_all | solution.py:318
  109.0 31.0 %collective-permute-start.4 = (f32[8,128,128]{2,1,0:T(8,128)}, f32[8,128,128]{2,1,0:T(8,128)}, u32[]{:S(2)}, u32[]{:S(2)}) collective-permute-start(f32[8,128,128]{2,1,0:T(8,128)} %get-tuple-element.86), channel_id=1, source_target_pairs={{0,2},{2,0},{4,6},{6,4},{8,10},{10,8},{12,14},{14,12},{16,18},{18,... | collective-permute-start | bytes 1572872 | tf_op jit(solution)/shard_map/ppermute | solution.py:326
  117.3 22.6 %all-to-all-start.3 = ((bf16[8,128,128]{2,1,0:T(8,128)(2,1)}), bf16[8,128,128]{2,1,0:T(8,128)(2,1)}, u32[]{:S(2)}, u32[]{:S(2)}) async-start(bf16[8,128,128]{2,1,0:T(8,128)(2,1)} %running.3), calls=%async_computation.3 | async-start | bytes 524288 | tf_op jit(solution)/shard_map/all_to_all | solution.py:318
  121.6 33.8 %collective-permute-start = (bf16[4,256,256]{2,1,0:T(8,128)(2,1)}, bf16[4,256,256]{2,1,0:T(8,128)(2,1)}, u32[]{:S(2)}, u32[]{:S(2)}) collective-permute-start(bf16[4,256,256]{2,1,0:T(8,128)(2,1)} %get-tuple-element.44), channel_id=1, source_target_pairs={{0,1},{1,0},{2,3},{3,2},{4,5},{5,4},{6,7},{7,6},{8,9},{9,8},{10,11... | collective-permute-start | bytes 1572872 | tf_op jit(solution)/shard_map/ppermute | solution.py:355
  123.1 22.7 %collective-permute-start.12 = (bf16[4,256,256]{2,1,0:T(8,128)(2,1)}, bf16[4,256,256]{2,1,0:T(8,128)(2,1)}, u32[]{:S(2)}, u32[]{:S(2)}) collective-permute-start(bf16[4,256,256]{2,1,0:T(8,128)(2,1)} %get-tuple-element.74), channel_id=1, source_target_pairs={{0,1},{1,0},{2,3},{3,2},{4,5},{5,4},{6,7},{7,6},{8,9},{9,8},{10,11... | collective-permute-start | bytes 1572872 | tf_op jit(solution)/shard_map/ppermute | solution.py:355
  127.6 12.4 %collective-permute-start.3 = (bf16[8,128,128]{2,1,0:T(8,128)(2,1)}, bf16[8,128,128]{2,1,0:T(8,128)(2,1)}, u32[]{:S(2)}, u32[]{:S(2)}) collective-permute-start(bf16[8,128,128]{2,1,0:T(8,128)(2,1)} %all-to-all-done.1.refs_7_), channel_id=1, source_target_pairs={{0,2},{2,0},{4,6},{6,4},{8,10},{10,8},{12,14},{14,12},{16,18},{18,... | collective-permute-start | bytes 786440 | tf_op jit(solution)/shard_map/ppermute | solution.py:329
  139.4 10.3 %collective-permute-start.11 = (bf16[8,128,128]{2,1,0:T(8,128)(2,1)}, bf16[8,128,128]{2,1,0:T(8,128)(2,1)}, u32[]{:S(2)}, u32[]{:S(2)}) collective-permute-start(bf16[8,128,128]{2,1,0:T(8,128)(2,1)} %get-tuple-element.69), channel_id=1, source_target_pairs={{0,2},{2,0},{4,6},{6,4},{8,10},{10,8},{12,14},{14,12},{16,18},{18,... | collective-permute-start | bytes 786440 | tf_op jit(solution)/shard_map/ppermute | solution.py:326
  140.0 9.8 %collective-permute-start.10 = (bf16[8,128,128]{2,1,0:T(8,128)(2,1)}, bf16[8,128,128]{2,1,0:T(8,128)(2,1)}, u32[]{:S(2)}, u32[]{:S(2)}) collective-permute-start(bf16[8,128,128]{2,1,0:T(8,128)(2,1)} %all-to-all-done.3.refs_0_), channel_id=1, source_target_pairs={{0,2},{2,0},{4,6},{6,4},{8,10},{10,8},{12,14},{14,12},{16,18},{18,... | collective-permute-start | bytes 786440 | tf_op jit(solution)/shard_map/ppermute | solution.py:329
